TPU v7x, 32 devices: a whole 2x2x4 slice. The times are simulated.
32 devices in a mesh: seq: 8 (over z, x), wa: 4 (over y, core).
Axes of the slice: x: 2, y: 2, z: 4, core: 2. Of those that a mesh axis runs over, the one named last changes fastest.
Arguments:
- tokens: bfloat16 [8, 1024, 2048], P('wa', 'seq'), may hold values from -6 to 6
- lengths: int32 [8], P('wa'), may hold values from 256 to 1024, as said below
- norm_gain: float32 [2048], replicated, may hold values from 0.25 to 1.75
- in_weight: bfloat16 [2048, 8512], P('wa'), may hold values from -0.125 to 0.125
- conv_weight: float32 [4, 4352], replicated, may hold values from -3 to 3
- conv_bias: float32 [4352], replicated, may hold values from -1.8 to 1.8
- dt_bias: float32 [64], replicated, may hold values from -8 to -2
- a_log: float32 [64], replicated, may hold values from 0 to 2.77
- skip_gain: float32 [64], replicated, may hold values from 0.5 to 2
- out_gain: float32 [4096], replicated, may hold values from 0.25 to 1.75
- out_weight: bfloat16 [4096, 2048], P('wa'), may hold values from -0.09375 to 0.09375
- cotangent: bfloat16 [8, 1024, 2048], P('wa', 'seq'), may hold values from -6 to 6
Outputs:
- mixed_out: bfloat16 [8, 1024, 2048], P('wa', 'seq')
- grad_tokens: float32 [8, 1024, 2048], P('wa', 'seq')
- grad_norm_gain: float32 [2048], replicated
- grad_in_weight: float32 [2048, 8512], P('wa')
- grad_conv_weight: float32 [4, 4352], replicated
- grad_conv_bias: float32 [4352], replicated
- grad_dt_bias: float32 [64], replicated
- grad_a_log: float32 [64], replicated
- grad_skip: float32 [64], replicated
- grad_out_gain: float32 [4096], replicated
- grad_out_weight: float32 [4096, 2048], P('wa')
Inputs may be any that keep to these rules, and one draw needn't show every extreme that they name: `lengths`: each sequence's used slots come first; in each group of 2 sequences laid out on one index of wa one sequence is full.
All inputs are finite; a program needn't handle non-finite values.
Results may differ from a plain program's by a relative error of at most 0.012.
Values may be sent and summed in bfloat16 or wider, within the bound.
A program may use at most 384 MiB of HBM per device.

v0:
```python
import jax
import jax.numpy as jnp
from jax import lax
from jax.sharding import PartitionSpec as P

KW = 4
BLOCK_LEN = 256


EPS = 1e-05
HIGH = lax.Precision.HIGHEST


def row_scale(values):
    return lax.rsqrt(jnp.mean(values * values, axis=-1, keepdims=True) + EPS)


def norm_backward(values, row_scales, gain_vec, grad_out):
    weighted = grad_out * gain_vec
    grad_gain = jnp.sum(grad_out * values * row_scales, axis=0)
    grad_values = row_scales * weighted - values * row_scales**3 * jnp.mean(
        weighted * values, axis=-1, keepdims=True
    )
    return (grad_values, grad_gain)


def block_chain(x_heads, dt_vals, rates, b_rows, c_rows, block_len):
    seqs_here, length, head_total, head_size = x_heads.shape
    block_count = length // block_len
    states_dim = b_rows.shape[-1]
    x_blocks = x_heads.reshape(seqs_here, block_count, block_len, head_total, head_size)
    dt_blocks = jnp.swapaxes(dt_vals.reshape(seqs_here, block_count, block_len, head_total), 2, 3)
    rate_blocks = jnp.swapaxes(rates.reshape(seqs_here, block_count, block_len, head_total), 2, 3)
    b_blocks = b_rows.reshape(seqs_here, block_count, block_len, states_dim)
    c_blocks = c_rows.reshape(seqs_here, block_count, block_len, states_dim)
    cumulative = jnp.cumsum(rate_blocks, axis=-1)
    causal_mask = jnp.arange(block_len)[:, None] >= jnp.arange(block_len)[None, :]
    log_decay = cumulative[..., :, None] - cumulative[..., None, :]
    decay_matrix = jnp.where(causal_mask, jnp.exp(jnp.where(causal_mask, log_decay, 0.0)), 0.0)
    scores = jnp.einsum("sbin,sbjn->sbij", c_blocks, b_blocks, precision=HIGH)
    weights = scores[:, :, None] * decay_matrix * dt_blocks[..., None, :]
    inner_part = jnp.einsum("sbhij,sbjhp->sbihp", weights, x_blocks, precision=HIGH)
    tail_decay = jnp.exp(cumulative[..., -1:] - cumulative) * dt_blocks
    block_states = jnp.einsum(
        "sbhj,sbjhp,sbjn->sbhpn", tail_decay, x_blocks, b_blocks, precision=HIGH
    )
    block_decay = jnp.exp(cumulative[..., -1])

    def carry_step(carry_state, pieces):
        decay_now, state_now = pieces
        return (decay_now[..., None, None] * carry_state + state_now, carry_state)

    start_state = jnp.zeros((seqs_here, head_total, head_size, states_dim), jnp.float32)
    final_state, entering = lax.scan(
        carry_step, start_state, (jnp.moveaxis(block_decay, 1, 0), jnp.moveaxis(block_states, 1, 0))
    )
    entering = jnp.moveaxis(entering, 0, 1)
    carried = jnp.swapaxes(jnp.exp(cumulative), 2, 3)[..., None] * jnp.einsum(
        "sbin,sbhpn->sbihp", c_blocks, entering, precision=HIGH
    )
    output = (inner_part + carried).reshape(seqs_here, length, head_total, head_size)
    return (output, final_state)


def mixer_front(
    extended, dt_raw, conv_w, conv_b, bias_part, log_rates, x_width, state_size, head_size
):
    seqs_here = extended.shape[0]
    length = extended.shape[1] - (KW - 1)
    conv_sum = conv_b
    for offset in range(KW):
        conv_sum = conv_sum + conv_w[offset] * extended[:, offset : offset + length]
    activated = jax.nn.silu(conv_sum)
    x_heads = activated[..., :x_width].reshape(seqs_here, length, x_width // head_size, head_size)
    b_rows = activated[..., x_width : x_width + state_size]
    c_rows = activated[..., x_width + state_size :]
    dt_vals = jax.nn.softplus(dt_raw + bias_part)
    rates = -jnp.exp(log_rates) * dt_vals
    block_len = min(BLOCK_LEN, length)
    y_local, local_state = block_chain(x_heads, dt_vals, rates, b_rows, c_rows, block_len)
    running = jnp.exp(jnp.cumsum(rates, axis=1))
    total_decay = running[:, -1]
    return (y_local, local_state, total_decay, x_heads, c_rows, running)


def mixer_finish(y_local, x_heads, gate_part, skip_part):
    y_heads = y_local + skip_part[:, None] * x_heads
    seqs_here, length = (y_heads.shape[0], y_heads.shape[1])
    return y_heads.reshape(seqs_here, length, -1) * jax.nn.silu(gate_part)


def body(
    tokens,
    lengths,
    norm_gain,
    in_weight,
    conv_weight,
    conv_bias,
    dt_bias,
    a_log,
    skip_gain,
    out_gain,
    out_weight,
    cotangent,
):
    seqs_here, slot_rows, width = tokens.shape
    row_count = seqs_here * slot_rows
    inner_width = out_gain.shape[0]
    channels = conv_bias.shape[0]
    state_size = (channels - inner_width) // 2
    head_count = dt_bias.shape[0]
    head_size = inner_width // head_count
    seq_devices = lax.axis_size("seq")
    seq_index = lax.axis_index("seq")
    positions = seq_index * slot_rows + jnp.arange(slot_rows)
    valid_rows = (positions[None, :] < lengths[:, None]).astype(jnp.float32).reshape(row_count, 1)
    flat_tokens = tokens.reshape(row_count, width).astype(jnp.float32)
    in_scale = row_scale(flat_tokens)
    normed = (flat_tokens * in_scale * norm_gain).astype(jnp.bfloat16)
    columns = normed
    projected = jnp.dot(
        columns,
        lax.all_gather(in_weight, "wa", axis=0, tiled=True),
        preferred_element_type=jnp.float32,
    ).astype(jnp.bfloat16)
    gate_part = projected[:, :inner_width].reshape(seqs_here, slot_rows, inner_width)
    conv_in = projected[:, inner_width : inner_width + channels].reshape(
        seqs_here, slot_rows, channels
    )
    dt_raw = projected[:, inner_width + channels :].reshape(seqs_here, slot_rows, head_count)
    local_heads = head_count // seq_devices
    local_width = local_heads * head_size
    channel_start = seq_index * local_width
    head_start = seq_index * local_heads
    gate_heads, x_heads_in, dt_heads = (
        lax.all_to_all(gate_part, "seq", split_axis=2, concat_axis=1, tiled=True),
        lax.all_to_all(conv_in[..., :inner_width], "seq", split_axis=2, concat_axis=1, tiled=True),
        lax.all_to_all(dt_raw, "seq", split_axis=2, concat_axis=1, tiled=True),
    )
    bc_heads = lax.all_gather(conv_in[..., inner_width:], "seq", axis=1, tiled=True)
    joined = jnp.concatenate([x_heads_in, bc_heads], axis=2).astype(jnp.float32)
    extended = jnp.concatenate(
        [jnp.zeros((seqs_here, KW - 1, joined.shape[2]), jnp.float32), joined], axis=1
    )
    conv_local = jnp.concatenate(
        [
            lax.dynamic_slice_in_dim(conv_weight, channel_start, local_width, 1),
            conv_weight[:, inner_width:],
        ],
        axis=1,
    )
    bias_local = jnp.concatenate(
        [
            lax.dynamic_slice_in_dim(conv_bias, channel_start, local_width, 0),
            conv_bias[inner_width:],
        ],
        axis=0,
    )
    shift_local = lax.dynamic_slice_in_dim(dt_bias, head_start, local_heads, 0)
    rates_local = lax.dynamic_slice_in_dim(a_log, head_start, local_heads, 0)
    skip_local = lax.dynamic_slice_in_dim(skip_gain, head_start, local_heads, 0)

    def front_fn(extended_in, dt_in, conv_w, conv_b, bias_part, log_rates):
        return mixer_front(
            extended_in,
            dt_in,
            conv_w,
            conv_b,
            bias_part,
            log_rates,
            local_width,
            state_size,
            head_size,
        )

    front_out, front_pull = jax.vjp(
        front_fn,
        extended,
        dt_heads.astype(jnp.float32),
        conv_local,
        bias_local,
        shift_local,
        rates_local,
    )
    y_local, local_state, total_decay, x_heads, c_rows, running = front_out

    def finish_fn(y_in, x_in, gate_in, skip_in):
        return mixer_finish(y_in, x_in, gate_in, skip_in)

    gated_heads, finish_pull = jax.vjp(
        finish_fn, y_local, x_heads, gate_heads.astype(jnp.float32), skip_local
    )
    gated_tok = lax.all_to_all(
        gated_heads.astype(jnp.bfloat16), "seq", split_axis=1, concat_axis=2, tiled=True
    )
    gated_rows = gated_tok.reshape(row_count, inner_width).astype(jnp.float32)
    out_scale = row_scale(gated_rows)
    normed_out = (gated_rows * out_scale * out_gain).astype(jnp.bfloat16)
    columns = normed_out
    branch = jnp.dot(
        columns,
        lax.all_gather(out_weight, "wa", axis=0, tiled=True),
        preferred_element_type=jnp.float32,
    )
    mixed_out = (flat_tokens + valid_rows * branch).astype(jnp.bfloat16).reshape(tokens.shape)
    cot_rows = cotangent.reshape(row_count, width)
    branch_grad = cot_rows * valid_rows.astype(jnp.bfloat16)
    columns = normed_out
    out_weight_grad = lax.psum_scatter(
        lax.dot_general(
            columns, branch_grad, (((0,), (0,)), ((), ())), preferred_element_type=jnp.float32
        ),
        "wa",
        scatter_dimension=0,
        tiled=True,
    )
    normed_out_grad = lax.dot_general(
        branch_grad,
        lax.all_gather(out_weight, "wa", axis=0, tiled=True),
        (((1,), (1,)), ((), ())),
        preferred_element_type=jnp.float32,
    )
    gated_grad, out_gain_grad = norm_backward(gated_rows, out_scale, out_gain, normed_out_grad)
    gated_grad = gated_grad.astype(jnp.bfloat16).reshape(seqs_here, slot_rows, inner_width)
    grad_heads = lax.all_to_all(gated_grad, "seq", split_axis=2, concat_axis=1, tiled=True).astype(
        jnp.float32
    )
    y_grad, x_grad, gate_grad, skip_part_grad = finish_pull(grad_heads)
    front_grads = front_pull(
        (
            y_grad,
            jnp.zeros_like(local_state),
            jnp.zeros_like(total_decay),
            x_grad,
            jnp.zeros_like(c_rows),
            jnp.zeros_like(running),
        )
    )
    extended_grad, dt_grad, conv_w_grad, conv_b_grad, shift_grad, rates_grad = front_grads
    conv_heads_grad = extended_grad[:, KW - 1 :]
    gate_back, x_back, dt_back = (
        lax.all_to_all(
            gate_grad.astype(jnp.bfloat16), "seq", split_axis=1, concat_axis=2, tiled=True
        ),
        lax.all_to_all(
            conv_heads_grad[..., :local_width].astype(jnp.bfloat16),
            "seq",
            split_axis=1,
            concat_axis=2,
            tiled=True,
        ),
        lax.all_to_all(
            dt_grad.astype(jnp.bfloat16), "seq", split_axis=1, concat_axis=2, tiled=True
        ),
    )
    bc_back = lax.psum_scatter(
        conv_heads_grad[..., local_width:].astype(jnp.bfloat16),
        "seq",
        scatter_dimension=1,
        tiled=True,
    )
    proj_grad = jnp.concatenate([gate_back, x_back, bc_back, dt_back], axis=2)
    x_taps = lax.dynamic_update_slice_in_dim(
        jnp.zeros((KW, inner_width), jnp.float32), conv_w_grad[:, :local_width], channel_start, 1
    )
    conv_weight_grad = jnp.concatenate([x_taps, conv_w_grad[:, local_width:]], axis=1)
    x_bias = lax.dynamic_update_slice_in_dim(
        jnp.zeros((inner_width,), jnp.float32), conv_b_grad[:local_width], channel_start, 0
    )
    conv_bias_grad = jnp.concatenate([x_bias, conv_b_grad[local_width:]], axis=0)
    head_zeros = jnp.zeros((head_count,), jnp.float32)
    dt_bias_grad = lax.dynamic_update_slice_in_dim(head_zeros, shift_grad, head_start, 0)
    a_log_grad = lax.dynamic_update_slice_in_dim(head_zeros, rates_grad, head_start, 0)
    skip_grad = lax.dynamic_update_slice_in_dim(head_zeros, skip_part_grad, head_start, 0)
    proj_rows = proj_grad.reshape(row_count, proj_grad.shape[2])
    columns = normed
    in_weight_grad = lax.psum_scatter(
        lax.dot_general(
            columns, proj_rows, (((0,), (0,)), ((), ())), preferred_element_type=jnp.float32
        ),
        "wa",
        scatter_dimension=0,
        tiled=True,
    )
    normed_grad = lax.dot_general(
        proj_rows,
        lax.all_gather(in_weight, "wa", axis=0, tiled=True),
        (((1,), (1,)), ((), ())),
        preferred_element_type=jnp.float32,
    )
    token_grad, norm_gain_grad = norm_backward(flat_tokens, in_scale, norm_gain, normed_grad)
    token_grad = token_grad + cot_rows.astype(jnp.float32)
    in_weight_grad, out_weight_grad = lax.psum((in_weight_grad, out_weight_grad), "seq")
    small_grads = lax.psum(
        (
            norm_gain_grad,
            conv_weight_grad,
            conv_bias_grad,
            dt_bias_grad,
            a_log_grad,
            skip_grad,
            out_gain_grad,
        ),
        ("seq", "wa"),
    )
    return (
        mixed_out,
        token_grad.reshape(tokens.shape),
        small_grads[0],
        in_weight_grad,
        small_grads[1],
        small_grads[2],
        small_grads[3],
        small_grads[4],
        small_grads[5],
        small_grads[6],
        out_weight_grad,
    )


def solution(mesh):
    placed = (
        P("wa", "seq", None),
        P("wa"),
        P(),
        P("wa", None),
        P(),
        P(),
        P(),
        P(),
        P(),
        P(),
        P("wa", None),
        P("wa", "seq", None),
    )
    return jax.shard_map(
        body,
        mesh=mesh,
        in_specs=placed,
        out_specs=(
            P("wa", "seq", None),
            P("wa", "seq", None),
            P(),
            P("wa", None),
            P(),
            P(),
            P(),
            P(),
            P(),
            P(),
            P("wa", None),
        ),
        check_vma=False,
    )
```

profile of v0, /device:TPU:0, one launch (start us, length us, event | category | flops | bytes accessed | tf_op | source)
XLA Modules:
  0.0 2436.3 jit_solution(2501192697912139225)
XLA Ops:
  10.1 213.5 %all-gather.4.cloned.1.call-done = bf16[2048,8512]{0,1:T(8,128)(2,1)} async-done(((bf16[512,8512]{0,1:T(8,128)(2,1)}), bf16[2048,8512]{0,1:T(8,128)(2,1)}) %all-gather.4.cloned.1.call-update) | async-done | bytes 34865168 | tf_op jit(solution)/shard_map/all_gather | solution.py:123
  223.6 15.1 convolution_convert_fusion
  277.8 43.5 %all-to-all-done = bf16[2,128,4096]{1,0,2:T(2,128)(2,1)S(1)} async-done(((bf16[2,128,4096]{1,0,2:T(2,128)(2,1)}), bf16[2,128,4096]{1,0,2:T(2,128)(2,1)S(1)}, u32[]{:S(2)}, u32[]{:S(2)}) %all-to-all-start) | async-done | bytes 2097184 | tf_op jit(solution)/shard_map/all_to_all | solution.py:137
  376.8 19.7 bitcast_add_fusion.3
  433.1 43.9 %all-to-all-done.3 = bf16[2,1024,512]{2,0,1:T(2,128)(2,1)} async-done(((bf16[2,1024,512]{2,0,1:T(2,128)(2,1)}), bf16[2,1024,512]{2,0,1:T(2,128)(2,1)}, u32[]{:S(2)}, u32[]{:S(2)}) %all-to-all-start.3) | async-done | bytes 2097184 | tf_op jit(solution)/shard_map/all_to_all | solution.py:193
  495.5 14.9 multiply_reduce_fusion.7
  540.0 35.0 %all-to-all-done.4 = bf16[2,128,4096]{1,0,2:T(2,128)(2,1)} async-done(((bf16[2,128,4096]{1,0,2:T(2,128)(2,1)}), bf16[2,128,4096]{1,0,2:T(2,128)(2,1)}, u32[]{:S(2)}, u32[]{:S(2)}) %all-to-all-start.4) | async-done | bytes 2097184 | tf_op jit(solution)/shard_map/all_to_all | solution.py:225
  596.0 29.8 %fusion.9 = (f32[2,4,8,256]{3,2,1,0:T(8,128)S(1)}, f32[2,4,8,256]{3,2,1,0:T(8,128)S(1)}, f32[2,4,8,256]{3,2,1,0:T(8,128)}, f32[2,4,256,256]{3,2,1,0:T(8,128)}) fusion(f32[2,4,8,256]{3,2,1,0:T(8,128)S(1)} %get-tuple-element.439, f32[2,4,8,256]{3,2,1,0:T(8,128)S(1)} %get-tuple-element.437, f32[2,4,256,256]{3,2,1,0:T(8,128)S(1)} %copy-done.32, ...), kind=kOutput, calls=%fused_computation.21 | convolution fusion | flops 3283566592 | bytes 12976128 | tf_op jit(solution)/shard_map/transpose(jvp(sbhij,sbjhp->sbihp))/dot_general | solution.py:42
  664.3 15.5 bitcast_add_fusion.2
  751.6 13.3 fusion.136
  771.0 19.8 reduce-window.34
  792.0 19.8 reduce-window.36
  817.8 16.8 add_convert_fusion
  853.6 44.1 %all-to-all-done.6 = bf16[2,1024,512]{2,0,1:T(2,128)(2,1)} async-done(((bf16[2,1024,512]{2,0,1:T(2,128)(2,1)}), bf16[2,1024,512]{2,0,1:T(2,128)(2,1)}, u32[]{:S(2)}, u32[]{:S(2)}) %all-to-all-start.6) | async-done | bytes 2097184 | tf_op jit(solution)/shard_map/all_to_all | solution.py:245
  907.8 42.0 %all-to-all-done.5 = bf16[2,1024,512]{2,0,1:T(2,128)(2,1)} async-done(((bf16[2,1024,512]{2,0,1:T(2,128)(2,1)}), bf16[2,1024,512]{2,0,1:T(2,128)(2,1)}, u32[]{:S(2)}, u32[]{:S(2)}) %all-to-all-start.5) | async-done | bytes 2097184 | tf_op jit(solution)/shard_map/all_to_all | solution.py:242
  954.8 28.3 %fusion.95 = f32[2048,8512]{0,1:T(8,128)} fusion(bf16[256,2048]{1,0:T(8,128)(2,1)} %copy-done.29, bf16[256,64]{1,0:T(8,128)(2,1)S(1)} %copy.528, bf16[256,256]{1,0:T(8,128)(2,1)S(1)} %bitcast.400, bf16[256,4096]{1,0:T(8,128)(2,1)S(1)} %bitcast.377, bf16[256,4096]{1,0:T(8,128)(2,1)} %bitcast.379), kind=kOutput, calls=%fused_computation.140 | convolution fusion | flops 8942911488 | bytes 75137024 | tf_op jit(solution)/shard_map/dot_general | solution.py:278
  984.6 59.7 %reduce-scatter.8.cloned.1.call-done = f32[1024,2048]{1,0:T(8,128)} async-done(((f32[4096,2048]{1,0:T(8,128)}), f32[1024,2048]{1,0:T(8,128)}) %reduce-scatter.8.cloned.1.call-update) | async-done | bytes 8388624 | tf_op jit(solution)/shard_map/reduce_scatter | solution.py:209
  1044.3 471.0 %reduce-scatter.6.cloned.1.call-done = f32[512,8512]{0,1:T(8,128)} async-done(((f32[2048,8512]{0,1:T(8,128)}), f32[512,8512]{0,1:T(8,128)}) %reduce-scatter.6.cloned.1.call-update) | async-done | bytes 17432592 | tf_op jit(solution)/shard_map/reduce_scatter | solution.py:277
  1516.6 12.6 fusion.49
  1530.5 18.1 fusion.58
  1548.7 40.5 %all-reduce.14 = (f32[2048]{0:T(1024)}, f32[4352]{0:T(1024)}, f32[64]{0:T(128)}, f32[64]{0:T(128)}, f32[64]{0:T(128)}, /*index=5*/f32[4096]{0:T(1024)}) all-reduce(f32[2048]{0:T(1024)S(1)} %get-tuple-element.389, f32[4352]{0:T(1024)S(1)} %pad_maximum_fusion.4, ...), channel_id=1, replica_groups=mesh['seq'=8,'wa'=4] {'seq','wa'}, use_global_device_ids=true, to_apply=%region_25.26 | all-reduce | flops 10688 | bytes 85504 | tf_op jit(solution)/shard_map/psum | solution.py:294
  1592.8 46.6 %all-reduce.19.cloned.1.call-done = f32[4,4352]{1,0:T(4,128)} async-done(((f32[4,4352]{1,0:T(4,128)}), f32[4,4352]{1,0:T(4,128)}) %all-reduce.19.cloned.1.call-update) | async-done | bytes 69648 | tf_op jit(solution)/shard_map/psum | solution.py:294
  1639.4 772.4 %all-reduce.21.cloned.1.call-done = (f32[512,8512]{0,1:T(8,128)}, f32[1024,2048]{1,0:T(8,128)}) async-done(((f32[512,8512]{0,1:T(8,128)}, f32[1024,2048]{1,0:T(8,128)}), (f32[512,8512]{0,1:T(8,128)}, f32[1024,2048]{1,0:T(8,128)})) %all-reduce.21.cloned.1.call-update) | async-done | bytes 25821200 | tf_op jit(solution)/shard_map/psum | solution.py:293
  2411.8 13.4 copy.711
  (405 shorter events, 384.7 us)
Async XLA Ops:
  7.2 216.4 %all-gather.4.cloned.1.call-start = ((), (), s32[]{:S(2)}) async-start(), calls=%async_computation.11 | async-start | bytes 43581440 | tf_op jit(solution)/shard_map/all_gather | solution.py:123
  7.9 323.9 %all-gather.6.cloned.1.call-start = ((), (), s32[]{:S(2)}) async-start(), calls=%async_computation.12 | async-start | bytes 1179648 | tf_op jit(solution)/shard_map/all_gather | solution.py:140
  10.1 228.5 %copy-start.29 = (bf16[256,2048]{1,0:T(8,128)(2,1)}, bf16[256,2048]{1,0:T(8,128)(2,1)S(1)}, u32[]{:S(2)}) copy-start(bf16[256,2048]{1,0:T(8,128)(2,1)S(1)} %fusion.52) | copy-start | bytes 3145732
  247.5 248.0 %all-gather.8.cloned.1.call-start = ((), (), s32[]{:S(2)}) async-start(), calls=%async_computation.13 | async-start | bytes 20971520 | tf_op jit(solution)/shard_map/all_gather | solution.py:202
  248.9 12.2 all-to-all-start.1
  261.1 60.2 %all-to-all-start = ((bf16[2,128,4096]{1,0,2:T(2,128)(2,1)}), bf16[2,128,4096]{1,0,2:T(2,128)(2,1)S(1)}, u32[]{:S(2)}, u32[]{:S(2)}) async-start(bf16[2,128,4096]{1,0,2:T(2,128)(2,1)} %slice.142), calls=%async_computation | async-start | bytes 4194304 | tf_op jit(solution)/shard_map/all_to_all | solution.py:137
  265.1 146.7 %copy-start.52 = (f32[512]{0:T(512)}, f32[512]{0:T(512)S(1)}, u32[]{:S(2)}) copy-start(f32[512]{0:T(512)S(1)} %mul.518) | copy-start | bytes 6148
  265.2 69.3 %copy-start.41 = (f32[768]{0:T(1024)}, f32[768]{0:T(1024)S(1)}, u32[]{:S(2)}) copy-start(f32[768]{0:T(1024)S(1)} %get-tuple-element.391) | copy-start | bytes 9220
  265.2 69.3 %copy-start.43 = (f32[768]{0:T(1024)}, f32[768]{0:T(1024)S(1)}, u32[]{:S(2)}) copy-start(f32[768]{0:T(1024)S(1)} %get-tuple-element.392) | copy-start | bytes 9220
  265.2 69.3 %copy-start.45 = (f32[768]{0:T(1024)}, f32[768]{0:T(1024)S(1)}, u32[]{:S(2)}) copy-start(f32[768]{0:T(1024)S(1)} %get-tuple-element.393) | copy-start | bytes 9220
  265.2 69.3 %copy-start.47 = (f32[768]{0:T(1024)}, f32[768]{0:T(1024)S(1)}, u32[]{:S(2)}) copy-start(f32[768]{0:T(1024)S(1)} %get-tuple-element.394) | copy-start | bytes 9220
  277.6 50.9 %copy-start.36 = (f32[2,4,8]{2,1,0:T(4,128)}, f32[2,4,8]{2,1,0:T(4,128)S(1)}, u32[]{:S(2)}) copy-start(f32[2,4,8]{2,1,0:T(4,128)S(1)} %slice_reduce_fusion.2) | copy-start | bytes 772
  321.3 85.9 %all-to-all-start.2 = ((bf16[2,128,4096]{1,0,2:T(2,128)(2,1)}), bf16[2,128,4096]{1,0,2:T(2,128)(2,1)}, u32[]{:S(2)}, u32[]{:S(2)}) async-start(bf16[2,128,4096]{1,0,2:T(2,128)(2,1)} %reshape.388), calls=%async_computation.2 | async-start | bytes 4194304 | tf_op jit(solution)/shard_map/all_to_all | solution.py:136
  424.1 53.0 %all-to-all-start.3 = ((bf16[2,1024,512]{2,0,1:T(2,128)(2,1)}), bf16[2,1024,512]{2,0,1:T(2,128)(2,1)}, u32[]{:S(2)}, u32[]{:S(2)}) async-start(bf16[2,1024,512]{2,0,1:T(2,128)(2,1)} %copy.495), calls=%async_computation.3 | async-start | bytes 4194304 | tf_op jit(solution)/shard_map/all_to_all | solution.py:193
  522.8 52.2 %all-to-all-start.4 = ((bf16[2,128,4096]{1,0,2:T(2,128)(2,1)}), bf16[2,128,4096]{1,0,2:T(2,128)(2,1)}, u32[]{:S(2)}, u32[]{:S(2)}) async-start(bf16[2,128,4096]{1,0,2:T(2,128)(2,1)} %copy.498), calls=%async_computation.4 | async-start | bytes 4194304 | tf_op jit(solution)/shard_map/all_to_all | solution.py:225
  527.2 376.0 %reduce-scatter.10.cloned.1.call-start = ((), (), s32[]{:S(2)}) async-start(), calls=%async_computation.17 | async-start | bytes 1179648
  745.3 299.0 %reduce-scatter.8.cloned.1.call-start = ((), (), s32[]{:S(2)}) async-start(), calls=%async_computation.16 | async-start | bytes 41943040 | tf_op jit(solution)/shard_map/reduce_scatter | solution.py:209
  814.0 29.6 %all-to-all-start.7 = ((bf16[8,2,1024]{2,1,0:T(2,128)(2,1)}), bf16[8,2,1024]{2,1,0:T(2,128)(2,1)S(1)}, u32[]{:S(2)}, u32[]{:S(2)}) async-start(bf16[8,2,1024]{2,1,0:T(2,128)(2,1)} %reshape.438), calls=%async_computation.7 | async-start | bytes 65536 | tf_op jit(solution)/shard_map/all_to_all | solution.py:252
  843.6 54.1 %all-to-all-start.6 = ((bf16[2,1024,512]{2,0,1:T(2,128)(2,1)}), bf16[2,1024,512]{2,0,1:T(2,128)(2,1)}, u32[]{:S(2)}, u32[]{:S(2)}) async-start(bf16[2,1024,512]{2,0,1:T(2,128)(2,1)} %copy.517), calls=%async_computation.6 | async-start | bytes 4194304 | tf_op jit(solution)/shard_map/all_to_all | solution.py:245
  897.7 52.2 %all-to-all-start.5 = ((bf16[2,1024,512]{2,0,1:T(2,128)(2,1)}), bf16[2,1024,512]{2,0,1:T(2,128)(2,1)}, u32[]{:S(2)}, u32[]{:S(2)}) async-start(bf16[2,1024,512]{2,0,1:T(2,128)(2,1)} %copy.501), calls=%async_computation.5 | async-start | bytes 4194304 | tf_op jit(solution)/shard_map/all_to_all | solution.py:242
  902.0 613.3 %reduce-scatter.6.cloned.1.call-start = ((), (), s32[]{:S(2)}) async-start(), calls=%async_computation.14 | async-start | bytes 87162880 | tf_op jit(solution)/shard_map/reduce_scatter | solution.py:277
  907.8 47.0 %copy-start.26 = (bf16[32,8,8,512]{3,1,2,0:T(8,128)(2,1)}, bf16[32,8,8,512]{3,1,2,0:T(8,128)(2,1)S(1)}, u32[]{:S(2)}) copy-start(bf16[32,8,8,512]{3,1,2,0:T(8,128)(2,1)S(1)} %copy.597) | copy-start | bytes 6291460
  983.1 656.3 %all-reduce.19.cloned.1.call-start = ((), (), s32[]{:S(2)}) async-start(), calls=%async_computation.15 | async-start | bytes 139264 | tf_op jit(solution)/shard_map/psum | solution.py:294
  984.6 1427.2 %all-reduce.21.cloned.1.call-start = ((), (), s32[]{:S(2)}) async-start(), calls=%async_computation.18 | async-start | bytes 51642368 | tf_op jit(solution)/shard_map/psum | solution.py:293
  (80 other events, 705.0 us)
Sparse Core Ops, SparseCore 0:
  9.6 213.9 all-gather.3
  247.6 67.1 all-gather.5
  316.4 104.4 all-gather.7
  745.5 62.2 reduce-scatter.9
  810.4 233.8 reduce-scatter.7
  1047.0 468.2 reduce-scatter.5
  1521.5 117.8 all-reduce.18
  1643.8 767.9 all-reduce.20
where the time goes:
time: 2440 us
  waiting for transfers between devices  1780 us (73%)
  matrix products  219 us (9%)
  local copies, waits for them, and re-layouts  179 us (7%)
  other arithmetic  166 us (7%)
  blocking collectives  40.5 us (2%)
  starting transfers between devices  38.5 us (2%)
    psum x1, waiting for transfers between devices, body(): lax.psum((in_weight_grad, out_weight_grad), 'seq')  772 us
    reduce_scatter x1, waiting for transfers between devices, body(): lax.psum_scatter(lax.dot_general(columns, proj_rows, (((0,), (0,)), ((),...  471 us
    all_gather x1, waiting for transfers between devices, body(): lax.all_gather(in_weight, 'wa', axis=0, tiled=True)  213 us
    another operation x14, other arithmetic  71.1 us
    dot_general x3, matrix products, block_chain(): jnp.einsum('sbhij,sbjhp->sbihp', weights, x_blocks, precision=HIGH)  65 us
    reduce_scatter x1, waiting for transfers between devices, body(): lax.psum_scatter(lax.dot_general(columns, branch_grad, (((0,), (0,)), (()...  59.7 us
    unnamed x184, local copies, waits for them, and re-layouts  53.7 us
  transfers between devices with their start and end apart: 16, of which 11 were waited for; matrix products, arithmetic and copies ran while one was open for 13% of the time, Pallas kernels for 0%

commit v1 on v0

v1 whole, which is shorter than its diff:
```python
import functools

import jax
import jax.numpy as jnp
from jax import lax
from jax.experimental import pallas as pl
from jax.experimental.pallas import tpu as pltpu
from jax.sharding import PartitionSpec as P

KW = 4
BLOCK_LEN = 128
MESH = pl.DeviceIdType.MESH


EPS = 1e-05
HIGH = lax.Precision.DEFAULT


def row_scale(values):
    return lax.rsqrt(jnp.mean(values * values, axis=-1, keepdims=True) + EPS)


def norm_backward(values, row_scales, gain_vec, grad_out):
    weighted = grad_out * gain_vec
    grad_gain = jnp.sum(grad_out * values * row_scales, axis=0)
    grad_values = row_scales * weighted - values * row_scales**3 * jnp.mean(
        weighted * values, axis=-1, keepdims=True
    )
    return (grad_values, grad_gain)


def block_chain(x_heads, dt_vals, rates, b_rows, c_rows, block_len):
    seqs_here, length, head_total, head_size = x_heads.shape
    block_count = length // block_len
    states_dim = b_rows.shape[-1]
    x_blocks = x_heads.reshape(seqs_here, block_count, block_len, head_total, head_size)
    dt_blocks = jnp.swapaxes(dt_vals.reshape(seqs_here, block_count, block_len, head_total), 2, 3)
    rate_blocks = jnp.swapaxes(rates.reshape(seqs_here, block_count, block_len, head_total), 2, 3)
    b_blocks = b_rows.reshape(seqs_here, block_count, block_len, states_dim)
    c_blocks = c_rows.reshape(seqs_here, block_count, block_len, states_dim)
    cumulative = jnp.cumsum(rate_blocks, axis=-1)
    causal_mask = jnp.arange(block_len)[:, None] >= jnp.arange(block_len)[None, :]
    log_decay = cumulative[..., :, None] - cumulative[..., None, :]
    decay_matrix = jnp.where(causal_mask, jnp.exp(jnp.where(causal_mask, log_decay, 0.0)), 0.0)
    scores = jnp.einsum("sbin,sbjn->sbij", c_blocks, b_blocks, precision=HIGH)
    weights = scores[:, :, None] * decay_matrix * dt_blocks[..., None, :]
    inner_part = jnp.einsum("sbhij,sbjhp->sbihp", weights, x_blocks, precision=HIGH)
    tail_decay = jnp.exp(cumulative[..., -1:] - cumulative) * dt_blocks
    block_states = jnp.einsum(
        "sbhj,sbjhp,sbjn->sbhpn", tail_decay, x_blocks, b_blocks, precision=HIGH
    )
    block_decay = jnp.exp(cumulative[..., -1])

    def carry_step(carry_state, pieces):
        decay_now, state_now = pieces
        return (decay_now[..., None, None] * carry_state + state_now, carry_state)

    start_state = jnp.zeros((seqs_here, head_total, head_size, states_dim), jnp.float32)
    final_state, entering = lax.scan(
        carry_step, start_state, (jnp.moveaxis(block_decay, 1, 0), jnp.moveaxis(block_states, 1, 0))
    )
    entering = jnp.moveaxis(entering, 0, 1)
    carried = jnp.swapaxes(jnp.exp(cumulative), 2, 3)[..., None] * jnp.einsum(
        "sbin,sbhpn->sbihp", c_blocks, entering, precision=HIGH
    )
    output = (inner_part + carried).reshape(seqs_here, length, head_total, head_size)
    return (output, final_state)


def mixer_front(
    extended, dt_raw, conv_w, conv_b, bias_part, log_rates, x_width, state_size, head_size
):
    seqs_here = extended.shape[0]
    length = extended.shape[1] - (KW - 1)
    conv_sum = conv_b
    for offset in range(KW):
        conv_sum = conv_sum + conv_w[offset] * extended[:, offset : offset + length]
    activated = jax.nn.silu(conv_sum)
    x_heads = activated[..., :x_width].reshape(seqs_here, length, x_width // head_size, head_size)
    b_rows = activated[..., x_width : x_width + state_size]
    c_rows = activated[..., x_width + state_size :]
    dt_vals = jax.nn.softplus(dt_raw + bias_part)
    rates = -jnp.exp(log_rates) * dt_vals
    block_len = min(BLOCK_LEN, length)
    y_local, local_state = block_chain(x_heads, dt_vals, rates, b_rows, c_rows, block_len)
    running = jnp.exp(jnp.cumsum(rates, axis=1))
    total_decay = running[:, -1]
    return (y_local, local_state, total_decay, x_heads, c_rows, running)


def mixer_finish(y_local, x_heads, gate_part, skip_part):
    y_heads = y_local + skip_part[:, None] * x_heads
    seqs_here, length = (y_heads.shape[0], y_heads.shape[1])
    return y_heads.reshape(seqs_here, length, -1) * jax.nn.silu(gate_part)


def ring_pos(index, size):
    row, side = index // 2, index % 2
    return row + side * (size - 1 - 2 * row)


def ring_index(pos, size):
    side = pos // (size // 2)
    row = pos + side * (size - 1 - 2 * pos)
    return row * 2 + side


def gather_kernel(size, chunks, x_ref, o_ref, local_sem, send_sem, recv_sem):
    me, group = lax.axis_index("seq"), lax.axis_index("wa")
    pos = ring_pos(me, size)
    right = ring_index((pos + 1) % size, size)
    left = ring_index((pos + size - 1) % size, size)
    barrier = pltpu.get_barrier_semaphore()
    for neighbour in (left, right):
        pl.semaphore_signal(barrier, inc=1, device_id=(neighbour, group), device_id_type=MESH)
    pl.semaphore_wait(barrier, 2)
    local = pltpu.make_async_copy(x_ref, o_ref.at[me], local_sem)
    local.start()
    copies = {}
    for step in range(size - 1):
        going_right = ring_index((pos - step + size) % size, size)
        going_left = ring_index((pos + step) % size, size)
        for chunk in range(chunks):
            for way, (block, target) in enumerate(((going_right, right), (going_left, left))):
                if step > 0:
                    copies[step - 1, chunk, way].wait_recv()
                source = x_ref.at[way, chunk] if step == 0 else o_ref.at[block, way, chunk]
                copy = pltpu.make_async_remote_copy(
                    source,
                    o_ref.at[block, way, chunk],
                    send_sem.at[step, chunk, way],
                    recv_sem.at[step, chunk, way],
                    device_id=(target, group),
                    device_id_type=MESH,
                )
                copy.start()
                copies[step, chunk, way] = copy
    for chunk in range(chunks):
        for way in range(2):
            copies[size - 2, chunk, way].wait_recv()
    for copy in copies.values():
        copy.wait_send()
    local.wait()


def ring_gather(x, collective_id):
    size = lax.axis_size("seq")
    rows, cols = x.shape
    chunks = 2
    parts = x.reshape(2, chunks, rows // (2 * chunks), cols)
    out = pl.pallas_call(
        functools.partial(gather_kernel, size, chunks),
        out_shape=jax.ShapeDtypeStruct((size,) + parts.shape, x.dtype),
        in_specs=[pl.BlockSpec(memory_space=pl.ANY)],
        out_specs=pl.BlockSpec(memory_space=pl.ANY),
        scratch_shapes=[
            pltpu.SemaphoreType.DMA,
            pltpu.SemaphoreType.DMA((size - 1, chunks, 2)),
            pltpu.SemaphoreType.DMA((size - 1, chunks, 2)),
        ],
        compiler_params=pltpu.CompilerParams(collective_id=collective_id, has_side_effects=True),
    )(parts)
    return out.reshape(size * rows, cols)


def body(
    tokens,
    lengths,
    norm_gain,
    in_weight,
    conv_weight,
    conv_bias,
    dt_bias,
    a_log,
    skip_gain,
    out_gain,
    out_weight,
    cotangent,
):
    seqs_here, slot_rows, width = tokens.shape
    row_count = seqs_here * slot_rows
    inner_width = out_gain.shape[0]
    channels = conv_bias.shape[0]
    bc_width = channels - inner_width
    state_size = bc_width // 2
    head_count = dt_bias.shape[0]
    head_size = inner_width // head_count
    seq_devices = lax.axis_size("seq")
    group_devices = lax.axis_size("wa")
    seq_index = lax.axis_index("seq")
    length = seq_devices * slot_rows
    local_heads = head_count // seq_devices
    local_width = local_heads * head_size
    channel_start = seq_index * local_width
    head_start = seq_index * local_heads
    bf16, f32 = jnp.bfloat16, jnp.float32

    def take(array, start, size, axis):
        return lax.dynamic_slice_in_dim(array, start, size, axis)

    def to_sequence(rows):
        blocks = rows.reshape(seq_devices, seqs_here, slot_rows, rows.shape[-1])
        return jnp.swapaxes(blocks, 0, 1).reshape(seqs_here, length, rows.shape[-1])

    def to_rows(values):
        blocks = values.reshape(seqs_here, seq_devices, slot_rows, values.shape[-1])
        return jnp.swapaxes(blocks, 0, 1).reshape(seq_devices * row_count, values.shape[-1])

    positions = seq_index * slot_rows + jnp.arange(slot_rows)
    valid_rows = (positions[None, :] < lengths[:, None]).astype(f32).reshape(row_count, 1)
    flat_tokens = tokens.reshape(row_count, width).astype(f32)
    in_scale = row_scale(flat_tokens)
    normed = (flat_tokens * in_scale * norm_gain).astype(bf16)
    normed_all = ring_gather(normed, 0)
    cot_rows = cotangent.reshape(row_count, width)
    branch_grad = ring_gather(cot_rows * valid_rows.astype(bf16), 1)

    local_columns = jnp.concatenate(
        [
            take(in_weight, channel_start, local_width, 1),
            take(in_weight, inner_width + channel_start, local_width, 1),
            in_weight[:, 2 * inner_width :],
        ],
        axis=1,
    )
    in_columns = lax.all_gather(local_columns, "wa", axis=0, tiled=True)
    projected = to_sequence(
        jnp.dot(normed_all, in_columns, preferred_element_type=f32).astype(bf16)
    )
    gate_part = projected[..., :local_width].astype(f32)
    joined = projected[..., local_width : 2 * local_width + bc_width].astype(f32)
    dt_raw = take(
        projected[..., 2 * local_width + bc_width :], head_start, local_heads, 2
    ).astype(f32)
    extended = jnp.concatenate(
        [jnp.zeros((seqs_here, KW - 1, joined.shape[2]), f32), joined], axis=1
    )
    conv_local = jnp.concatenate(
        [take(conv_weight, channel_start, local_width, 1), conv_weight[:, inner_width:]], axis=1
    )
    bias_local = jnp.concatenate(
        [take(conv_bias, channel_start, local_width, 0), conv_bias[inner_width:]], axis=0
    )
    shift_local = take(dt_bias, head_start, local_heads, 0)
    rates_local = take(a_log, head_start, local_heads, 0)
    skip_local = take(skip_gain, head_start, local_heads, 0)
    gain_local = take(out_gain, channel_start, local_width, 0)

    def front_fn(extended_in, dt_in, conv_w, conv_b, bias_part, log_rates):
        return mixer_front(
            extended_in, dt_in, conv_w, conv_b, bias_part, log_rates, local_width, state_size, head_size
        )

    front_out, front_pull = jax.vjp(
        front_fn, extended, dt_raw, conv_local, bias_local, shift_local, rates_local
    )
    y_local, local_state, total_decay, x_heads, c_rows, running = front_out
    gated_heads, finish_pull = jax.vjp(mixer_finish, y_local, x_heads, gate_part, skip_local)
    gated = to_rows(gated_heads.astype(bf16)).astype(f32)

    row_group = inner_width // group_devices
    owner = channel_start // row_group
    out_rows = lax.psum(
        jnp.where(
            lax.axis_index("wa") == owner,
            take(out_weight, channel_start - owner * row_group, local_width, 0),
            jnp.zeros((local_width, width), bf16),
        ),
        "wa",
    )
    out_grad = lax.dot_general(
        branch_grad, out_rows, (((1,), (1,)), ((), ())), preferred_element_type=f32
    )
    weighted = out_grad * gain_local
    sums = lax.psum(
        jnp.stack([jnp.sum(gated * gated, axis=-1), jnp.sum(weighted * gated, axis=-1)]), "seq"
    )
    out_scale = lax.rsqrt(sums[0] / inner_width + EPS)[:, None]
    mean_dot = (sums[1] / inner_width)[:, None]
    normed_out = (gated * out_scale * gain_local).astype(bf16)
    out_gain_part = jnp.sum(out_grad * gated * out_scale, axis=0)
    gated_grad = (out_scale * weighted - gated * out_scale**3 * mean_dot).astype(bf16)

    branch = lax.psum_scatter(
        jnp.dot(normed_out, out_rows, preferred_element_type=f32).astype(bf16),
        "seq",
        scatter_dimension=0,
        tiled=True,
    ).astype(f32)
    mixed_out = (flat_tokens + valid_rows * branch).astype(bf16).reshape(tokens.shape)
    out_weight_part = lax.psum_scatter(
        lax.dot_general(
            normed_out, branch_grad, (((0,), (0,)), ((), ())), preferred_element_type=f32
        ).astype(bf16),
        "wa",
        scatter_dimension=0,
        tiled=True,
    )
    piece = local_width // group_devices
    per_owner = seq_devices // group_devices
    pieces = lax.all_gather(out_weight_part, "seq", axis=0, tiled=False)
    pieces = lax.all_to_all(
        pieces.reshape(group_devices, per_owner, piece, width), "wa", 0, 0, tiled=True
    )
    out_weight_grad = jnp.swapaxes(pieces, 0, 1).reshape(row_group, width).astype(f32)

    y_grad, x_grad, gate_grad, skip_grad = finish_pull(to_sequence(gated_grad).astype(f32))
    extended_grad, dt_grad, conv_w_grad, conv_b_grad, shift_grad, rates_grad = front_pull(
        (
            y_grad,
            jnp.zeros_like(local_state),
            jnp.zeros_like(total_decay),
            x_grad,
            jnp.zeros_like(c_rows),
            jnp.zeros_like(running),
        )
    )
    dt_wide = lax.dynamic_update_slice_in_dim(
        jnp.zeros((seqs_here, length, head_count), f32), dt_grad, head_start, 2
    )
    proj_grad = to_rows(
        jnp.concatenate([gate_grad, extended_grad[:, KW - 1 :], dt_wide], axis=2).astype(bf16)
    )
    in_weight_part = lax.psum_scatter(
        lax.dot_general(
            normed_all, proj_grad, (((0,), (0,)), ((), ())), preferred_element_type=f32
        ).astype(bf16),
        "wa",
        scatter_dimension=0,
        tiled=True,
    )
    own = ring_gather(in_weight_part[:, : 2 * local_width], 2)
    own = own.reshape(seq_devices, in_weight.shape[0], 2, local_width)
    own = jnp.transpose(own, (1, 2, 0, 3)).reshape(in_weight.shape[0], 2 * inner_width)
    shared = lax.psum(in_weight_part[:, 2 * local_width :].astype(f32), "seq")
    in_weight_grad = jnp.concatenate([own.astype(f32), shared], axis=1)
    normed_grad = lax.psum_scatter(
        lax.dot_general(
            proj_grad, in_columns, (((1,), (1,)), ((), ())), preferred_element_type=f32
        ).astype(bf16),
        "seq",
        scatter_dimension=0,
        tiled=True,
    ).astype(f32)
    token_grad, norm_gain_grad = norm_backward(flat_tokens, in_scale, norm_gain, normed_grad)
    token_grad = token_grad + cot_rows.astype(f32)

    def place(part, total, start, axis):
        shape = list(part.shape)
        shape[axis] = total
        return lax.dynamic_update_slice_in_dim(jnp.zeros(shape, f32), part, start, axis)

    conv_weight_grad = jnp.concatenate(
        [place(conv_w_grad[:, :local_width], inner_width, channel_start, 1), conv_w_grad[:, local_width:]],
        axis=1,
    )
    conv_bias_grad = jnp.concatenate(
        [place(conv_b_grad[:local_width], inner_width, channel_start, 0), conv_b_grad[local_width:]],
        axis=0,
    )
    small = lax.psum(
        jnp.concatenate(
            [
                norm_gain_grad,
                conv_weight_grad.reshape(-1),
                conv_bias_grad,
                place(shift_grad, head_count, head_start, 0),
                place(rates_grad, head_count, head_start, 0),
                place(skip_grad, head_count, head_start, 0),
                place(out_gain_part, inner_width, channel_start, 0),
            ]
        ),
        ("seq", "wa"),
    )
    bounds, at = [], 0
    for extent in (width, KW * channels, channels, head_count, head_count, head_count, inner_width):
        bounds.append(small[at : at + extent])
        at += extent
    return (
        mixed_out,
        token_grad.reshape(tokens.shape),
        bounds[0],
        in_weight_grad,
        bounds[1].reshape(KW, channels),
        bounds[2],
        bounds[3],
        bounds[4],
        bounds[5],
        bounds[6],
        out_weight_grad,
    )


def solution(mesh):
    placed = (
        P("wa", "seq", None),
        P("wa"),
        P(),
        P("wa", None),
        P(),
        P(),
        P(),
        P(),
        P(),
        P(),
        P("wa", None),
        P("wa", "seq", None),
    )
    return jax.shard_map(
        body,
        mesh=mesh,
        in_specs=placed,
        out_specs=(
            P("wa", "seq", None),
            P("wa", "seq", None),
            P(),
            P("wa", None),
            P(),
            P(),
            P(),
            P(),
            P(),
            P(),
            P("wa", None),
        ),
        check_vma=False,
    )
```

time: 2440 us -> 1300 us (0.53)
  waiting for transfers between devices: 1780 us -> 420 us
  Pallas kernels: 0 us -> 283 us
  matrix products: 219 us -> 126 us
  other arithmetic: 166 us -> 202 us
  starting transfers between devices: 38.5 us -> 5.37 us
    psum x2 -> x3, waiting for transfers between devices: 819 us -> 121 us  [the longest x1 121 us: body(): lax.psum(jnp.concatenate([norm_gain_grad, conv_weight_grad.reshape(-1), c...]
    pallas_call x0 -> x3, Pallas kernels: none -> 283 us  [ring_gather(): pl.pallas_call(functools.partial(gather_kernel, size, chunks), out_shape=...]
    reduce_scatter x2 -> x4, waiting for transfers between devices: 531 us -> 253 us  [the longest x1 149 us: body(): lax.psum_scatter(jnp.dot(normed_out, out_rows, preferred_element_type=f32...]
    all_to_all x8 -> x1, waiting for transfers between devices: 212 us -> 0.01 us  [body(): lax.all_to_all(pieces.reshape(group_devices, per_owner, piece, width), 'w...]
    all_gather x3 -> x2, waiting for transfers between devices: 214 us -> 45.4 us  [the longest x1 45.4 us: body(): pieces = lax.all_gather(out_weight_part, 'seq', axis=0, tiled=False)]
    dot_general x3, matrix products: 65 us -> 19.6 us  [block_chain(): jnp.einsum('sbhij,sbjhp->sbihp', weights, x_blocks, precision=HIGH)]
    all_to_all x8 -> x1, starting transfers between devices: 38.2 us -> 5 us  [body(): lax.all_to_all(pieces.reshape(group_devices, per_owner, piece, width), 'w...]
    unnamed x184 -> x134, local copies, waits for them, and re-layouts: 53.7 us -> 21.3 us
  transfers between devices with their start and end apart: 16 -> 10, of which waited for: 11 -> 5; matrix products, arithmetic and copies ran while one was open for 13% -> 25% of each run, Pallas kernels for 0% -> 22%
where the time goes in v1:
time: 1300 us; the launch traced here: 1290 us
  waiting for transfers between devices  420 us (32%)
  Pallas kernels  283 us (22%)
  other arithmetic  202 us (16%)
  local copies, waits for them, and re-layouts  201 us (15%)
  matrix products  126 us (10%)
  blocking collectives  35.5 us (3%)
  between operations  15.1 us (1%)
    pallas_call x3, Pallas kernels, ring_gather(): pl.pallas_call(functools.partial(gather_kernel, size, chunks), out_shape=...  283 us
    reduce_scatter x1, waiting for transfers between devices, body(): lax.psum_scatter(jnp.dot(normed_out, out_rows, preferred_element_type=f32...  149 us
    psum x1, waiting for transfers between devices, body(): lax.psum(jnp.concatenate([norm_gain_grad, conv_weight_grad.reshape(-1), c...  121 us
    reduce_scatter x1, waiting for transfers between devices, body(): lax.psum_scatter(lax.dot_general(proj_grad, in_columns, (((1,), (1,)), ((...  53.3 us
    reduce_scatter x1, waiting for transfers between devices, body(): lax.psum_scatter(lax.dot_general(normed_all, proj_grad, (((0,), (0,)), ((...  49.9 us
    convert_element_type x2, local copies, waits for them, and re-layouts, body(): in_weight_grad = jnp.concatenate([own.astype(f32), shared], axis=1)  46.6 us
    all_gather x1, waiting for transfers between devices, body(): pieces = lax.all_gather(out_weight_part, 'seq', axis=0, tiled=False)  45.4 us
    psum x1, blocking collectives, body(): lax.psum(jnp.stack([jnp.sum(gated * gated, axis=-1), jnp.sum(weighted * g...  35.5 us
  transfers between devices with their start and end apart: 10, of which 5 were waited for; matrix products, arithmetic and copies ran while one was open for 25% of the time, Pallas kernels for 22%

profile of v1, /device:TPU:0, one launch (start us, length us, event | category | flops | bytes accessed | tf_op | source)
XLA Modules:
  0.0 1288.5 jit_solution(1815775976145980190)
XLA Ops:
  20.3 84.7 %shard_map.203 = bf16[8,2,2,64,2048]{4,3,2,1,0:T(8,128)(2,1)} custom-call(bf16[2,2,64,2048]{3,2,1,0:T(8,128)(2,1)} %multiply_convert_fusion.1.x_ref), custom_call_target="tpu_custom_call" | custom-call | tf_op jit(solution)/shard_map/pallas_call | solution.py:151
  107.8 82.1 %shard_map.204 = bf16[8,2,2,64,2048]{4,3,2,1,0:T(8,128)(2,1)} custom-call(bf16[2,2,64,2048]{3,2,1,0:T(8,128)(2,1)} %broadcast_multiply_fusion.4.x_ref), custom_call_target="tpu_custom_call" | custom-call | tf_op jit(solution)/shard_map/pallas_call | solution.py:151
  190.9 17.5 %convolution_convert_fusion.3 = bf16[2048,1344]{0,1:T(8,128)(2,1)} fusion(bf16[2048,2048]{1,0:T(8,128)(2,1)} %bitcast.350, bf16[2048,1344]{0,1:T(8,128)(2,1)} %all-gather.4.cloned.1.call-done), kind=kOutput, calls=%fused_computation.24 | convolution fusion | flops 11277041664 | bytes 19398656 | tf_op jit(solution)/shard_map/dot_general | solution.py:228
  208.3 13.4 %reshape.374 = bf16[8,2,128,1344]{2,1,0,3:T(2,128)(2,1)} reshape(bf16[2048,1344]{0,1:T(8,128)(2,1)} %convolution_convert_fusion.3) | data formatting | bytes 11010048 | tf_op jit(solution)/shard_map/reshape | solution.py:202
  228.2 9.5 reshape.375
  271.7 26.2 %while.36 = (s32[]{:T(128)}, f32[2,8,64,128]{3,2,1,0:T(8,128)S(1)}, f32[8,2,8,64,128]{4,3,2,1,0:T(8,128)}, f32[8,2,8,1,1]{2,1,4,3,0:T(2,128)}, f32[8,2,8]{2,0,1:T(8,128)}, /*index=5*/f32[8,2,8,64,128]{4,3,2,0,1:T(8,128)}) while((s32[]{:T(128)}, f32[2,8,64,128]{3,2,1,0:T(8,128)S(1)}, f32[8,2,8,64,128]{4,3,2,1,0:T(8,128)}, ...), condition=%wide.region_3.4_spmd.clone.clone, body=%wide.region_2.3_spmd.clone.sunk.clone | while | flops 524291 | bytes 2622824 | solution.py:59
  333.4 12.0 fusion.20
  345.3 35.5 %psum.29 = f32[2,2048]{1,0:T(2,128)S(1)} all-reduce(f32[2,2048]{1,0:T(2,128)S(1)} %pad_maximum_fusion.4), channel_id=1, replica_groups=mesh['seq'=8,'wa'=4] {'seq'}, use_global_device_ids=true, to_apply=%region_7.8 | all-reduce | flops 4096 | bytes 32768 | tf_op jit(solution)/shard_map/psum | solution.py:275
  421.5 10.0 fusion.13
  432.1 32.5 %while.37 = (s32[]{:T(128)}, f32[2,8,64,128]{3,2,1,0:T(8,128)S(1)}, f32[8,2,8]{2,0,1:T(8,128)}, bf16[8,2,8,64,128]{4,3,2,1,0:T(8,128)(2,1)S(1)}, f32[8,2,8,64,12...) while((s32[]{:T(128)}, f32[2,8,64,128]{3,2,1,0:T(8,128)S(1)}, ...), condition=%wide.region_12.13_spmd.clone.clone, body=%wide.region_10.12_spmd.clone.sunk.clone | while | flops 786420 | bytes 2884092 | solution.py:59
  479.7 19.8 %reduce-window.16 = f32[2,8,8,128]{3,2,1,0:T(8,128)S(1)} reduce-window(f32[2,8,8,128]{3,2,1,0:T(8,128)S(1)} %exponential_multiply_fusion, f32[]{:T(128)} %constant.140.clone.1), window={size=1x1x1x128 pad=0_0x0_0x0_0x0_127}, to_apply=%region_16.17 | reduce-window | flops 2080768 | bytes 131076 | tf_op jit(solution)/shard_map/reduce-window.2
  501.2 19.8 %reduce_window_sum.54 = f32[2,8,8,128]{3,2,1,0:T(8,128)S(1)} reduce-window(f32[2,8,8,128]{3,2,1,0:T(8,128)S(1)} %fusion.105, f32[]{:T(128)} %constant.140.clone.1), window={size=1x1x1x128 pad=0_0x0_0x0_0x0_127}, to_apply=%region_22.23 | reduce-window | flops 2080768 | bytes 131076 | tf_op jit(solution)/shard_map/transpose(jvp(jit(cumsum)))/reduce_window_sum | solution.py:41
  565.3 14.0 %multiply_reduce_fusion.4 = (f32[768]{0:T(1024)S(1)}, f32[768]{0:T(1024)S(1)}, f32[768]{0:T(1024)S(1)}, f32[768]{0:T(1024)S(1)}, f32[768]{0:T(1024)S(1)}, /*index=5*/f32[2,1024,768]{1,2,0:T(8,128)S(1)}) fusion(f32[2,1024,768]{1,2,0:T(8,128)} %copy-done.6, bf16[2,1024,1344]{1,2,0:T(8,128)(2,1)} %reshape.375, f32[2,1024,768]{1,2,0:T(8,128)} %get-tuple-element.347, ...), kind=kLoop, calls=%fused_computation.36 | loop fusion | flops 33026304 | bytes 28326912 | tf_op jit(solution)/shard_map/transpose(jvp())/reduce_sum | solution.py:77
  610.0 16.1 %convolution_convert_fusion.2 = bf16[2048,1344]{0,1:T(8,128)(2,1)} fusion(bf16[2048,2048]{1,0:T(8,128)(2,1)} %bitcast.351, bf16[2048,1344]{1,0:T(8,128)(2,1)S(1)} %bitcast.357), kind=kOutput, calls=%fused_computation.23 | convolution fusion | flops 11277041664 | bytes 19398656 | tf_op jit(solution)/shard_map/dot_general | solution.py:325
  626.7 49.9 %reduce-scatter.9.cloned.1.call-done = bf16[512,1344]{0,1:T(8,128)(2,1)} async-done(((bf16[2048,1344]{0,1:T(8,128)(2,1)}), bf16[512,1344]{0,1:T(8,128)(2,1)}) %reduce-scatter.9.cloned.1.call-update) | async-done | bytes 1376272 | tf_op jit(solution)/shard_map/reduce_scatter | solution.py:324
  678.6 18.3 %convolution_convert_fusion = bf16[2048,2048]{1,0:T(8,128)(2,1)} fusion(bf16[2048,1344]{1,0:T(8,128)(2,1)} %bitcast.358, bf16[2048,1344]{0,1:T(8,128)(2,1)} %all-gather.4.cloned.1.call-done), kind=kOutput, calls=%fused_computation.21 | convolution fusion | flops 11278483456 | bytes 19398656 | tf_op jit(solution)/shard_map/dot_general | solution.py:338
  706.8 45.4 %all-gather.6.cloned.1.call-done = bf16[1024,2048]{1,0:T(8,128)(2,1)} async-done(((bf16[128,2048]{1,0:T(8,128)(2,1)}), bf16[1024,2048]{1,0:T(8,128)(2,1)}) %all-gather.6.cloned.1.call-update) | async-done | bytes 4194320 | tf_op jit(solution)/shard_map/all_gather | solution.py:301
  760.6 115.8 %shard_map.205 = bf16[8,2,2,128,1024]{4,3,2,1,0:T(8,128)(2,1)} custom-call(bf16[2,2,128,1024]{3,2,1,0:T(8,128)(2,1)} %bitcast.361), custom_call_target="tpu_custom_call" | custom-call | tf_op jit(solution)/shard_map/pallas_call | solution.py:151
  876.4 21.6 %reshape.413 = f32[8,512,2,512]{3,2,1,0:T(2,128)} reshape(bf16[8,2,2,128,1024]{4,3,2,1,0:T(8,128)(2,1)} %shard_map.205) | data formatting | bytes 25165824 | tf_op jit(solution)/shard_map/convert_element_type | solution.py:336
  897.9 25.1 %copy.174 = f32[512,2,8,512]{0,3,2,1:T(8,128)} copy(f32[512,2,8,512]{3,1,0,2:T(2,128)} %bitcast.332) | data formatting | bytes 33554432 | tf_op jit(solution)/shard_map/convert_element_type | solution.py:336
  923.0 13.7 %pad_maximum_fusion = f32[512,8512]{0,1:T(8,128)} fusion(f32[512,320]{0,1:T(8,128)} %all-reduce.22.cloned.1.call-done, f32[512,8192]{0,1:T(8,128)} %bitcast.331), kind=kLoop, calls=%fused_computation.9 | loop fusion | flops 4358144 | bytes 34865152 | tf_op jit(solution)/shard_map/concatenate | solution.py:336
  944.1 53.3 %reduce-scatter.7.cloned.1.call-done = bf16[256,2048]{1,0:T(8,128)(2,1)} async-done(((bf16[2048,2048]{1,0:T(8,128)(2,1)}), bf16[256,2048]{1,0:T(8,128)(2,1)}) %reduce-scatter.7.cloned.1.call-update) | async-done | bytes 1048592 | tf_op jit(solution)/shard_map/reduce_scatter | solution.py:337
  1000.0 149.4 %reduce-scatter.5.cloned.1.call-done = bf16[256,2048]{1,0:T(8,128)(2,1)} async-done(((bf16[2048,2048]{1,0:T(8,128)(2,1)}), bf16[256,2048]{1,0:T(8,128)(2,1)}) %reduce-scatter.5.cloned.1.call-update) | async-done | bytes 1048592 | tf_op jit(solution)/shard_map/reduce_scatter | solution.py:284
  1153.8 121.0 %all-reduce.20.cloned.1.call-done = f32[28096]{0:T(1024)} async-done(((f32[28096]{0:T(1024)}), f32[28096]{0:T(1024)}) %all-reduce.20.cloned.1.call-update) | async-done | bytes 112400 | tf_op jit(solution)/shard_map/psum | solution.py:361
  (368 shorter events, 325.1 us)
Async XLA Ops:
  7.2 183.7 %all-gather.4.cloned.1.call-start = ((), (), s32[]{:S(2)}) async-start(), calls=%async_computation.5 | async-start | bytes 6881280 | tf_op jit(solution)/shard_map/all_gather | solution.py:226
  10.7 322.6 %all-reduce.18.cloned.1.call-start = ((), (), s32[]{:S(2)}) async-start(), calls=%async_computation.6 | async-start | bytes 4194304 | tf_op jit(solution)/shard_map/psum | solution.py:263
  14.3 611.9 %reduce-scatter.11.cloned.1.call-start = ((), (), s32[]{:S(2)}) async-start(), calls=%async_computation.12 | async-start | bytes 2621440 | tf_op jit(solution)/shard_map/reduce_scatter | solution.py:291
  17.1 87.9 %copy-start.49 = (f32[2,128]{1,0:T(2,128)}, f32[2,128]{1,0:T(2,128)S(1)}, u32[]{:S(2)}) copy-start(f32[2,128]{1,0:T(2,128)S(1)} %fusion.74) | copy-start | bytes 3076
  20.3 84.7 %copy-start.62 = (f32[64]{0:T(128)S(1)}, f32[64]{0:T(128)}, u32[]{:S(2)}) copy-start(f32[64]{0:T(128)} %param.22) | copy-start | bytes 772
  20.3 84.8 %copy-start.60 = (f32[64]{0:T(128)S(1)}, f32[64]{0:T(128)}, u32[]{:S(2)}) copy-start(f32[64]{0:T(128)} %param.23) | copy-start | bytes 772
  20.3 84.9 %copy-start.63 = (f32[64]{0:T(128)S(1)}, f32[64]{0:T(128)}, u32[]{:S(2)}) copy-start(f32[64]{0:T(128)} %param.24) | copy-start | bytes 772
  20.3 85.1 %copy-start.57 = (s32[2]{0:T(128)S(1)}, s32[2]{0:T(128)}, u32[]{:S(2)}) copy-start(s32[2]{0:T(128)} %param.17) | copy-start | bytes 28
  105.1 147.9 %copy-start.47 = (f32[8]{0:T(128)}, f32[8]{0:T(128)S(1)}, u32[]{:S(2)}) copy-start(f32[8]{0:T(128)S(1)} %dynamic_slice.72) | copy-start | bytes 100
  105.2 147.8 %copy-start.55 = (f32[8]{0:T(128)}, f32[8]{0:T(128)S(1)}, u32[]{:S(2)}) copy-start(f32[8]{0:T(128)S(1)} %fusion.119) | copy-start | bytes 100
  105.4 211.9 %copy-start.39 = (f32[512]{0:T(512)}, f32[512]{0:T(512)S(1)}, u32[]{:S(2)}) copy-start(f32[512]{0:T(512)S(1)} %mul.499) | copy-start | bytes 6148
  107.8 82.1 %slice-start.1 = ((f32[4,4352]{1,0:T(4,128)}), f32[4,256]{1,0:T(4,128)S(1)}, s32[]{:S(2)}) async-start(f32[4,4352]{1,0:T(4,128)} %param.20), calls=%async_computation.15 | async-start | bytes 8192 | tf_op jit(solution)/shard_map/slice | solution.py:239
  107.8 82.2 %slice-start.2 = ((f32[4352]{0:T(1024)}), f32[256]{0:T(256)S(1)}, s32[]{:S(2)}) async-start(f32[4352]{0:T(1024)} %param.21), calls=%async_computation.16 | async-start | bytes 2048 | tf_op jit(solution)/shard_map/slice | solution.py:242
  190.9 142.5 %copy-start.42 = (f32[512]{0:T(512)}, f32[512]{0:T(512)S(1)}, u32[]{:S(2)}) copy-start(f32[512]{0:T(512)S(1)} %dynamic_slice.75) | copy-start | bytes 6148
  261.0 203.6 %copy-start.24 = (f32[2,8,128,8]{2,3,1,0:T(8,128)}, f32[2,8,128,8]{2,3,1,0:T(8,128)S(1)}, u32[]{:S(2)}) copy-start(f32[2,8,128,8]{2,3,1,0:T(8,128)S(1)} %get-tuple-element.372) | copy-start | bytes 196612
  565.2 111.4 %reduce-scatter.9.cloned.1.call-start = ((), (), s32[]{:S(2)}) async-start(), calls=%async_computation.10 | async-start | bytes 6881280 | tf_op jit(solution)/shard_map/reduce_scatter | solution.py:324
  626.1 126.2 %all-gather.6.cloned.1.call-start = ((), (), s32[]{:S(2)}) async-start(), calls=%async_computation.13 | async-start | bytes 4718592 | tf_op jit(solution)/shard_map/all_gather | solution.py:301
  626.7 296.3 %all-reduce.22.cloned.1.call-start = ((), (), s32[]{:S(2)}) async-start(), calls=%async_computation.11 | async-start | bytes 1310720 | tf_op jit(solution)/shard_map/psum | solution.py:335
  678.5 318.9 %reduce-scatter.7.cloned.1.call-start = ((), (), s32[]{:S(2)}) async-start(), calls=%async_computation.8 | async-start | bytes 9437184 | tf_op jit(solution)/shard_map/reduce_scatter | solution.py:337
  696.9 452.6 %reduce-scatter.5.cloned.1.call-start = ((), (), s32[]{:S(2)}) async-start(), calls=%async_computation.7 | async-start | bytes 9437184 | tf_op jit(solution)/shard_map/reduce_scatter | solution.py:284
  752.3 184.4 %all-to-all-start = ((bf16[4,2,128,2048]{3,2,1,0:T(8,128)(2,1)}), bf16[4,2,128,2048]{3,2,1,0:T(8,128)(2,1)}, u32[]{:S(2)}, u32[]{:S(2)}) async-start(bf16[4,2,128,2048]{3,2,1,0:T(8,128)(2,1)} %bitcast.362), calls=%async_computation.4 | async-start | bytes 8388608 | tf_op jit(solution)/shard_map/all_to_all | solution.py:302
  757.3 517.5 %all-reduce.20.cloned.1.call-start = ((), (), s32[]{:S(2)}) async-start(), calls=%async_computation.9 | async-start | bytes 229376 | tf_op jit(solution)/shard_map/psum | solution.py:361
  940.0 57.4 %copy-start.11 = (bf16[2,128,2048]{2,1,0:T(8,128)(2,1)S(1)}, bf16[2,128,2048]{2,1,0:T(8,128)(2,1)}, u32[]{:S(2)}) copy-start(bf16[2,128,2048]{2,1,0:T(8,128)(2,1)} %param.16) | copy-start | bytes 3145732
  940.1 209.4 %copy-start.19 = (bf16[2,128,2048]{2,1,0:T(8,128)(2,1)S(1)}, bf16[2,128,2048]{2,1,0:T(8,128)(2,1)}, u32[]{:S(2)}) copy-start(bf16[2,128,2048]{2,1,0:T(8,128)(2,1)} %param.27) | copy-start | bytes 3145732
  (53 other events, 572.3 us)
Sparse Core Ops, SparseCore 0:
  10.8 44.6 all-gather.3
  58.4 51.3 all-reduce.17
  565.3 28.7 reduce-scatter.10
  626.2 50.3 reduce-scatter.8
  678.8 73.3 all-gather.5
  755.9 80.7 all-reduce.21
  840.3 157.0 reduce-scatter.6
  1001.4 147.9 reduce-scatter.4
  1155.0 119.7 all-reduce.19

commit v2 on v1

v2 whole, which is shorter than its diff:
```python
import functools

import jax
import jax.numpy as jnp
from jax import lax
from jax.experimental import pallas as pl
from jax.experimental.pallas import tpu as pltpu
from jax.sharding import PartitionSpec as P

KW = 4
EPS = 1e-05
HIGHEST = lax.Precision.HIGHEST
MESH = pl.DeviceIdType.MESH


def row_scale(values):
    return lax.rsqrt(jnp.mean(values * values, axis=-1, keepdims=True) + EPS)


def norm_backward(values, row_scales, gain_vec, grad_out):
    weighted = grad_out * gain_vec
    grad_gain = jnp.sum(grad_out * values * row_scales, axis=0)
    grad_values = row_scales * weighted - values * row_scales**3 * jnp.mean(
        weighted * values, axis=-1, keepdims=True
    )
    return (grad_values, grad_gain)


def dot(a, b, ca, cb, precision=None):
    return lax.dot_general(
        a, b, (((ca,), (cb,)), ((), ())), precision=precision, preferred_element_type=jnp.float32
    )


def chunk_front(proj_ref, ext, taps_ref, shift_ref, bias_ref, slope_ref, tri_ref, widths):
    lw, bc = widths
    rows = proj_ref.shape[2]
    ext[8:, :] = proj_ref[0, 0, :, lw : 2 * lw + bc].astype(jnp.float32)
    conv = shift_ref[0:1, :]
    for k in range(KW):
        conv = conv + taps_ref[k : k + 1, :] * ext[5 + k : 5 + k + rows, :]
    conv_sig = lax.logistic(conv)
    act = conv * conv_sig
    step_in = proj_ref[0, 0, :, 2 * lw + bc :].astype(jnp.float32) + bias_ref[0:1, :]
    steps = jnp.maximum(step_in, 0.0) + jnp.log1p(jnp.exp(-jnp.abs(step_in)))
    rates = slope_ref[0:1, :] * steps
    cum = dot(tri_ref[...], rates, 1, 0, HIGHEST)
    return conv, conv_sig, act, step_in, steps, rates, cum


def head_masks(rows, head_size):
    lane = lax.broadcasted_iota(jnp.int32, (rows, 128), 1)
    row = lax.broadcasted_iota(jnp.int32, (rows, rows), 0)
    col = lax.broadcasted_iota(jnp.int32, (rows, rows), 1)
    return lane, row >= col


def forward_kernel(
    widths,
    head_size,
    proj_ref,
    taps_ref,
    shift_ref,
    bias_ref,
    slope_ref,
    skip_ref,
    spread_ref,
    tri_ref,
    gated_ref,
    y_ref,
    enter_ref,
    state,
    ext,
    halo,
):
    lw, bc = widths
    bf16, f32 = jnp.bfloat16, jnp.float32
    rows = proj_ref.shape[2]
    per_tile = 128 // head_size

    @pl.when(pl.program_id(1) == 0)
    def _():
        state[...] = jnp.zeros_like(state)
        halo[...] = jnp.zeros_like(halo)

    ext[0:8, :] = halo[...]
    _, _, act, _, steps, _, cum = chunk_front(
        proj_ref, ext, taps_ref, shift_ref, bias_ref, slope_ref, tri_ref, widths
    )
    halo[...] = ext[rows : rows + 8, :]
    x = act[:, :lw]
    xb = x.astype(bf16)
    b_rows = act[:, lw : lw + bc // 2].astype(bf16)
    c_rows = act[:, lw + bc // 2 :].astype(bf16)
    cum_t, steps_t = cum.T, steps.T
    last = cum[rows - 1 : rows, :]
    grow = dot(jnp.exp(cum).astype(bf16), spread_ref[...], 1, 0)
    tail = dot((jnp.exp(last - cum) * steps).astype(bf16), spread_ref[...], 1, 0)
    scores = dot(c_rows, b_rows, 1, 1)
    entering = state[...].astype(bf16)
    enter_ref[0, 0] = entering
    y = dot(c_rows, entering, 1, 1) * grow + skip_ref[0:1, :] * x
    added = dot((x * tail).astype(bf16), b_rows, 0, 0)
    lane, causal = head_masks(rows, head_size)
    gate = proj_ref[0, 0, :, :lw].astype(f32)
    silu_gate = gate * lax.logistic(gate)
    for tile in range(lw // 128):
        cols = slice(tile * 128, (tile + 1) * 128)
        inner = None
        for sub in range(per_tile):
            head = tile * per_tile + sub
            log_decay = cum[:, head : head + 1] - cum_t[head : head + 1, :]
            decay = jnp.exp(jnp.where(causal, log_decay, -1e30))
            weights = (scores * decay * steps_t[head : head + 1, :]).astype(bf16)
            part = dot(weights, xb[:, cols], 1, 0)
            inner = part if inner is None else jnp.where(lane >= sub * head_size, part, inner)
            span = slice(head * head_size, (head + 1) * head_size)
            state[span, :] = (
                jnp.exp(cum[rows - 1 : rows, head : head + 1]) * state[span, :] + added[span, :]
            )
        y_tile = y[:, cols] + inner
        y_ref[0, 0, :, cols] = y_tile.astype(bf16)
        gated_ref[0, 0, :, cols] = (y_tile * silu_gate[:, cols]).astype(bf16)


def backward_kernel(
    widths,
    head_size,
    chunks,
    proj_ref,
    before_ref,
    y_ref,
    enter_ref,
    grad_ref,
    taps_ref,
    shift_ref,
    bias_ref,
    slope_ref,
    skip_ref,
    spread_ref,
    fold_ref,
    tri_ref,
    upper_ref,
    out_ref,
    taps_acc,
    skip_acc,
    head_acc,
    lam,
    ext,
    later,
    after,
):
    lw, bc = widths
    state_size = bc // 2
    bf16, f32 = jnp.bfloat16, jnp.float32
    rows = proj_ref.shape[2]
    per_tile = 128 // head_size
    chunk = chunks - 1 - pl.program_id(1)

    @pl.when((pl.program_id(0) == 0) & (pl.program_id(1) == 0))
    def _():
        taps_acc[...] = jnp.zeros_like(taps_acc)
        skip_acc[...] = jnp.zeros_like(skip_acc)
        head_acc[...] = jnp.zeros_like(head_acc)

    @pl.when(pl.program_id(1) == 0)
    def _():
        lam[...] = jnp.zeros_like(lam)
        after[...] = jnp.zeros_like(after)

    ext[0:8, :] = jnp.where(
        chunk > 0, before_ref[0, 0, 8:16, lw : 2 * lw + bc].astype(f32), 0.0
    )
    conv, conv_sig, act, step_in, steps, rates, cum = chunk_front(
        proj_ref, ext, taps_ref, shift_ref, bias_ref, slope_ref, tri_ref, widths
    )
    x = act[:, :lw]
    xb = x.astype(bf16)
    b_rows = act[:, lw : lw + state_size].astype(bf16)
    c_rows = act[:, lw + state_size :].astype(bf16)
    cum_t, steps_t = cum.T, steps.T
    last = cum[rows - 1 : rows, :]
    to_end = jnp.exp(last - cum)
    tail_heads = to_end * steps
    grow = dot(jnp.exp(cum).astype(bf16), spread_ref[...], 1, 0)
    tail = dot(tail_heads.astype(bf16), spread_ref[...], 1, 0)
    scores = dot(c_rows, b_rows, 1, 1)

    gate = proj_ref[0, 0, :, :lw].astype(f32)
    gate_sig = lax.logistic(gate)
    grad = grad_ref[0, 0].astype(f32)
    y_grad = grad * gate * gate_sig
    out_ref[0, 0, :, :lw] = (
        grad * y_ref[0, 0].astype(f32) * (gate_sig * (1.0 + gate * (1.0 - gate_sig)))
    ).astype(bf16)
    yb = y_grad.astype(bf16)

    entering = enter_ref[0, 0]
    grown = y_grad * grow
    grown_b = grown.astype(bf16)
    c_grad = dot(grown_b, entering, 1, 0)
    carried = dot((grown * dot(c_rows, entering, 1, 1)).astype(bf16), fold_ref[...], 1, 0)
    lam_now = lam[...]
    lam_b = lam_now.astype(bf16)
    from_lam = dot(b_rows, lam_b, 1, 1)
    b_grad = dot((x * tail).astype(bf16), lam_b, 1, 0)
    x_lam = dot((x * from_lam).astype(bf16), fold_ref[...], 1, 0)
    x_grad = skip_ref[0:1, :] * y_grad + tail * from_lam
    skip_acc[0:1, :] += jnp.sum(y_grad * x, axis=0, keepdims=True)
    ones = jnp.ones((8, state_size), bf16)
    kept = dot(
        dot(ones, (lam_now * entering.astype(f32)).astype(bf16), 1, 1),
        fold_ref[...].astype(f32),
        1,
        0,
        HIGHEST,
    )
    through = jnp.exp(last) * kept[0:1, :]
    lam_add = dot(grown_b, c_rows, 0, 0)

    lane, causal = head_masks(rows, head_size)
    score_grad = None
    row_sums = jnp.zeros((rows, 128), f32)
    col_sums = []
    x_tiles = []
    for tile in range(lw // 128):
        cols = slice(tile * 128, (tile + 1) * 128)
        inner = None
        for sub in range(per_tile):
            head = tile * per_tile + sub
            log_decay = cum[:, head : head + 1] - cum_t[head : head + 1, :]
            decay = jnp.exp(jnp.where(causal, log_decay, -1e30))
            step_row = steps_t[head : head + 1, :]
            weights = (scores * decay * step_row).astype(bf16)
            inside = (lane >= sub * head_size) & (lane < (sub + 1) * head_size)
            y_head = jnp.where(inside, yb[:, cols], jnp.zeros_like(yb[:, cols]))
            weights_grad = dot(y_head, xb[:, cols], 1, 1)
            part = dot(weights, yb[:, cols], 0, 0)
            inner = part if inner is None else jnp.where(lane >= sub * head_size, part, inner)
            decayed = weights_grad * decay
            stepped = decayed * step_row
            score_grad = stepped if score_grad is None else score_grad + stepped
            col_sums.append(jnp.sum(decayed * scores, axis=0, keepdims=True))
            row_sum = jnp.sum(stepped * scores, axis=1, keepdims=True)
            row_sums = row_sums + jnp.where(lane == head, row_sum, 0.0)
            span = slice(head * head_size, (head + 1) * head_size)
            lam[span, :] = (
                jnp.exp(cum[rows - 1 : rows, head : head + 1]) * lam_now[span, :] + lam_add[span, :]
            )
        x_tiles.append(x_grad[:, cols] + inner)
    col_sums.append(jnp.zeros((rows - len(col_sums), rows), f32))
    col_sum = jnp.concatenate(col_sums, axis=0).T
    source = row_sums - steps * col_sum + carried
    rates_grad = (
        dot(upper_ref[...], source, 1, 0, HIGHEST)
        + dot(1.0 - upper_ref[...], tail_heads * x_lam, 1, 0, HIGHEST)
        + through
    )
    steps_grad = col_sum + to_end * x_lam + rates_grad * slope_ref[0:1, :]
    raw_grad = steps_grad * lax.logistic(step_in)
    out_ref[0, 0, :, 2 * lw + bc :] = raw_grad.astype(bf16)
    head_acc[0:1, :] += jnp.sum(raw_grad, axis=0, keepdims=True)
    head_acc[1:2, :] += jnp.sum(rates_grad * rates, axis=0, keepdims=True)
    score_b = score_grad.astype(bf16)
    c_grad = c_grad + dot(score_b, b_rows, 1, 0)
    b_grad = b_grad + dot(score_b, c_rows, 0, 0)
    act_grad = jnp.concatenate(x_tiles + [b_grad, c_grad], axis=1)
    conv_grad = act_grad * (conv_sig * (1.0 + conv * (1.0 - conv_sig)))
    later[0:rows, :] = conv_grad
    later[rows : rows + 8, :] = after[...]
    after[...] = conv_grad[0:8, :]
    total = None
    for k in range(KW):
        term = taps_ref[k : k + 1, :] * later[3 - k : 3 - k + rows, :]
        total = term if total is None else total + term
        taps_acc[k : k + 1, :] += jnp.sum(conv_grad * ext[5 + k : 5 + k + rows, :], axis=0, keepdims=True)
    taps_acc[KW : KW + 1, :] += jnp.sum(conv_grad, axis=0, keepdims=True)
    out_ref[0, 0, :, lw : 2 * lw + bc] = total.astype(bf16)


def whole_spec(array):
    return pl.BlockSpec(array.shape, lambda q, c: (0,) * array.ndim)


def scan_tables(rows, local_width, head_size):
    head_of = jnp.arange(local_width) // head_size
    spread = (jnp.arange(128)[:, None] == head_of[None, :]).astype(jnp.bfloat16)
    tri = (jnp.arange(rows)[:, None] >= jnp.arange(rows)[None, :]).astype(jnp.float32)
    return spread, spread.T, tri, tri.T


def scan_forward(proj, taps, shift, bias, slope, skip, spread, tri, widths, head_size):
    chunks, seqs, rows, _ = proj.shape
    lw, bc = widths
    block = lambda *tail: pl.BlockSpec((1, 1) + tail, lambda q, c: (c, q, 0, 0))
    tables = (taps, shift, bias, slope, skip, spread, tri)
    return pl.pallas_call(
        functools.partial(forward_kernel, widths, head_size),
        grid=(seqs, chunks),
        in_specs=[block(rows, proj.shape[3])] + [whole_spec(t) for t in tables],
        out_specs=[block(rows, lw), block(rows, lw), block(lw, bc // 2)],
        out_shape=[
            jax.ShapeDtypeStruct((chunks, seqs, rows, lw), jnp.bfloat16),
            jax.ShapeDtypeStruct((chunks, seqs, rows, lw), jnp.bfloat16),
            jax.ShapeDtypeStruct((chunks, seqs, lw, bc // 2), jnp.bfloat16),
        ],
        scratch_shapes=[
            pltpu.VMEM((lw, bc // 2), jnp.float32),
            pltpu.VMEM((rows + 8, lw + bc), jnp.float32),
            pltpu.VMEM((8, lw + bc), jnp.float32),
        ],
        compiler_params=pltpu.CompilerParams(vmem_limit_bytes=48 * 2**20),
        name="scan_forward",
    )(proj, *tables)


def scan_backward(
    proj, y, enter, grad, taps, shift, bias, slope, skip, spread, fold, tri, upper, widths, head_size
):
    chunks, seqs, rows, cols = proj.shape
    lw, bc = widths
    block = lambda *tail: pl.BlockSpec((1, 1) + tail, lambda q, c: (chunks - 1 - c, q, 0, 0))
    before = pl.BlockSpec(
        (1, 1, 16, cols),
        lambda q, c: (jnp.maximum(chunks - 2 - c, 0), q, rows // 16 - 1, 0),
    )
    tables = (taps, shift, bias, slope, skip, spread, fold, tri, upper)
    sums = [(8, lw + bc), (8, lw), (8, 128)]
    return pl.pallas_call(
        functools.partial(backward_kernel, widths, head_size, chunks),
        grid=(seqs, chunks),
        in_specs=[block(rows, cols), before, block(rows, lw), block(lw, bc // 2), block(rows, lw)]
        + [whole_spec(t) for t in tables],
        out_specs=[block(rows, cols)] + [pl.BlockSpec(s, lambda q, c: (0, 0)) for s in sums],
        out_shape=[jax.ShapeDtypeStruct(proj.shape, jnp.bfloat16)]
        + [jax.ShapeDtypeStruct(s, jnp.float32) for s in sums],
        scratch_shapes=[
            pltpu.VMEM((lw, bc // 2), jnp.float32),
            pltpu.VMEM((rows + 8, lw + bc), jnp.float32),
            pltpu.VMEM((rows + 8, lw + bc), jnp.float32),
            pltpu.VMEM((8, lw + bc), jnp.float32),
        ],
        compiler_params=pltpu.CompilerParams(vmem_limit_bytes=48 * 2**20),
        name="scan_backward",
    )(proj, proj, y, enter, grad, *tables)


def ring_pos(index, size):
    row, side = index // 2, index % 2
    return row + side * (size - 1 - 2 * row)


def ring_index(pos, size):
    side = pos // (size // 2)
    row = pos + side * (size - 1 - 2 * pos)
    return row * 2 + side


def greet(peers):
    barrier = pltpu.get_barrier_semaphore()
    for peer in peers:
        pl.semaphore_signal(barrier, inc=1, device_id=peer, device_id_type=MESH)
    pl.semaphore_wait(barrier, len(peers))


def push(source, target, send_sem, recv_sem, peer):
    return pltpu.make_async_remote_copy(
        source, target, send_sem, recv_sem, device_id=peer, device_id_type=MESH
    )


def neighbours(size):
    me, group = lax.axis_index("seq"), lax.axis_index("wa")
    pos = ring_pos(me, size)
    right = (ring_index((pos + 1) % size, size), group)
    left = (ring_index((pos + size - 1) % size, size), group)
    return me, group, pos, right, left


def others(index, size):
    return [(index + offset) % size for offset in range(1, size)]


ANY = pl.BlockSpec(memory_space=pl.ANY)
VMEM = pl.BlockSpec(memory_space=pltpu.VMEM)


def comm_params(collective_id, megabytes=None):
    limit = None if megabytes is None else megabytes * 2**20
    return pltpu.CompilerParams(
        collective_id=collective_id, has_side_effects=True, vmem_limit_bytes=limit
    )


class RingGather:
    def __init__(self, size, x_ref, o_ref, send_sem, recv_sem, local_sem):
        self.size, self.x, self.o = size, x_ref, o_ref
        self.send, self.recv, self.local = send_sem, recv_sem, local_sem
        self.chunks = x_ref.shape[1]
        self.me, _, self.pos, self.right, self.left = neighbours(size)

    def copy(self, step, chunk, way, first=False):
        size = self.size
        if way == 0:
            block, peer = ring_index((self.pos - step + size) % size, size), self.right
        else:
            block, peer = ring_index((self.pos + step) % size, size), self.left
        source = self.x.at[way, chunk] if first else self.o.at[block, way, chunk]
        return push(
            source,
            self.o.at[block, way, chunk],
            self.send.at[step, chunk, way],
            self.recv.at[step, chunk, way],
            peer,
        )

    def start(self):
        self.kept = pltpu.make_async_copy(self.x, self.o.at[self.me], self.local)
        self.kept.start()
        for chunk in range(self.chunks):
            for way in range(2):
                self.copy(0, chunk, way, True).start()

    def advance(self, step):
        for chunk in range(self.chunks):
            for way in range(2):
                self.copy(step - 1, chunk, way).wait_recv()
                self.copy(step, chunk, way).start()

    def finish(self):
        last = self.size - 2
        for chunk in range(self.chunks):
            for way in range(2):
                self.copy(last, chunk, way).wait_recv()

        def drain(step, carry):
            for chunk in range(self.chunks):
                for way in range(2):
                    self.copy(step, chunk, way).wait_send()
            return carry

        lax.fori_loop(0, self.size - 1, drain, 0)
        self.kept.wait()


def ring_parts(x, chunks):
    return x.reshape(2, chunks, x.shape[0] // (2 * chunks), x.shape[1])


def ring_sems(size, chunks):
    return [
        pltpu.SemaphoreType.DMA((size - 1, chunks, 2)),
        pltpu.SemaphoreType.DMA((size - 1, chunks, 2)),
        pltpu.SemaphoreType.DMA,
    ]


def gather_kernel(size, x_ref, o_ref, send_sem, recv_sem, local_sem):
    _, _, _, right, left = neighbours(size)
    greet([right, left])
    ring = RingGather(size, x_ref, o_ref, send_sem, recv_sem, local_sem)
    ring.start()
    lax.fori_loop(1, size - 1, lambda step, carry: (ring.advance(step), carry)[1], 0)
    ring.finish()


def ring_gather(x, collective_id):
    size = lax.axis_size("seq")
    parts = ring_parts(x, 2)
    out = pl.pallas_call(
        functools.partial(gather_kernel, size),
        out_shape=jax.ShapeDtypeStruct((size,) + parts.shape, x.dtype),
        in_specs=[ANY],
        out_specs=ANY,
        scratch_shapes=ring_sems(size, 2),
        compiler_params=comm_params(collective_id),
        name="gather_rows",
    )(parts)
    return out.reshape(size * x.shape[0], x.shape[1])


def total_kernel(size, x_ref, o_ref, landing, send_sem, recv_sem):
    me, group = lax.axis_index("seq"), lax.axis_index("wa")
    peers = [(index, group) for index in others(me, size)]
    greet(peers)
    copies = [
        push(x_ref, landing.at[k], send_sem.at[k], recv_sem.at[k], peer)
        for k, peer in enumerate(peers)
    ]
    for copy in copies:
        copy.start()
    total = x_ref[...]
    for k, copy in enumerate(copies):
        copy.wait_recv()
        total = total + landing[k]
    o_ref[...] = total
    for copy in copies:
        copy.wait_send()


def seq_total(x, collective_id):
    size = lax.axis_size("seq")
    return pl.pallas_call(
        functools.partial(total_kernel, size),
        out_shape=jax.ShapeDtypeStruct(x.shape, x.dtype),
        in_specs=[VMEM],
        out_specs=VMEM,
        scratch_shapes=[
            pltpu.VMEM((size - 1,) + x.shape, x.dtype),
            pltpu.SemaphoreType.DMA((size - 1,)),
            pltpu.SemaphoreType.DMA((size - 1,)),
        ],
        compiler_params=comm_params(collective_id),
        name="seq_total",
    )(x)


def reduce_kernel(
    size,
    groups,
    grad_ref,
    weight_ref,
    piece_ref,
    part_ref,
    rows_ref,
    pieces_ref,
    landing_ref,
    slots,
    first,
    send_sem,
    recv_sem,
    piece_send,
    piece_recv,
    piece_local,
    part_send,
    part_recv,
):
    me, group, pos, right, left = neighbours(size)
    mates = [(me, index) for index in others(group, groups)]
    greet([right, left] + mates)
    tiles, tile = slots.shape[2], slots.shape[4]
    parts = [
        push(part_ref.at[mate[1]], landing_ref.at[k], part_send.at[k], part_recv.at[k], mate)
        for k, mate in enumerate(mates)
    ]
    for copy in parts:
        copy.start()
    ring = RingGather(size, piece_ref, pieces_ref, piece_send, piece_recv, piece_local)
    ring.start()

    def term(block, way, at):
        columns = pl.ds(pl.multiple_of(at * tile, tile), tile)
        return lax.dot_general(
            grad_ref[block, way],
            weight_ref[columns, :],
            (((1,), (1,)), ((), ())),
            preferred_element_type=jnp.float32,
        )

    def target(step, way):
        shift = (pos - 1 - step + 2 * size) if way == 0 else (pos + 1 + step)
        return ring_index(shift % size, size)

    def hop(step, way, at, source):
        return push(
            source,
            slots.at[step, way, at],
            send_sem.at[step, way, at],
            recv_sem.at[step, way, at],
            right if way == 0 else left,
        )

    def begin(at, carry):
        for way in range(2):
            first[way, at] = term(target(0, way), way, at).astype(jnp.bfloat16)
            hop(0, way, at, first.at[way, at]).start()
        return carry

    lax.fori_loop(0, tiles, begin, 0)

    def advance(step, carry):
        def one(at, inner):
            for way in range(2):
                own = term(target(step, way), way, at)
                hop(step - 1, way, at, first.at[way, at]).wait_recv()
                slots[step - 1, way, at] = (
                    slots[step - 1, way, at].astype(jnp.float32) + own
                ).astype(jnp.bfloat16)
                hop(step, way, at, slots.at[step - 1, way, at]).start()
            return inner

        lax.fori_loop(0, tiles, one, 0)
        ring.advance(step)
        return carry

    lax.fori_loop(1, size - 1, advance, 0)

    def end(at, carry):
        columns = pl.ds(pl.multiple_of(at * tile, tile), tile)
        for way in range(2):
            own = term(me, way, at)
            hop(size - 2, way, at, first.at[way, at]).wait_recv()
            rows_ref[way, :, columns] = slots[size - 2, way, at].astype(jnp.float32) + own
        return carry

    lax.fori_loop(0, tiles, end, 0)

    def drain(step, carry):
        def one(at, inner):
            for way in range(2):
                hop(step, way, at, first.at[way, at]).wait_send()
            return inner

        return lax.fori_loop(0, tiles, one, carry)

    lax.fori_loop(0, size - 1, drain, 0)
    ring.finish()
    for copy in parts:
        copy.wait()


def reduce_rows(grad, weight, piece, part, collective_id):
    size, groups = lax.axis_size("seq"), lax.axis_size("wa")
    _, ways, rows, _ = grad.shape
    width = weight.shape[0]
    tile = 512
    tiles = width // tile
    pieces = ring_parts(piece, 1)
    bf16 = jnp.bfloat16
    return pl.pallas_call(
        functools.partial(reduce_kernel, size, groups),
        out_shape=[
            jax.ShapeDtypeStruct((ways, rows, width), jnp.float32),
            jax.ShapeDtypeStruct((size,) + pieces.shape, bf16),
            jax.ShapeDtypeStruct((groups - 1,) + part.shape[1:], bf16),
        ],
        in_specs=[VMEM, VMEM, ANY, ANY],
        out_specs=[VMEM, ANY, ANY],
        scratch_shapes=[
            pltpu.VMEM((size - 1, 2, tiles, rows, tile), bf16),
            pltpu.VMEM((2, tiles, rows, tile), bf16),
            pltpu.SemaphoreType.DMA((size - 1, 2, tiles)),
            pltpu.SemaphoreType.DMA((size - 1, 2, tiles)),
        ]
        + ring_sems(size, 1)
        + [pltpu.SemaphoreType.DMA((groups - 1,)), pltpu.SemaphoreType.DMA((groups - 1,))],
        compiler_params=comm_params(collective_id, 60),
        name="reduce_rows",
    )(grad, weight, pieces, part)


def spread_kernel(
    size,
    groups,
    main_ref,
    pieces_ref,
    shared_ref,
    small_ref,
    gathered_ref,
    owned_ref,
    shared_out,
    small_out,
    shared_land,
    shared_sum,
    small_land,
    small_sum,
    main_send,
    main_recv,
    main_local,
    piece_send,
    piece_recv,
    piece_local,
    pair_send,
    pair_recv,
    mate_send,
    mate_recv,
):
    me, group, pos, right, left = neighbours(size)
    mates = [(me, index) for index in others(group, groups)]
    peers = [(index, group) for index in others(me, size)]
    greet(mates + peers)
    ring = RingGather(size, main_ref, gathered_ref, main_send, main_recv, main_local)
    ring.start()
    owned = [
        push(pieces_ref.at[mate[1]], owned_ref.at[group], piece_send.at[k], piece_recv.at[k], mate)
        for k, mate in enumerate(mates)
    ]
    kept = pltpu.make_async_copy(pieces_ref.at[group], owned_ref.at[group], piece_local)
    small_in = [
        push(small_ref, small_land.at[k], mate_send.at[k], mate_recv.at[k], mate)
        for k, mate in enumerate(mates)
    ]
    shared_in = [
        push(
            shared_ref.at[peer[0]], shared_land.at[k], pair_send.at[0, k], pair_recv.at[0, k], peer
        )
        for k, peer in enumerate(peers)
    ]
    for copy in small_in + shared_in:
        copy.start()
    kept.start()
    for copy in owned:
        copy.start()
    total = small_ref[...]
    for k, copy in enumerate(small_in):
        copy.wait_recv()
        total = total + small_land[k]
    small_sum[...] = total
    small_out[pl.ds(me, 1)] = total[None]
    total = shared_ref[me].astype(jnp.float32)
    for k, copy in enumerate(shared_in):
        copy.wait_recv()
        total = total + shared_land[k].astype(jnp.float32)
    shared_sum[...] = total.astype(jnp.bfloat16)
    shared_out[pl.ds(me, 1)] = total.astype(jnp.bfloat16)[None]
    second = []
    for k, peer in enumerate(peers):
        second.append(
            push(small_sum, small_out.at[me], pair_send.at[1, k], pair_recv.at[1, k], peer)
        )
        second.append(
            push(shared_sum, shared_out.at[me], pair_send.at[2, k], pair_recv.at[2, k], peer)
        )
    for copy in second:
        copy.start()
    lax.fori_loop(1, size - 1, lambda step, carry: (ring.advance(step), carry)[1], 0)
    ring.finish()
    for copy in small_in + shared_in:
        copy.wait_send()
    for copy in second + owned:
        copy.wait()
    kept.wait()


def spread_grads(main, pieces, shared, small, collective_id):
    size, groups = lax.axis_size("seq"), lax.axis_size("wa")
    parts = ring_parts(main, 2)
    bf16, f32 = jnp.bfloat16, jnp.float32
    DMA = pltpu.SemaphoreType.DMA
    return pl.pallas_call(
        functools.partial(spread_kernel, size, groups),
        out_shape=[
            jax.ShapeDtypeStruct((size,) + parts.shape, bf16),
            jax.ShapeDtypeStruct(pieces.shape, bf16),
            jax.ShapeDtypeStruct(shared.shape, bf16),
            jax.ShapeDtypeStruct((size,) + small.shape, f32),
        ],
        in_specs=[ANY, ANY, VMEM, VMEM],
        out_specs=[ANY, ANY, VMEM, VMEM],
        scratch_shapes=[
            pltpu.VMEM((size - 1,) + shared.shape[1:], bf16),
            pltpu.VMEM(shared.shape[1:], bf16),
            pltpu.VMEM((groups - 1,) + small.shape, f32),
            pltpu.VMEM(small.shape, f32),
        ]
        + ring_sems(size, 2)
        + [
            DMA((groups - 1,)),
            DMA((groups - 1,)),
            DMA,
            DMA((3, size - 1)),
            DMA((3, size - 1)),
            DMA((groups - 1,)),
            DMA((groups - 1,)),
        ],
        compiler_params=comm_params(collective_id, 32),
        name="spread_grads",
    )(parts, pieces, shared, small)


def assemble_kernel(lw, gathered_ref, shared_ref, o_ref):
    size = gathered_ref.shape[0]
    inner = size * lw
    for block in range(size):
        for half in range(2):
            at = half * inner + block * lw
            o_ref[:, at : at + lw] = gathered_ref[block, :, half * lw : (half + 1) * lw].astype(
                jnp.float32
            )
    tail = o_ref.shape[1] - 2 * inner
    o_ref[:, 2 * inner :] = shared_ref[:, :tail].astype(jnp.float32)


def assemble_in(gathered, shared, columns):
    size, rows, both = gathered.shape
    step = 64
    return pl.pallas_call(
        functools.partial(assemble_kernel, both // 2),
        grid=(rows // step,),
        in_specs=[
            pl.BlockSpec((size, step, both), lambda i: (0, i, 0)),
            pl.BlockSpec((step, shared.shape[1]), lambda i: (i, 0)),
        ],
        out_specs=pl.BlockSpec((step, columns), lambda i: (i, 0)),
        out_shape=jax.ShapeDtypeStruct((rows, columns), jnp.float32),
        compiler_params=pltpu.CompilerParams(vmem_limit_bytes=40 * 2**20),
        name="assemble_in",
    )(gathered, shared)


def widen_kernel(x_ref, o_ref):
    o_ref[...] = x_ref[0, 0].astype(jnp.float32)


def assemble_out(owned):
    groups, count, rows, width = owned.shape
    return pl.pallas_call(
        widen_kernel,
        grid=(count, groups),
        in_specs=[pl.BlockSpec((1, 1, rows, width), lambda t, g: (g, t, 0, 0))],
        out_specs=pl.BlockSpec((rows, width), lambda t, g: (t * groups + g, 0)),
        out_shape=jax.ShapeDtypeStruct((groups * count * rows, width), jnp.float32),
        name="assemble_out",
    )(owned)


def body(
    tokens,
    lengths,
    norm_gain,
    in_weight,
    conv_weight,
    conv_bias,
    dt_bias,
    a_log,
    skip_gain,
    out_gain,
    out_weight,
    cotangent,
):
    seqs_here, slot_rows, width = tokens.shape
    row_count = seqs_here * slot_rows
    inner_width = out_gain.shape[0]
    channels = conv_bias.shape[0]
    bc_width = channels - inner_width
    state_size = bc_width // 2
    head_count = dt_bias.shape[0]
    head_size = inner_width // head_count
    seq_devices = lax.axis_size("seq")
    group_devices = lax.axis_size("wa")
    seq_index = lax.axis_index("seq")
    length = seq_devices * slot_rows
    local_heads = head_count // seq_devices
    local_width = local_heads * head_size
    channel_start = seq_index * local_width
    head_start = seq_index * local_heads
    bf16, f32 = jnp.bfloat16, jnp.float32

    def take(array, start, size, axis):
        return lax.dynamic_slice_in_dim(array, start, size, axis)

    positions = seq_index * slot_rows + jnp.arange(slot_rows)
    valid_rows = (positions[None, :] < lengths[:, None]).astype(f32).reshape(row_count, 1)
    flat_tokens = tokens.reshape(row_count, width).astype(f32)
    in_scale = row_scale(flat_tokens)
    normed = (flat_tokens * in_scale * norm_gain).astype(bf16)
    normed_all = ring_gather(normed, 0)
    cot_rows = cotangent.reshape(row_count, width)
    branch_grad = ring_gather(cot_rows * valid_rows.astype(bf16), 1)

    dt_pad = jnp.zeros((in_weight.shape[0], 128 - local_heads), bf16)
    local_columns = jnp.concatenate(
        [
            take(in_weight, channel_start, local_width, 1),
            take(in_weight, inner_width + channel_start, local_width, 1),
            in_weight[:, 2 * inner_width : 2 * inner_width + bc_width],
            take(in_weight, 2 * inner_width + bc_width + head_start, local_heads, 1),
            dt_pad,
        ],
        axis=1,
    )
    in_columns = lax.all_gather(local_columns, "wa", axis=0, tiled=True)
    columns_here = in_columns.shape[1]
    blocks = (seq_devices, seqs_here, slot_rows)
    projected = (
        jnp.dot(normed_all, in_columns, preferred_element_type=f32)
        .astype(bf16)
        .reshape(blocks + (columns_here,))
    )

    def lanes(part):
        return jnp.pad(part[None], ((0, 7), (0, 128 - local_heads)))

    taps = jnp.pad(
        jnp.concatenate(
            [take(conv_weight, channel_start, local_width, 1), conv_weight[:, inner_width:]], axis=1
        ),
        ((0, 8 - KW), (0, 0)),
    )
    shift = jnp.concatenate(
        [take(conv_bias, channel_start, local_width, 0), conv_bias[inner_width:]]
    )[None]
    bias = lanes(take(dt_bias, head_start, local_heads, 0))
    slope = lanes(-jnp.exp(take(a_log, head_start, local_heads, 0)))
    skip = jnp.repeat(take(skip_gain, head_start, local_heads, 0), head_size)[None]
    gain_local = take(out_gain, channel_start, local_width, 0)
    spread, fold, tri, upper = scan_tables(slot_rows, local_width, head_size)
    widths = (local_width, bc_width)
    gated_heads, y_heads, entering = scan_forward(
        projected, taps, shift, bias, slope, skip, spread, tri, widths, head_size
    )
    gated = gated_heads.reshape(-1, local_width).astype(f32)

    out_full = lax.all_gather(out_weight, "wa", axis=0, tiled=True)
    out_rows = take(out_full, channel_start, local_width, 0)
    out_grad = lax.dot_general(
        branch_grad, out_rows, (((1,), (1,)), ((), ())), preferred_element_type=f32
    )
    weighted = out_grad * gain_local
    sums = seq_total(
        jnp.stack(
            [jnp.sum(gated * gated, axis=-1), jnp.sum(weighted * gated, axis=-1)]
        ).reshape(-1, 128),
        2,
    ).reshape(2, -1)
    out_scale = lax.rsqrt(sums[0] / inner_width + EPS)[:, None]
    mean_dot = (sums[1] / inner_width)[:, None]
    normed_out = (gated * out_scale * gain_local).astype(bf16)
    out_gain_part = jnp.sum(out_grad * gated * out_scale, axis=0)
    gated_grad = (out_scale * weighted - gated * out_scale**3 * mean_dot).astype(bf16)

    swapped = lax.all_to_all(
        normed_out.reshape(seq_devices, row_count, local_width), "seq", 0, 0, tiled=True
    )
    out_weight_part = lax.psum_scatter(
        lax.dot_general(
            normed_out, branch_grad, (((0,), (0,)), ((), ())), preferred_element_type=f32
        ).astype(bf16),
        "wa",
        scatter_dimension=0,
        tiled=True,
    )
    proj_grad, taps_sum, skip_sum, head_sum = scan_backward(
        projected,
        y_heads,
        entering,
        gated_grad.reshape(blocks + (local_width,)),
        taps,
        shift,
        bias,
        slope,
        skip,
        spread,
        fold,
        tri,
        upper,
        widths,
        head_size,
    )
    proj_grad = proj_grad.reshape(-1, columns_here)
    conv_w_grad, conv_b_grad = taps_sum[:KW], taps_sum[KW]
    skip_grad = jnp.sum(skip_sum[0].reshape(local_heads, head_size), axis=1)
    shift_grad, rates_grad = head_sum[0, :local_heads], head_sum[1, :local_heads]
    in_rows = in_weight.shape[0]
    in_weight_part = (
        lax.dot_general(
            normed_all, proj_grad, (((0,), (0,)), ((), ())), preferred_element_type=f32
        )
        .astype(bf16)
        .reshape(group_devices, in_rows, columns_here)
    )
    branch = jnp.dot(
        jnp.swapaxes(swapped, 0, 1).reshape(row_count, inner_width),
        out_full,
        preferred_element_type=f32,
    )
    mixed_out = (flat_tokens + valid_rows * branch).astype(bf16).reshape(tokens.shape)
    normed_grad, pieces, landed = reduce_rows(
        proj_grad.reshape(blocks + (columns_here,)),
        in_columns,
        out_weight_part,
        in_weight_part,
        3,
    )
    normed_grad = normed_grad.reshape(row_count, width)
    in_weight_sum = lax.dynamic_index_in_dim(
        in_weight_part, lax.axis_index("wa"), 0, keepdims=False
    ).astype(f32) + jnp.sum(landed.astype(f32), axis=0)
    token_grad, norm_gain_grad = norm_backward(flat_tokens, in_scale, norm_gain, normed_grad)
    token_grad = token_grad + cot_rows.astype(f32)

    dt_wide = lax.dynamic_update_slice_in_dim(
        jnp.zeros((in_rows, 128), f32),
        in_weight_sum[:, 2 * local_width + bc_width :][:, :local_heads],
        head_start,
        1,
    )
    shared = jnp.concatenate(
        [in_weight_sum[:, 2 * local_width : 2 * local_width + bc_width], dt_wide], axis=1
    ).astype(bf16)
    shared_columns = shared.shape[1]
    heads = jnp.stack(
        [
            jnp.pad(part, (0, 128 - local_heads))
            for part in (shift_grad, rates_grad, skip_grad)
        ]
    )
    own_parts = [conv_w_grad[:, :local_width], conv_b_grad[:local_width], out_gain_part, heads]
    sum_parts = [conv_w_grad[:, local_width:], conv_b_grad[local_width:], norm_gain_grad]
    packed = jnp.concatenate([part.reshape(-1, 128) for part in own_parts + sum_parts])
    packed_rows = packed.shape[0]
    packed = jnp.pad(packed, ((0, -packed_rows % 8), (0, 0)))
    per_owner = seq_devices // group_devices
    gathered, owned, shared_all, small_all = spread_grads(
        in_weight_sum[:, : 2 * local_width].astype(bf16),
        pieces.reshape(group_devices, per_owner, local_width // group_devices, width),
        shared.reshape(seq_devices, in_rows // seq_devices, shared_columns),
        packed,
        4,
    )
    in_weight_grad = assemble_in(
        gathered.reshape(seq_devices, in_rows, 2 * local_width),
        shared_all.reshape(in_rows, shared_columns),
        in_weight.shape[1],
    )
    out_weight_grad = assemble_out(owned)

    tile_rows = local_width // 128
    own_rows = (KW + 2) * tile_rows
    own_all = small_all[:, :own_rows].reshape(seq_devices, KW + 2, local_width)
    own_all = jnp.swapaxes(own_all, 0, 1).reshape(KW + 2, inner_width)
    head_all = jnp.swapaxes(small_all[:, own_rows : own_rows + 3, :local_heads], 0, 1)
    head_all = head_all.reshape(3, head_count)
    summed = jnp.sum(small_all[:, own_rows + 3 : packed_rows], axis=0).reshape(-1)
    conv_weight_grad = jnp.concatenate(
        [own_all[:KW], summed[: KW * bc_width].reshape(KW, bc_width)], axis=1
    )
    conv_bias_grad = jnp.concatenate(
        [own_all[KW], summed[KW * bc_width : (KW + 1) * bc_width]]
    )
    norm_gain_total = summed[(KW + 1) * bc_width :]
    return (
        mixed_out,
        token_grad.reshape(tokens.shape),
        norm_gain_total,
        in_weight_grad,
        conv_weight_grad,
        conv_bias_grad,
        head_all[0],
        head_all[1],
        head_all[2],
        own_all[KW + 1],
        out_weight_grad,
    )


def solution(mesh):
    placed = (
        P("wa", "seq", None),
        P("wa"),
        P(),
        P("wa", None),
        P(),
        P(),
        P(),
        P(),
        P(),
        P(),
        P("wa", None),
        P("wa", "seq", None),
    )
    return jax.shard_map(
        body,
        mesh=mesh,
        in_specs=placed,
        out_specs=(
            P("wa", "seq", None),
            P("wa", "seq", None),
            P(),
            P("wa", None),
            P(),
            P(),
            P(),
            P(),
            P(),
            P(),
            P("wa", None),
        ),
        check_vma=False,
    )
```

time: 1300 us -> 644 us (0.50)
  waiting for transfers between devices: 420 us -> 2.26 us
  Pallas kernels: 283 us -> 480 us
  other arithmetic: 202 us -> 25.6 us
  local copies, waits for them, and re-layouts: 201 us -> 44.1 us
  matrix products: 126 us -> 69.6 us
  blocking collectives: 35.5 us -> 0 us
    reduce_scatter x3 -> x0, waiting for transfers between devices: 253 us -> none  [the longest x1 149 us: body(): lax.psum_scatter(jnp.dot(normed_out, out_rows, preferred_element_type=f32...]
    pallas_call x3 -> x9, Pallas kernels: 283 us -> 480 us  [the longest x2 167 us: ring_gather(): pl.pallas_call(functools.partial(gather_kernel, size), out_shape=jax.Shap...]
    psum x3 -> x0, waiting for transfers between devices: 121 us -> none  [the longest x1 121 us: body(): lax.psum(jnp.concatenate([norm_gain_grad, conv_weight_grad.reshape(-1), c...]
    convert_element_type x6 -> x1, local copies, waits for them, and re-layouts: 66.1 us -> 2.8 us  [body(): gated = gated_heads.reshape(-1, local_width).astype(f32)]
    dot_general x14 -> x1, matrix products: 71.4 us -> 11.9 us  [body(): jnp.dot(jnp.swapaxes(swapped, 0, 1).reshape(row_count, inner_width), out_...]
    another operation x9 -> x0, other arithmetic: 58 us -> none
    all_gather x1, waiting for transfers between devices: 45.4 us -> 0.02 us  [body(): out_full = lax.all_gather(out_weight, 'wa', axis=0, tiled=True)]
    reshape x12 -> x5, local copies, waits for them, and re-layouts: 44.2 us -> 0.66 us  [the longest x1 0.62 us: body(): sums = seq_total(jnp.stack([jnp.sum(gated * gated, axis=-1), jnp.sum(weig...]
  transfers between devices with their start and end apart: 10 -> 4, of which waited for: 5 -> 1; matrix products, arithmetic and copies ran while one was open for 25% -> 10% of each run, Pallas kernels for 22% -> 35%
where the time goes in v2:
time: 644 us; the launch traced here: 640 us
  Pallas kernels  480 us (75%)
  matrix products  69.6 us (11%)
  local copies, waits for them, and re-layouts  44.1 us (7%)
  other arithmetic  25.6 us (4%)
  between operations  14.3 us (2%)
    pallas_call x2, Pallas kernels, ring_gather(): pl.pallas_call(functools.partial(gather_kernel, size), out_shape=jax.Shap...  167 us
    pallas_call x1, Pallas kernels, reduce_rows(): pl.pallas_call(functools.partial(reduce_kernel, size, groups), out_shape=...  129 us
    pallas_call x1, Pallas kernels, spread_grads(): pl.pallas_call(functools.partial(spread_kernel, size, groups), out_shape=...  103 us
    pallas_call x1, Pallas kernels, scan_backward(): pl.pallas_call(functools.partial(backward_kernel, widths, head_size, chun...  41.8 us
    unnamed x45, local copies, waits for them, and re-layouts  31.3 us
    dot_general x1, matrix products, body(): lax.dot_general(normed_all, proj_grad, (((0,), (0,)), ((), ())), preferre...  19.2 us
    dot_general x1, matrix products, body(): jnp.dot(normed_all, in_columns, preferred_element_type=f32).astype(bf16)  18.4 us
    pallas_call x1, Pallas kernels, scan_forward(): pl.pallas_call(functools.partial(forward_kernel, widths, head_size), grid...  17.7 us
  transfers between devices with their start and end apart: 4, of which 1 were waited for; matrix products, arithmetic and copies ran while one was open for 10% of the time, Pallas kernels for 35%

profile of v2, /device:TPU:0, one launch (start us, length us, event | category | flops | bytes accessed | tf_op | source)
XLA Modules:
  0.0 640.4 jit_solution(15520245019203680663)
XLA Ops:
  14.8 84.6 %gather_rows.2 = bf16[8,2,2,64,2048]{4,3,2,1,0:T(8,128)(2,1)} custom-call(bf16[2,2,64,2048]{3,2,1,0:T(8,128)(2,1)} %multiply_convert_fusion.1.x_ref), custom_call_target="tpu_custom_call" | custom-call | tf_op jit(solution)/shard_map/gather_rows/pallas_call | solution.py:470
  100.0 2.3 broadcast_multiply_fusion.x_ref
  102.3 82.1 %gather_rows.3 = bf16[8,2,2,64,2048]{4,3,2,1,0:T(8,128)(2,1)} custom-call(bf16[2,2,64,2048]{3,2,1,0:T(8,128)(2,1)} %broadcast_multiply_fusion.x_ref), custom_call_target="tpu_custom_call" | custom-call | tf_op jit(solution)/shard_map/gather_rows/pallas_call | solution.py:470
  185.6 18.4 %convolution_convert_fusion = bf16[2048,1408]{1,0:T(8,128)(2,1)} fusion(bf16[2048,2048]{1,0:T(8,128)(2,1)} %bitcast.102, bf16[2048,1408]{1,0:T(8,128)(2,1)} %all-gather.3.cloned.1.call-done.weight_ref), kind=kOutput, calls=%fused_computation.1 | convolution fusion | flops 11814043648 | bytes 19922944 | tf_op jit(solution)/shard_map/dot_general | solution.py:876
  204.0 17.7 %scan_forward.1 = (bf16[8,2,128,512]{3,2,1,0:T(8,128)(2,1)S(1)}, bf16[8,2,128,512]{3,2,1,0:T(8,128)(2,1)S(1)}, bf16[8,2,512,128]{3,2,1,0:T(8,128)(2,1)}) custom-call(bf16[8,2,128,1408]{3,2,1,0:T(8,128)(2,1)} %bitcast.94, f32[8,768]{1,0:T(8,128)S(1)} %select_maximum_fusion.taps_ref, f32[1,768]{1,0:T(1,128)S(1)} %broadcast_in_dim.13.shift_ref, ...), custom_call_target="tpu_custom_call" | custom-call | tf_op jit(solution)/shard_map/scan_forward/pallas_call | solution.py:297
  223.0 2.8 copy.33
  226.3 10.8 %fusion.3 = (f32[2048]{0:T(1024)S(1)}, f32[2048,512]{1,0:T(8,128)}) fusion(bf16[8,2,128,512]{3,2,1,0:T(8,128)(2,1)S(1)} %get-tuple-element.25, f32[512]{0:T(512)S(1)} %dynamic_slice.43, bf16[2048,2048]{1,0:T(8,128)(2,1)} %bitcast.104, bf16[4096,2048]{1,0:T(8,128)(2,1)} %all-gather.5.cloned.1.call-done, s32[]{:T(128)S(6)} %select_n.48), kind=kOutput, calls=%fused_computation.11 | convolution fusion | flops 4299159552 | bytes 16787460 | tf_op jit(solution)/shard_map/dot_general | solution.py:906
  237.7 7.9 %seq_total.1 = f32[32,128]{1,0:T(8,128)} custom-call(f32[32,128]{1,0:T(8,128)} %reshape.336.x_ref), custom_call_target="tpu_custom_call" | custom-call | tf_op jit(solution)/shard_map/seq_total/pallas_call | solution.py:503
  247.6 9.3 %convolution_convert_fusion.2 = bf16[512,2048]{1,0:T(8,128)(2,1)} fusion(bf16[2048,512]{1,0:T(8,128)(2,1)S(1)} %bitcast.108, bf16[2048,2048]{1,0:T(8,128)(2,1)} %bitcast.105), kind=kOutput, calls=%fused_computation.18 | convolution fusion | flops 4296015872 | bytes 12582912 | tf_op jit(solution)/shard_map/dot_general | solution.py:926
  256.9 4.0 multiply_convert_fusion
  260.9 4.5 all-to-all-start
  265.5 4.3 fusion.8
  269.8 41.8 %scan_backward.1 = (bf16[8,2,128,1408]{3,2,1,0:T(8,128)(2,1)}, f32[8,768]{1,0:T(8,128)S(1)}, f32[8,512]{1,0:T(8,128)S(1)}, f32[8,128]{1,0:T(8,128)S(1)}) custom-call(bf16[8,2,128,1408]{3,2,1,0:T(8,128)(2,1)} %bitcast.95, bf16[8,2,128,1408]{3,2,1,0:T(8,128)(2,1)} %bitcast.96, bf16[8,2,128,512]{3,2,1,0:T(8,128)(2,1)S(1)} %copy-done.5, ...), custom_call_target="tpu_custom_call" | custom-call | tf_op jit(solution)/shard_map/scan_backward/pallas_call | solution.py:329
  311.9 19.2 %convolution_convert_fusion.1 = bf16[2048,1408]{1,0:T(8,128)(2,1)} fusion(bf16[2048,2048]{1,0:T(8,128)(2,1)} %bitcast.103, bf16[2048,1408]{1,0:T(8,128)(2,1)} %bitcast.106), kind=kOutput, calls=%fused_computation.2 | convolution fusion | flops 11814043648 | bytes 19922944 | tf_op jit(solution)/shard_map/dot_general | solution.py:956
  331.1 11.9 %fusion.10 = bf16[256,2048]{1,0:T(8,128)(2,1)} fusion(f32[256,2048]{1,0:T(8,128)S(1)} %bitcast.98, bf16[256,4096]{0,1:T(8,128)(2,1)} %bitcast.14, bf16[4096,2048]{1,0:T(8,128)(2,1)} %all-gather.5.cloned.1.call-done, f32[256]{0:T(256)S(1)} %fusion.29), kind=kOutput, calls=%fused_computation.22 | convolution fusion | flops 4296540160 | bytes 22021120 | tf_op jit(solution)/shard_map/dot_general | solution.py:962
  344.5 128.7 %reduce_rows.1 = (f32[2,128,2048]{2,1,0:T(8,128)}, bf16[8,2,1,64,2048]{4,3,2,1,0:T(8,128)(2,1)}, bf16[3,512,1408]{2,1,0:T(8,128)(2,1)}) custom-call(bf16[8,2,128,1408]{3,2,1,0:T(8,128)(2,1)} %get-tuple-element.28.grad_ref, bf16[2048,1408]{1,0:T(8,128)(2,1)} %all-gather.3.cloned.1.call-done.weight_ref, bf16[2,1,64,2048]{3,2,1,0:T(8,128)(2,1)} %bitcast.111, ...), custom_call_target="tpu_custom_call" | custom-call | tf_op jit(solution)/shard_map/reduce_rows/pallas_call | solution.py:630
  473.2 3.3 convert_reduce_fusion
  482.4 102.7 %spread_grads.1 = (bf16[8,2,2,128,1024]{4,3,2,1,0:T(8,128)(2,1)S(1)}, bf16[4,2,128,2048]{3,2,1,0:T(8,128)(2,1)S(1)}, bf16[8,64,384]{2,1,0:T(8,128)(2,1)S(1)}, f32[8,56,128]{2,1,0:T(8,128)S(1)}) custom-call(bf16[2,2,128,1024]{3,2,1,0:T(8,128)(2,1)S(1)} %bitcast.91, bf16[4,2,128,2048]{3,2,1,0:T(8,128)(2,1)S(1)} %bitcast.92, ...), custom_call_target="tpu_custom_call" | custom-call | tf_op jit(solution)/shard_map/spread_grads/pallas_call | solution.py:740
  585.1 3.4 copy-done
  591.8 3.4 copy-done.1
  595.2 7.1 %assemble_in.1 = f32[512,8512]{1,0:T(8,128)} custom-call(bf16[8,512,1024]{2,1,0:T(8,128)(2,1)S(1)} %bitcast.90, bf16[512,384]{1,0:T(8,128)(2,1)S(1)} %bitcast.93), custom_call_target="tpu_custom_call" | custom-call | tf_op jit(solution)/shard_map/assemble_in/pallas_call | solution.py:787
  602.3 17.9 %copy.34 = f32[512,8512]{0,1:T(8,128)} copy(f32[512,8512]{1,0:T(8,128)} %assemble_in.1) | data formatting | bytes 34865152
  620.2 7.4 %assemble_out.1 = f32[1024,2048]{1,0:T(8,128)} custom-call(bf16[4,2,128,2048]{3,2,1,0:T(8,128)(2,1)} %copy-done.2), custom_call_target="tpu_custom_call" | custom-call | tf_op jit(solution)/shard_map/assemble_out/pallas_call | solution.py:807
  630.7 3.2 fusion.14
  (134 shorter events, 27.6 us)
Async XLA Ops:
  7.2 2.7 slice-start
  7.2 178.4 %all-gather.3.cloned.1.call-start = ((), (), s32[]{:S(2)}) async-start(), calls=%async_computation.2 | async-start | bytes 7208960 | tf_op jit(solution)/shard_map/all_gather | solution.py:872
  10.0 2.8 copy-start.9
  12.1 214.2 %all-gather.5.cloned.1.call-start = ((), (), s32[]{:S(2)}) async-start(), calls=%async_computation.3 | async-start | bytes 20971520 | tf_op jit(solution)/shard_map/all_gather | solution.py:904
  13.1 86.3 %copy-start.7 = (f32[2,128,2048]{2,1,0:T(8,128)}, f32[2,128,2048]{2,1,0:T(8,128)S(1)}, u32[]{:S(2)}) copy-start(f32[2,128,2048]{2,1,0:T(8,128)S(1)} %convert_element_type.158) | copy-start | bytes 6291460
  14.8 84.7 %copy-start.15 = (f32[4352]{0:T(1024)S(1)}, f32[4352]{0:T(1024)}, u32[]{:S(2)}) copy-start(f32[4352]{0:T(1024)} %param.17) | copy-start | bytes 52228
  14.8 84.7 %slice-start.2 = ((f32[4352]{0:T(1024)}), f32[256]{0:T(256)S(1)}, s32[]{:S(2)}) async-start(f32[4352]{0:T(1024)} %param.17), calls=%async_computation.7 | async-start | bytes 2048 | tf_op jit(solution)/shard_map/slice | solution.py:891
  14.8 84.8 %copy-start.17 = (f32[64]{0:T(128)S(1)}, f32[64]{0:T(128)}, u32[]{:S(2)}) copy-start(f32[64]{0:T(128)} %param.19) | copy-start | bytes 772
  14.8 84.8 %copy-start.18 = (f32[64]{0:T(128)S(1)}, f32[64]{0:T(128)}, u32[]{:S(2)}) copy-start(f32[64]{0:T(128)} %param.18) | copy-start | bytes 772
  14.8 84.9 %copy-start.19 = (f32[64]{0:T(128)S(1)}, f32[64]{0:T(128)}, u32[]{:S(2)}) copy-start(f32[64]{0:T(128)} %param.20) | copy-start | bytes 772
  14.8 85.1 %copy-start.16 = (s32[2]{0:T(128)S(1)}, s32[2]{0:T(128)}, u32[]{:S(2)}) copy-start(s32[2]{0:T(128)} %param.13) | copy-start | bytes 28
  102.3 82.9 %copy-start.14 = (f32[4,4352]{1,0:T(4,128)S(1)}, f32[4,4352]{1,0:T(4,128)}, u32[]{:S(2)}) copy-start(f32[4,4352]{1,0:T(4,128)} %param.16) | copy-start | bytes 208900
  102.3 82.9 %slice-start.1 = ((f32[4,4352]{1,0:T(4,128)}), f32[4,256]{1,0:T(4,128)S(1)}, s32[]{:S(2)}) async-start(f32[4,4352]{1,0:T(4,128)} %param.16), calls=%async_computation.6 | async-start | bytes 8192 | tf_op jit(solution)/shard_map/slice | solution.py:886
  260.9 70.2 %all-to-all-start = ((bf16[8,256,512]{1,2,0:T(8,128)(2,1)}), bf16[8,256,512]{1,2,0:T(8,128)(2,1)}, u32[]{:S(2)}, u32[]{:S(2)}) async-start(bf16[8,256,512]{1,2,0:T(8,128)(2,1)} %multiply_convert_fusion), calls=%async_computation | async-start | bytes 4194304 | tf_op jit(solution)/shard_map/all_to_all | solution.py:922
  265.4 79.1 %reduce-scatter.2.cloned.1.call-start = ((), (), s32[]{:S(2)}) async-start(), calls=%async_computation.4 | async-start | bytes 2621440 | tf_op jit(solution)/shard_map/reduce_scatter | solution.py:925
  265.4 4.3 copy-start.5
  265.4 4.3 copy-start.6
  311.9 19.2 %copy-start.8 = (f32[2,128,2048]{2,1,0:T(8,128)S(1)}, f32[2,128,2048]{2,1,0:T(8,128)}, u32[]{:S(2)}) copy-start(f32[2,128,2048]{2,1,0:T(8,128)} %copy-done.7) | copy-start | bytes 6291460
  476.5 2.0 copy-start.10
  476.5 2.3 copy-start.11
  480.2 2.2 copy-start.3
  585.1 3.4 copy-start
  591.8 3.4 copy-start.1
  620.2 10.5 %copy-start.12 = (f32[2,128,2048]{2,1,0:T(8,128)S(1)}, f32[2,128,2048]{2,1,0:T(8,128)}, u32[]{:S(2)}) copy-start(f32[2,128,2048]{2,1,0:T(8,128)} %get-tuple-element.29) | copy-start | bytes 6291460
  (3 other events, 4.7 us)
Sparse Core Ops, SparseCore 0:
  12.2 46.0 all-gather.2
  59.9 105.9 all-gather.4
  311.7 32.7 reduce-scatter.1

commit v3 on v2

--- a/solution.py
+++ b/solution.py
@@ -55,9 +55,10 @@
     return lane, row >= col
 
 
-def forward_kernel(
+def forward_chunk(
     widths,
     head_size,
+    start,
     proj_ref,
     taps_ref,
     shift_ref,
@@ -78,7 +79,7 @@
     rows = proj_ref.shape[2]
     per_tile = 128 // head_size
 
-    @pl.when(pl.program_id(1) == 0)
+    @pl.when(start)
     def _():
         state[...] = jnp.zeros_like(state)
         halo[...] = jnp.zeros_like(halo)
@@ -120,7 +121,7 @@
             )
         y_tile = y[:, cols] + inner
         y_ref[0, 0, :, cols] = y_tile.astype(bf16)
-        gated_ref[0, 0, :, cols] = (y_tile * silu_gate[:, cols]).astype(bf16)
+        gated_ref[:, cols] = (y_tile * silu_gate[:, cols]).astype(bf16)
 
 
 def backward_kernel(
@@ -142,6 +143,7 @@
     tri_ref,
     upper_ref,
     out_ref,
+    turned_ref,
     taps_acc,
     skip_acc,
     head_acc,
@@ -276,6 +278,7 @@
         taps_acc[k : k + 1, :] += jnp.sum(conv_grad * ext[5 + k : 5 + k + rows, :], axis=0, keepdims=True)
     taps_acc[KW : KW + 1, :] += jnp.sum(conv_grad, axis=0, keepdims=True)
     out_ref[0, 0, :, lw : 2 * lw + bc] = total.astype(bf16)
+    turned_ref[...] = out_ref[0, 0].T
 
 
 def whole_spec(array):
@@ -287,31 +290,6 @@
     spread = (jnp.arange(128)[:, None] == head_of[None, :]).astype(jnp.bfloat16)
     tri = (jnp.arange(rows)[:, None] >= jnp.arange(rows)[None, :]).astype(jnp.float32)
     return spread, spread.T, tri, tri.T
-
-
-def scan_forward(proj, taps, shift, bias, slope, skip, spread, tri, widths, head_size):
-    chunks, seqs, rows, _ = proj.shape
-    lw, bc = widths
-    block = lambda *tail: pl.BlockSpec((1, 1) + tail, lambda q, c: (c, q, 0, 0))
-    tables = (taps, shift, bias, slope, skip, spread, tri)
-    return pl.pallas_call(
-        functools.partial(forward_kernel, widths, head_size),
-        grid=(seqs, chunks),
-        in_specs=[block(rows, proj.shape[3])] + [whole_spec(t) for t in tables],
-        out_specs=[block(rows, lw), block(rows, lw), block(lw, bc // 2)],
-        out_shape=[
-            jax.ShapeDtypeStruct((chunks, seqs, rows, lw), jnp.bfloat16),
-            jax.ShapeDtypeStruct((chunks, seqs, rows, lw), jnp.bfloat16),
-            jax.ShapeDtypeStruct((chunks, seqs, lw, bc // 2), jnp.bfloat16),
-        ],
-        scratch_shapes=[
-            pltpu.VMEM((lw, bc // 2), jnp.float32),
-            pltpu.VMEM((rows + 8, lw + bc), jnp.float32),
-            pltpu.VMEM((8, lw + bc), jnp.float32),
-        ],
-        compiler_params=pltpu.CompilerParams(vmem_limit_bytes=48 * 2**20),
-        name="scan_forward",
-    )(proj, *tables)
 
 
 def scan_backward(
@@ -331,8 +309,15 @@
         grid=(seqs, chunks),
         in_specs=[block(rows, cols), before, block(rows, lw), block(lw, bc // 2), block(rows, lw)]
         + [whole_spec(t) for t in tables],
-        out_specs=[block(rows, cols)] + [pl.BlockSpec(s, lambda q, c: (0, 0)) for s in sums],
-        out_shape=[jax.ShapeDtypeStruct(proj.shape, jnp.bfloat16)]
+        out_specs=[
+            block(rows, cols),
+            pl.BlockSpec((cols, rows), lambda q, c: (0, (chunks - 1 - c) * seqs + q)),
+        ]
+        + [pl.BlockSpec(s, lambda q, c: (0, 0)) for s in sums],
+        out_shape=[
+            jax.ShapeDtypeStruct(proj.shape, jnp.bfloat16),
+            jax.ShapeDtypeStruct((cols, chunks * seqs * rows), jnp.bfloat16),
+        ]
         + [jax.ShapeDtypeStruct(s, jnp.float32) for s in sums],
         scratch_shapes=[
             pltpu.VMEM((lw, bc // 2), jnp.float32),
@@ -414,9 +399,11 @@
             peer,
         )
 
+    def kept(self):
+        return pltpu.make_async_copy(self.x, self.o.at[self.me], self.local)
+
     def start(self):
-        self.kept = pltpu.make_async_copy(self.x, self.o.at[self.me], self.local)
-        self.kept.start()
+        self.kept().start()
         for chunk in range(self.chunks):
             for way in range(2):
                 self.copy(0, chunk, way, True).start()
@@ -440,7 +427,7 @@
             return carry
 
         lax.fori_loop(0, self.size - 1, drain, 0)
-        self.kept.wait()
+        self.kept().wait()
 
 
 def ring_parts(x, chunks):
@@ -455,64 +442,438 @@
     ]
 
 
-def gather_kernel(size, x_ref, o_ref, send_sem, recv_sem, local_sem):
-    _, _, _, right, left = neighbours(size)
-    greet([right, left])
-    ring = RingGather(size, x_ref, o_ref, send_sem, recv_sem, local_sem)
+def project_kernel(
+    size,
+    groups,
+    x_ref,
+    w_ref,
+    rows_ref,
+    weights_ref,
+    proj_ref,
+    taken,
+    weights,
+    made,
+    send_sem,
+    recv_sem,
+    local_sem,
+    weight_send,
+    weight_recv,
+    weight_local,
+    take_sem,
+    made_sem,
+):
+    me, group, pos, right, left = neighbours(size)
+    mates = [(me, index) for index in others(group, groups)]
+    greet([right, left] + mates)
+    ring = RingGather(size, x_ref, rows_ref, send_sem, recv_sem, local_sem)
     ring.start()
-    lax.fori_loop(1, size - 1, lambda step, carry: (ring.advance(step), carry)[1], 0)
+    sent = [
+        push(w_ref, weights.at[group], weight_send.at[k], weight_recv.at[k], mate)
+        for k, mate in enumerate(mates)
+    ]
+    for copy in sent:
+        copy.start()
+    kept = pltpu.make_async_copy(w_ref, weights.at[group], weight_local.at[0])
+    kept.start()
+    depth = weights.shape[2]
+
+    def block_of(pair, way):
+        return ring_index((pos - pair + size) % size if way == 0 else (pos + pair) % size, size)
+
+    def take(pair, slot, way, own=False):
+        source = x_ref.at[way] if own else rows_ref.at[block_of(pair, way), way]
+        return pltpu.make_async_copy(source, taken.at[slot, way], take_sem.at[slot, way])
+
+    def put(pair, slot, way):
+        return pltpu.make_async_copy(
+            made.at[slot, way], proj_ref.at[block_of(pair, way), way], made_sem.at[slot, way]
+        )
+
+    def compute(pair, slot):
+        for way in range(2):
+            x = taken[slot, way].reshape(made.shape[2], taken.shape[4])
+            total = None
+            for part in range(groups):
+                term = lax.dot_general(
+                    x[:, part * depth : (part + 1) * depth],
+                    weights[part],
+                    (((1,), (1,)), ((), ())),
+                    preferred_element_type=jnp.float32,
+                )
+                total = term if total is None else total + term
+            made[slot, way] = total.astype(jnp.bfloat16)
+            put(pair, slot, way).start()
+
+    def advance(step, carry):
+        ring.advance(step)
+        return carry
+
+    middle = size // 2 + 1
+    lax.fori_loop(1, middle, advance, 0)
+    for way in range(2):
+        take(0, 0, way, True).start()
+    kept.wait()
+    for copy in sent:
+        copy.wait_recv()
+    flushed = pltpu.make_async_copy(weights, weights_ref, weight_local.at[1])
+    flushed.start()
+    for way in range(2):
+        take(0, 0, way, True).wait()
+    compute(0, 0)
+
+    def pairs(low, high):
+        for way in range(2):
+            take(low, lax.rem(low, 2), way).start()
+
+        def one(pair, carry):
+            slot = lax.rem(pair, 2)
+            for way in range(2):
+                take(pair, slot, way).wait()
+
+            @pl.when(pair + 1 < high)
+            def _():
+                for way in range(2):
+                    take(pair + 1, 1 - slot, way).start()
+
+            @pl.when(pair >= 2)
+            def _():
+                for way in range(2):
+                    put(pair - 2, slot, way).wait()
+
+            compute(pair, slot)
+            return carry
+
+        lax.fori_loop(low, high, one, 0)
+
+    count = size - 1 - middle
+
+    def late(step, carry):
+        ring.advance(step)
+        turn = step - middle
+        pairs(1 + (turn * (size - 2)) // count, 1 + ((turn + 1) * (size - 2)) // count)
+        return carry
+
+    lax.fori_loop(middle, size - 1, late, 0)
     ring.finish()
-
-
-def ring_gather(x, collective_id):
-    size = lax.axis_size("seq")
+    pairs(size - 1, size)
+    for pair in (size - 2, size - 1):
+        for way in range(2):
+            put(pair, pair % 2, way).wait()
+    for copy in sent:
+        copy.wait_send()
+    flushed.wait()
+
+
+def project(x, weight, collective_id):
+    size, groups = lax.axis_size("seq"), lax.axis_size("wa")
     parts = ring_parts(x, 2)
-    out = pl.pallas_call(
-        functools.partial(gather_kernel, size),
-        out_shape=jax.ShapeDtypeStruct((size,) + parts.shape, x.dtype),
-        in_specs=[ANY],
-        out_specs=ANY,
-        scratch_shapes=ring_sems(size, 2),
-        compiler_params=comm_params(collective_id),
-        name="gather_rows",
-    )(parts)
-    return out.reshape(size * x.shape[0], x.shape[1])
-
-
-def total_kernel(size, x_ref, o_ref, landing, send_sem, recv_sem):
-    me, group = lax.axis_index("seq"), lax.axis_index("wa")
-    peers = [(index, group) for index in others(me, size)]
-    greet(peers)
-    copies = [
-        push(x_ref, landing.at[k], send_sem.at[k], recv_sem.at[k], peer)
-        for k, peer in enumerate(peers)
-    ]
-    for copy in copies:
-        copy.start()
-    total = x_ref[...]
-    for k, copy in enumerate(copies):
-        copy.wait_recv()
-        total = total + landing[k]
-    o_ref[...] = total
-    for copy in copies:
-        copy.wait_send()
-
-
-def seq_total(x, collective_id):
-    size = lax.axis_size("seq")
+    cols, depth = weight.shape
+    rows = x.shape[0] // 2
+    bf16, DMA = jnp.bfloat16, pltpu.SemaphoreType.DMA
     return pl.pallas_call(
-        functools.partial(total_kernel, size),
-        out_shape=jax.ShapeDtypeStruct(x.shape, x.dtype),
-        in_specs=[VMEM],
-        out_specs=VMEM,
+        functools.partial(project_kernel, size, groups),
+        out_shape=[
+            jax.ShapeDtypeStruct((size,) + parts.shape, bf16),
+            jax.ShapeDtypeStruct((groups, cols, depth), bf16),
+            jax.ShapeDtypeStruct((size, 2, rows, cols), bf16),
+        ],
+        in_specs=[ANY, ANY],
+        out_specs=[ANY, ANY, ANY],
         scratch_shapes=[
-            pltpu.VMEM((size - 1,) + x.shape, x.dtype),
-            pltpu.SemaphoreType.DMA((size - 1,)),
-            pltpu.SemaphoreType.DMA((size - 1,)),
+            pltpu.VMEM((2,) + parts.shape, bf16),
+            pltpu.VMEM((groups, cols, depth), bf16),
+            pltpu.VMEM((2, 2, rows, cols), bf16),
+        ]
+        + ring_sems(size, 2)
+        + [DMA((groups - 1,)), DMA((groups - 1,)), DMA((2,)), DMA((2, 2)), DMA((2, 2))],
+        compiler_params=comm_params(collective_id, 60),
+        name="project",
+    )(parts, weight)
+
+
+def middle_kernel(
+    widths,
+    head_size,
+    size,
+    groups,
+    inner,
+    proj_ref,
+    taps_ref,
+    shift_ref,
+    bias_ref,
+    slope_ref,
+    skip_ref,
+    spread_ref,
+    tri_ref,
+    gain_ref,
+    cot_ref,
+    shard_ref,
+    y_ref,
+    enter_ref,
+    normed_ref,
+    grad_ref,
+    gain_acc,
+    branch_ref,
+    part_ref,
+    state,
+    ext,
+    halo,
+    gated,
+    out_grad,
+    sums,
+    landing,
+    taken,
+    weights,
+    turned,
+    send_sem,
+    recv_sem,
+    local_sem,
+    pair_send,
+    pair_recv,
+    shard_send,
+    shard_recv,
+    shard_local,
+    take_sem,
+):
+    bf16, f32 = jnp.bfloat16, jnp.float32
+    index = pl.program_id(0)
+    seq, chunk = index // size, lax.rem(index, size)
+    me, group, pos, right, left = neighbours(size)
+    rows, lw = gated.shape[2:]
+    peers = [(other, group) for other in others(me, size)]
+    sibling = (me, group + 1 - 2 * lax.rem(group, 2))
+    across = (me, lax.rem(group + 2, groups))
+    ring = RingGather(size, cot_ref, branch_ref, send_sem, recv_sem, local_sem)
+    chosen = lax.rem(me, size // groups)
+    owner = me // (size // groups)
+
+    def shard(step, source, slot, peer):
+        return push(
+            source, part_ref.at[slot], shard_send.at[step], shard_recv.at[step], peer
+        )
+
+    def shards(step):
+        if step == 2:
+            return shard(2, part_ref.at[across[1]], across[1], sibling)
+        return shard(step, shard_ref.at[chosen], group, across if step == 0 else sibling)
+
+    @pl.when(index == 0)
+    def _():
+        greet([right, left, across, sibling] + [p for p in peers])
+        ring.start()
+        shards(0).start()
+        shards(1).start()
+
+    forward_chunk(
+        widths,
+        head_size,
+        chunk == 0,
+        proj_ref,
+        taps_ref,
+        shift_ref,
+        bias_ref,
+        slope_ref,
+        skip_ref,
+        spread_ref,
+        tri_ref,
+        gated.at[chunk, seq],
+        y_ref,
+        enter_ref,
+        state,
+        ext,
+        halo,
+    )
+
+    @pl.when(index == size + 2)
+    def _():
+        ring.advance(1)
+
+    def block_of(pair, way):
+        return ring_index((pos - pair + size) % size if way == 0 else (pos + pair) % size, size)
+
+    def take(pair, slot, way, own=False):
+        source = cot_ref.at[way] if own else branch_ref.at[block_of(pair, way), way]
+        return pltpu.make_async_copy(source, taken.at[slot, way], take_sem.at[slot, way])
+
+    ones = jnp.ones((8, lw), bf16)
+
+    def compute(pair, slot):
+        for way in range(2):
+            block = block_of(pair, way)
+            values = dot(taken[slot, way].reshape(rows, taken.shape[4]), turned[...], 1, 0)
+            out_grad[block, way] = values
+            here = gated[block, way].astype(f32)
+            weighted = values * gain_ref[0:1, :] * here
+            at = pl.ds(block * 2 + way, 1)
+            sums[0, at, :] = dot(ones, (here * here).astype(bf16), 1, 1)[0:1, :]
+            sums[1, at, :] = dot(ones, weighted.astype(bf16), 1, 1)[0:1, :]
+
+    def pairs(low, high):
+        for way in range(2):
+            take(low, lax.rem(low, 2), way).start()
+
+        def one(pair, carry):
+            slot = lax.rem(pair, 2)
+            for way in range(2):
+                take(pair, slot, way).wait()
+
+            @pl.when(pair + 1 < high)
+            def _():
+                for way in range(2):
+                    take(pair + 1, 1 - slot, way).start()
+
+            compute(pair, slot)
+            return carry
+
+        lax.fori_loop(low, high, one, 0)
+
+    @pl.when(index == 2 * size - 1)
+    def _():
+        def advance(step, carry):
+            ring.advance(step)
+            return carry
+
+        middle = size // 2 + 1
+        lax.fori_loop(2, middle, advance, 0)
+        for way in range(2):
+            take(0, 0, way, True).start()
+        first, second, third = (shards(step) for step in range(3))
+        first.wait_recv()
+        third.start()
+        second.wait_recv()
+        ring.advance(middle)
+        third.wait_recv()
+
+        @pl.when(owner == group)
+        def _():
+            loaded = pltpu.make_async_copy(shard_ref.at[chosen], weights, shard_local.at[0])
+            loaded.start()
+            loaded.wait()
+
+        @pl.when(owner != group)
+        def _():
+            loaded = pltpu.make_async_copy(part_ref.at[owner], weights, shard_local.at[1])
+            loaded.start()
+            loaded.wait()
+
+        turned[...] = weights[...].T
+        for way in range(2):
+            take(0, 0, way, True).wait()
+        compute(0, 0)
+        count = size - 1 - middle
+
+        def batch(turn):
+            pairs(1 + (turn * (size - 2)) // count, 1 + ((turn + 1) * (size - 2)) // count)
+
+        batch(0)
+
+        def late(step, carry):
+            ring.advance(step)
+            batch(step - middle)
+            return carry
+
+        lax.fori_loop(middle + 1, size - 1, late, 0)
+        ring.finish()
+        pairs(size - 1, size)
+        copies = [
+            push(sums, landing.at[k], pair_send.at[k], pair_recv.at[k], peer)
+            for k, peer in enumerate(peers)
+        ]
+        for copy in copies:
+            copy.start()
+        total = sums[...]
+        for k, copy in enumerate(copies):
+            copy.wait_recv()
+            total = total + landing[k]
+        scale = lax.rsqrt(total[0] / inner + EPS)
+        pull = scale * scale * scale * (total[1] / inner)
+        fill = jnp.zeros((128 - 2 * size, rows), f32)
+        scale_turned = jnp.concatenate([scale, fill]).T
+        pull_turned = jnp.concatenate([pull, fill]).T
+        lane = lax.broadcasted_iota(jnp.int32, (rows, 128), 1)
+        gain_acc[...] = jnp.zeros_like(gain_acc)
+
+        def finish(block, carry):
+            for way in range(2):
+                mask = lane == block * 2 + way
+                by = jnp.sum(jnp.where(mask, scale_turned, 0.0), axis=1, keepdims=True)
+                less = jnp.sum(jnp.where(mask, pull_turned, 0.0), axis=1, keepdims=True)
+                here = gated[block, way].astype(f32)
+                values = out_grad[block, way]
+                scaled = here * by
+                normed_ref[block, way] = (scaled * gain_ref[0:1, :]).astype(bf16)
+                grad_ref[block, way] = (values * gain_ref[0:1, :] * by - here * less).astype(bf16)
+                gain_acc[0:1, :] += jnp.sum(values * scaled, axis=0, keepdims=True)
+            return carry
+
+        lax.fori_loop(0, size, finish, 0)
+        for copy in copies:
+            copy.wait_send()
+        for copy in (first, second, third):
+            copy.wait_send()
+
+
+def middle(proj, tables, gain, cot, shard, inner, widths, head_size, collective_id):
+    size, groups = lax.axis_size("seq"), lax.axis_size("wa")
+    chunks, seqs, rows, cols = proj.shape
+    lw, bc = widths
+    parts = ring_parts(cot, 2)
+    bf16, f32, DMA = jnp.bfloat16, jnp.float32, pltpu.SemaphoreType.DMA
+    width = shard.shape[2]
+
+    def block(*tail):
+        return pl.BlockSpec((1, 1) + tail, lambda i: (lax.rem(i, chunks), i // chunks, 0, 0))
+
+    def fixed(shape):
+        return pl.BlockSpec(shape, lambda i: (0,) * len(shape))
+
+    whole = (chunks, seqs, rows, lw)
+    return pl.pallas_call(
+        functools.partial(middle_kernel, widths, head_size, size, groups, inner),
+        grid=(seqs * chunks,),
+        in_specs=[block(rows, cols)] + [fixed(t.shape) for t in tables + (gain,)] + [ANY, ANY],
+        out_specs=[
+            block(rows, lw),
+            block(lw, bc // 2),
+            fixed(whole),
+            fixed(whole),
+            fixed((8, lw)),
+            ANY,
+            ANY,
         ],
-        compiler_params=comm_params(collective_id),
-        name="seq_total",
-    )(x)
+        out_shape=[
+            jax.ShapeDtypeStruct(whole, bf16),
+            jax.ShapeDtypeStruct((chunks, seqs, lw, bc // 2), bf16),
+            jax.ShapeDtypeStruct(whole, bf16),
+            jax.ShapeDtypeStruct(whole, bf16),
+            jax.ShapeDtypeStruct((8, lw), f32),
+            jax.ShapeDtypeStruct((size,) + parts.shape, bf16),
+            jax.ShapeDtypeStruct((groups, lw, width), bf16),
+        ],
+        scratch_shapes=[
+            pltpu.VMEM((lw, bc // 2), f32),
+            pltpu.VMEM((rows + 8, lw + bc), f32),
+            pltpu.VMEM((8, lw + bc), f32),
+            pltpu.VMEM(whole, bf16),
+            pltpu.VMEM(whole, f32),
+            pltpu.VMEM((2, 2 * chunks, rows), f32),
+            pltpu.VMEM((size - 1, 2, 2 * chunks, rows), f32),
+            pltpu.VMEM((2,) + parts.shape, bf16),
+            pltpu.VMEM((lw, width), bf16),
+            pltpu.VMEM((width, lw), bf16),
+        ]
+        + ring_sems(size, 2)
+        + [
+            DMA((size - 1,)),
+            DMA((size - 1,)),
+            DMA((3,)),
+            DMA((3,)),
+            DMA((2,)),
+            DMA((2, 2)),
+        ],
+        compiler_params=comm_params(collective_id, 60),
+        name="middle",
+    )(proj, *tables, gain, parts, shard)
 
 
 def reduce_kernel(
@@ -521,12 +882,20 @@
     grad_ref,
     weight_ref,
     piece_ref,
-    part_ref,
+    normed_ref,
+    turned_ref,
     rows_ref,
     pieces_ref,
-    landing_ref,
+    main_ref,
+    shared_ref,
+    own_ref,
     slots,
     first,
+    landing,
+    parts,
+    total,
+    taken,
+    turned,
     send_sem,
     recv_sem,
     piece_send,
@@ -534,28 +903,19 @@
     piece_local,
     part_send,
     part_recv,
+    take_sem,
 ):
     me, group, pos, right, left = neighbours(size)
     mates = [(me, index) for index in others(group, groups)]
     greet([right, left] + mates)
-    tiles, tile = slots.shape[2], slots.shape[4]
-    parts = [
-        push(part_ref.at[mate[1]], landing_ref.at[k], part_send.at[k], part_recv.at[k], mate)
-        for k, mate in enumerate(mates)
-    ]
-    for copy in parts:
-        copy.start()
+    tiles, rows, tile = slots.shape[2:]
+    cols = total.shape[0]
+    bf16, f32 = jnp.bfloat16, jnp.float32
     ring = RingGather(size, piece_ref, pieces_ref, piece_send, piece_recv, piece_local)
     ring.start()
 
     def term(block, way, at):
-        columns = pl.ds(pl.multiple_of(at * tile, tile), tile)
-        return lax.dot_general(
-            grad_ref[block, way],
-            weight_ref[columns, :],
-            (((1,), (1,)), ((), ())),
-            preferred_element_type=jnp.float32,
-        )
+        return dot(grad_ref[block, way], weight_ref[at], 1, 0)
 
     def target(step, way):
         shift = (pos - 1 - step + 2 * size) if way == 0 else (pos + 1 + step)
@@ -572,35 +932,103 @@
 
     def begin(at, carry):
         for way in range(2):
-            first[way, at] = term(target(0, way), way, at).astype(jnp.bfloat16)
+            first[way, at] = term(target(0, way), way, at).astype(bf16)
             hop(0, way, at, first.at[way, at]).start()
         return carry
 
     lax.fori_loop(0, tiles, begin, 0)
+
+    def send_part(offset):
+        mate = (group + offset) % groups
+        return push(
+            parts.at[offset - 1],
+            landing.at[offset - 1],
+            part_send.at[offset - 1],
+            part_recv.at[offset - 1],
+            (me, mate),
+        )
+
+    def weight_part(offset):
+        mate = (group + offset) % groups
+        columns = pl.ds(pl.multiple_of(mate * tile, tile), tile)
+
+        def take(block, slot):
+            tokens = pl.ds(pl.multiple_of(block * 2 * rows, 2 * rows), 2 * rows)
+            return [
+                pltpu.make_async_copy(
+                    normed_ref.at[block, :, :, columns], taken.at[slot], take_sem.at[slot, 0]
+                ),
+                pltpu.make_async_copy(
+                    turned_ref.at[:, tokens], turned.at[slot], take_sem.at[slot, 1]
+                ),
+            ]
+
+        for copy in take(0, 0):
+            copy.start()
+
+        def one(block, carry):
+            slot = lax.rem(block, 2)
+
+            @pl.when(block + 1 < size)
+            def _():
+                for copy in take(block + 1, 1 - slot):
+                    copy.start()
+
+            for copy in take(block, slot):
+                copy.wait()
+            values = dot(turned[slot], taken[slot].reshape(2 * rows, tile), 1, 0)
+
+            @pl.when(block == 0)
+            def _():
+                total[...] = values
+
+            @pl.when(block > 0)
+            def _():
+                total[...] += values
+
+            return carry
+
+        lax.fori_loop(0, size, one, 0)
 
     def advance(step, carry):
         def one(at, inner):
             for way in range(2):
                 own = term(target(step, way), way, at)
                 hop(step - 1, way, at, first.at[way, at]).wait_recv()
-                slots[step - 1, way, at] = (
-                    slots[step - 1, way, at].astype(jnp.float32) + own
-                ).astype(jnp.bfloat16)
+                slots[step - 1, way, at] = (slots[step - 1, way, at].astype(f32) + own).astype(bf16)
                 hop(step, way, at, slots.at[step - 1, way, at]).start()
             return inner
 
         lax.fori_loop(0, tiles, one, 0)
         ring.advance(step)
+
+        @pl.when(step <= groups)
+        def _():
+            weight_part(step)
+
+        @pl.when(step < groups)
+        def _():
+            parts[step - 1] = total[...].astype(bf16)
+            send_part(step).start()
+
         return carry
 
     lax.fori_loop(1, size - 1, advance, 0)
+    for offset in range(1, groups):
+        send_part(offset).wait_recv()
+        total[...] += landing[offset - 1].astype(f32)
+    at = 0
+    for out_ref in (main_ref, shared_ref, own_ref):
+        count = out_ref.shape[0]
+        out_ref[...] = total[at : at + count].astype(bf16)
+        at += count
 
     def end(at, carry):
         columns = pl.ds(pl.multiple_of(at * tile, tile), tile)
         for way in range(2):
             own = term(me, way, at)
             hop(size - 2, way, at, first.at[way, at]).wait_recv()
-            rows_ref[way, :, columns] = slots[size - 2, way, at].astype(jnp.float32) + own
+            rows_ref[way, :, columns] = slots[size - 2, way, at].astype(f32) + own
         return carry
 
     lax.fori_loop(0, tiles, end, 0)
@@ -615,38 +1043,42 @@
 
     lax.fori_loop(0, size - 1, drain, 0)
     ring.finish()
-    for copy in parts:
-        copy.wait()
-
-
-def reduce_rows(grad, weight, piece, part, collective_id):
+    for offset in range(1, groups):
+        send_part(offset).wait_send()
+
+
+def reduce_rows(grad, weight, piece, normed, turned, counts, collective_id):
     size, groups = lax.axis_size("seq"), lax.axis_size("wa")
-    _, ways, rows, _ = grad.shape
-    width = weight.shape[0]
-    tile = 512
-    tiles = width // tile
+    _, ways, rows, cols = grad.shape
+    tile = weight.shape[2]
+    tiles = groups
     pieces = ring_parts(piece, 1)
-    bf16 = jnp.bfloat16
+    bf16, f32, DMA = jnp.bfloat16, jnp.float32, pltpu.SemaphoreType.DMA
     return pl.pallas_call(
         functools.partial(reduce_kernel, size, groups),
         out_shape=[
-            jax.ShapeDtypeStruct((ways, rows, width), jnp.float32),
+            jax.ShapeDtypeStruct((ways, rows, tiles * tile), f32),
             jax.ShapeDtypeStruct((size,) + pieces.shape, bf16),
-            jax.ShapeDtypeStruct((groups - 1,) + part.shape[1:], bf16),
-        ],
-        in_specs=[VMEM, VMEM, ANY, ANY],
-        out_specs=[VMEM, ANY, ANY],
+        ]
+        + [jax.ShapeDtypeStruct((count, tile), bf16) for count in counts],
+        in_specs=[VMEM, VMEM, ANY, ANY, ANY],
+        out_specs=[VMEM, ANY] + [VMEM] * len(counts),
         scratch_shapes=[
             pltpu.VMEM((size - 1, 2, tiles, rows, tile), bf16),
             pltpu.VMEM((2, tiles, rows, tile), bf16),
-            pltpu.SemaphoreType.DMA((size - 1, 2, tiles)),
-            pltpu.SemaphoreType.DMA((size - 1, 2, tiles)),
+            pltpu.VMEM((groups - 1, cols, tile), bf16),
+            pltpu.VMEM((groups - 1, cols, tile), bf16),
+            pltpu.VMEM((cols, tile), f32),
+            pltpu.VMEM((2, ways, rows, tile), bf16),
+            pltpu.VMEM((2, cols, 2 * rows), bf16),
+            DMA((size - 1, 2, tiles)),
+            DMA((size - 1, 2, tiles)),
         ]
         + ring_sems(size, 1)
-        + [pltpu.SemaphoreType.DMA((groups - 1,)), pltpu.SemaphoreType.DMA((groups - 1,))],
-        compiler_params=comm_params(collective_id, 60),
+        + [DMA((groups - 1,)), DMA((groups - 1,)), DMA((2, 2))],
+        compiler_params=comm_params(collective_id, 62),
         name="reduce_rows",
-    )(grad, weight, pieces, part)
+    )(grad, weight, pieces, normed, turned)
 
 
 def spread_kernel(
@@ -655,15 +1087,20 @@
     main_ref,
     pieces_ref,
     shared_ref,
+    own_ref,
     small_ref,
+    tokens_ref,
+    weight_ref,
     gathered_ref,
     owned_ref,
     shared_out,
     small_out,
+    branch_ref,
     shared_land,
     shared_sum,
     small_land,
     small_sum,
+    taken,
     main_send,
     main_recv,
     main_local,
@@ -674,13 +1111,14 @@
     pair_recv,
     mate_send,
     mate_recv,
+    take_sem,
 ):
     me, group, pos, right, left = neighbours(size)
     mates = [(me, index) for index in others(group, groups)]
     peers = [(index, group) for index in others(me, size)]
     greet(mates + peers)
+    f32, bf16 = jnp.float32, jnp.bfloat16
     ring = RingGather(size, main_ref, gathered_ref, main_send, main_recv, main_local)
-    ring.start()
     owned = [
         push(pieces_ref.at[mate[1]], owned_ref.at[group], piece_send.at[k], piece_recv.at[k], mate)
         for k, mate in enumerate(mates)
@@ -698,21 +1136,50 @@
     ]
     for copy in small_in + shared_in:
         copy.start()
+    ring.start()
     kept.start()
     for copy in owned:
         copy.start()
+
+    def take(block, slot):
+        return pltpu.make_async_copy(weight_ref.at[block], taken.at[slot], take_sem.at[slot])
+
+    take(0, 0).start()
+    branch_ref[...] = jnp.zeros_like(branch_ref)
+
+    def multiply(block, carry):
+        slot = lax.rem(block, 2)
+
+        @pl.when(block + 1 < size)
+        def _():
+            take(block + 1, 1 - slot).start()
+
+        take(block, slot).wait()
+        branch_ref[...] += dot(tokens_ref[block], taken[slot], 1, 0)
+        return carry
+
+    count = size - 2
+
+    def advance(step, carry):
+        ring.advance(step)
+        lax.fori_loop(((step - 1) * size) // count, (step * size) // count, multiply, 0)
+        return carry
+
+    lax.fori_loop(1, 2, advance, 0)
     total = small_ref[...]
     for k, copy in enumerate(small_in):
         copy.wait_recv()
         total = total + small_land[k]
     small_sum[...] = total
     small_out[pl.ds(me, 1)] = total[None]
-    total = shared_ref[me].astype(jnp.float32)
+    total = shared_ref[me].astype(f32)
     for k, copy in enumerate(shared_in):
         copy.wait_recv()
-        total = total + shared_land[k].astype(jnp.float32)
-    shared_sum[...] = total.astype(jnp.bfloat16)
-    shared_out[pl.ds(me, 1)] = total.astype(jnp.bfloat16)[None]
+        total = total + shared_land[k].astype(f32)
+    shared_rows = total.shape[0]
+    shared_sum[:shared_rows] = total.astype(bf16)
+    shared_sum[shared_rows:] = own_ref[...]
+    shared_out[pl.ds(me, 1)] = shared_sum[...][None]
     second = []
     for k, peer in enumerate(peers):
         second.append(
@@ -723,7 +1190,7 @@
         )
     for copy in second:
         copy.start()
-    lax.fori_loop(1, size - 1, lambda step, carry: (ring.advance(step), carry)[1], 0)
+    lax.fori_loop(2, size - 1, advance, 0)
     ring.finish()
     for copy in small_in + shared_in:
         copy.wait_send()
@@ -732,26 +1199,29 @@
     kept.wait()
 
 
-def spread_grads(main, pieces, shared, small, collective_id):
+def spread_grads(main, pieces, shared, own, small, tokens, weight, collective_id):
     size, groups = lax.axis_size("seq"), lax.axis_size("wa")
     parts = ring_parts(main, 2)
     bf16, f32 = jnp.bfloat16, jnp.float32
     DMA = pltpu.SemaphoreType.DMA
+    both = (shared.shape[1] + own.shape[0], shared.shape[2])
     return pl.pallas_call(
         functools.partial(spread_kernel, size, groups),
         out_shape=[
             jax.ShapeDtypeStruct((size,) + parts.shape, bf16),
             jax.ShapeDtypeStruct(pieces.shape, bf16),
-            jax.ShapeDtypeStruct(shared.shape, bf16),
+            jax.ShapeDtypeStruct((size,) + both, bf16),
             jax.ShapeDtypeStruct((size,) + small.shape, f32),
+            jax.ShapeDtypeStruct((tokens.shape[1], weight.shape[2]), f32),
         ],
-        in_specs=[ANY, ANY, VMEM, VMEM],
-        out_specs=[ANY, ANY, VMEM, VMEM],
+        in_specs=[ANY, ANY, VMEM, VMEM, VMEM, VMEM, ANY],
+        out_specs=[ANY, ANY, VMEM, VMEM, VMEM],
         scratch_shapes=[
             pltpu.VMEM((size - 1,) + shared.shape[1:], bf16),
-            pltpu.VMEM(shared.shape[1:], bf16),
+            pltpu.VMEM(both, bf16),
             pltpu.VMEM((groups - 1,) + small.shape, f32),
             pltpu.VMEM(small.shape, f32),
+            pltpu.VMEM((2,) + weight.shape[1:], bf16),
         ]
         + ring_sems(size, 2)
         + [
@@ -762,40 +1232,48 @@
             DMA((3, size - 1)),
             DMA((groups - 1,)),
             DMA((groups - 1,)),
+            DMA((2,)),
         ],
-        compiler_params=comm_params(collective_id, 32),
+        compiler_params=comm_params(collective_id, 60),
         name="spread_grads",
-    )(parts, pieces, shared, small)
-
-
-def assemble_kernel(lw, gathered_ref, shared_ref, o_ref):
-    size = gathered_ref.shape[0]
-    inner = size * lw
-    for block in range(size):
-        for half in range(2):
-            at = half * inner + block * lw
-            o_ref[:, at : at + lw] = gathered_ref[block, :, half * lw : (half + 1) * lw].astype(
-                jnp.float32
-            )
-    tail = o_ref.shape[1] - 2 * inner
-    o_ref[:, 2 * inner :] = shared_ref[:, :tail].astype(jnp.float32)
-
-
-def assemble_in(gathered, shared, columns):
-    size, rows, both = gathered.shape
-    step = 64
+    )(parts, pieces, shared, own, small, tokens, weight)
+
+
+def assemble_kernel(blocks, gathered_ref, tail_ref, o_ref):
+    @pl.when(pl.program_id(0) < blocks)
+    def _():
+        o_ref[...] = gathered_ref[0, 0].reshape(o_ref.shape).astype(jnp.float32)
+
+    @pl.when(pl.program_id(0) == blocks)
+    def _():
+        o_ref[...] = tail_ref[...].astype(jnp.float32)
+
+
+def assemble_in(gathered, tail):
+    size, ways, chunks, rows, width = gathered.shape
+    step = chunks * rows
+    blocks = size * ways
+    total = blocks * step + tail.shape[0]
+    steps = blocks + 1
+    pad = -tail.shape[0] % step
+    if tail.shape[0] > step:
+        out = jnp.swapaxes(gathered, 0, 1).reshape(blocks * step, width)
+        return jnp.concatenate([out, tail]).astype(jnp.float32)
     return pl.pallas_call(
-        functools.partial(assemble_kernel, both // 2),
-        grid=(rows // step,),
+        functools.partial(assemble_kernel, blocks),
+        grid=(steps,),
         in_specs=[
-            pl.BlockSpec((size, step, both), lambda i: (0, i, 0)),
-            pl.BlockSpec((step, shared.shape[1]), lambda i: (i, 0)),
+            pl.BlockSpec(
+                (1, 1, chunks, rows, width),
+                lambda i: (lax.rem(i, size), jnp.minimum(i // size, ways - 1), 0, 0, 0),
+            ),
+            pl.BlockSpec((step, width), lambda i: (0, 0)),
         ],
-        out_specs=pl.BlockSpec((step, columns), lambda i: (i, 0)),
-        out_shape=jax.ShapeDtypeStruct((rows, columns), jnp.float32),
-        compiler_params=pltpu.CompilerParams(vmem_limit_bytes=40 * 2**20),
+        out_specs=pl.BlockSpec((step, width), lambda i: (i, 0)),
+        out_shape=jax.ShapeDtypeStruct((total, width), jnp.float32),
+        compiler_params=pltpu.CompilerParams(vmem_limit_bytes=32 * 2**20),
         name="assemble_in",
-    )(gathered, shared)
+    )(gathered, jnp.pad(tail, ((0, pad), (0, 0))))
 
 
 def widen_kernel(x_ref, o_ref):
@@ -854,29 +1332,21 @@
     flat_tokens = tokens.reshape(row_count, width).astype(f32)
     in_scale = row_scale(flat_tokens)
     normed = (flat_tokens * in_scale * norm_gain).astype(bf16)
-    normed_all = ring_gather(normed, 0)
     cot_rows = cotangent.reshape(row_count, width)
-    branch_grad = ring_gather(cot_rows * valid_rows.astype(bf16), 1)
-
-    dt_pad = jnp.zeros((in_weight.shape[0], 128 - local_heads), bf16)
+
+    in_turned = in_weight.T
     local_columns = jnp.concatenate(
         [
-            take(in_weight, channel_start, local_width, 1),
-            take(in_weight, inner_width + channel_start, local_width, 1),
-            in_weight[:, 2 * inner_width : 2 * inner_width + bc_width],
-            take(in_weight, 2 * inner_width + bc_width + head_start, local_heads, 1),
-            dt_pad,
-        ],
-        axis=1,
-    )
-    in_columns = lax.all_gather(local_columns, "wa", axis=0, tiled=True)
-    columns_here = in_columns.shape[1]
+            take(in_turned, channel_start, local_width, 0),
+            take(in_turned, inner_width + channel_start, local_width, 0),
+            in_turned[2 * inner_width : 2 * inner_width + bc_width],
+            take(in_turned, 2 * inner_width + bc_width + head_start, local_heads, 0),
+            jnp.zeros((128 - local_heads, in_weight.shape[0]), bf16),
+        ]
+    )
+    columns_here = local_columns.shape[0]
     blocks = (seq_devices, seqs_here, slot_rows)
-    projected = (
-        jnp.dot(normed_all, in_columns, preferred_element_type=f32)
-        .astype(bf16)
-        .reshape(blocks + (columns_here,))
-    )
+    normed_all, in_columns, projected = project(normed, local_columns, 0)
 
     def lanes(part):
         return jnp.pad(part[None], ((0, 7), (0, 128 - local_heads)))
@@ -896,28 +1366,24 @@
     gain_local = take(out_gain, channel_start, local_width, 0)
     spread, fold, tri, upper = scan_tables(slot_rows, local_width, head_size)
     widths = (local_width, bc_width)
-    gated_heads, y_heads, entering = scan_forward(
-        projected, taps, shift, bias, slope, skip, spread, tri, widths, head_size
-    )
-    gated = gated_heads.reshape(-1, local_width).astype(f32)
-
-    out_full = lax.all_gather(out_weight, "wa", axis=0, tiled=True)
-    out_rows = take(out_full, channel_start, local_width, 0)
-    out_grad = lax.dot_general(
-        branch_grad, out_rows, (((1,), (1,)), ((), ())), preferred_element_type=f32
-    )
-    weighted = out_grad * gain_local
-    sums = seq_total(
-        jnp.stack(
-            [jnp.sum(gated * gated, axis=-1), jnp.sum(weighted * gated, axis=-1)]
-        ).reshape(-1, 128),
-        2,
-    ).reshape(2, -1)
-    out_scale = lax.rsqrt(sums[0] / inner_width + EPS)[:, None]
-    mean_dot = (sums[1] / inner_width)[:, None]
-    normed_out = (gated * out_scale * gain_local).astype(bf16)
-    out_gain_part = jnp.sum(out_grad * gated * out_scale, axis=0)
-    gated_grad = (out_scale * weighted - gated * out_scale**3 * mean_dot).astype(bf16)
+    per_owner = seq_devices // group_devices
+    y_heads, entering, normed_out, gated_grad, gain_sum, branch_grad, out_part = middle(
+        projected,
+        (taps, shift, bias, slope, skip, spread, tri),
+        gain_local[None],
+        cot_rows * valid_rows.astype(bf16),
+        out_weight.reshape(per_owner, local_width, width),
+        inner_width,
+        widths,
+        head_size,
+        1,
+    )
+    normed_out = normed_out.reshape(-1, local_width)
+    branch_grad = branch_grad.reshape(-1, width)
+    out_gain_part = gain_sum[0]
+    out_full = lax.all_gather(
+        lax.optimization_barrier((out_weight, gain_sum))[0], "wa", axis=0, tiled=True
+    )
 
     swapped = lax.all_to_all(
         normed_out.reshape(seq_devices, row_count, local_width), "seq", 0, 0, tiled=True
@@ -930,11 +1396,11 @@
         scatter_dimension=0,
         tiled=True,
     )
-    proj_grad, taps_sum, skip_sum, head_sum = scan_backward(
+    proj_grad, turned_grad, taps_sum, skip_sum, head_sum = scan_backward(
         projected,
         y_heads,
         entering,
-        gated_grad.reshape(blocks + (local_width,)),
+        gated_grad,
         taps,
         shift,
         bias,
@@ -952,43 +1418,21 @@
     skip_grad = jnp.sum(skip_sum[0].reshape(local_heads, head_size), axis=1)
     shift_grad, rates_grad = head_sum[0, :local_heads], head_sum[1, :local_heads]
     in_rows = in_weight.shape[0]
-    in_weight_part = (
-        lax.dot_general(
-            normed_all, proj_grad, (((0,), (0,)), ((), ())), preferred_element_type=f32
-        )
-        .astype(bf16)
-        .reshape(group_devices, in_rows, columns_here)
-    )
-    branch = jnp.dot(
-        jnp.swapaxes(swapped, 0, 1).reshape(row_count, inner_width),
-        out_full,
-        preferred_element_type=f32,
-    )
-    mixed_out = (flat_tokens + valid_rows * branch).astype(bf16).reshape(tokens.shape)
-    normed_grad, pieces, landed = reduce_rows(
+    at_shared = 2 * local_width
+    normed_grad, pieces, main_part, shared_part, own_part = reduce_rows(
         proj_grad.reshape(blocks + (columns_here,)),
         in_columns,
         out_weight_part,
-        in_weight_part,
+        normed_all.reshape(blocks + (width,)),
+        turned_grad,
+        (at_shared, bc_width, 16),
         3,
     )
     normed_grad = normed_grad.reshape(row_count, width)
-    in_weight_sum = lax.dynamic_index_in_dim(
-        in_weight_part, lax.axis_index("wa"), 0, keepdims=False
-    ).astype(f32) + jnp.sum(landed.astype(f32), axis=0)
     token_grad, norm_gain_grad = norm_backward(flat_tokens, in_scale, norm_gain, normed_grad)
     token_grad = token_grad + cot_rows.astype(f32)
 
-    dt_wide = lax.dynamic_update_slice_in_dim(
-        jnp.zeros((in_rows, 128), f32),
-        in_weight_sum[:, 2 * local_width + bc_width :][:, :local_heads],
-        head_start,
-        1,
-    )
-    shared = jnp.concatenate(
-        [in_weight_sum[:, 2 * local_width : 2 * local_width + bc_width], dt_wide], axis=1
-    ).astype(bf16)
-    shared_columns = shared.shape[1]
+    shared_rows = bc_width // seq_devices
     heads = jnp.stack(
         [
             jnp.pad(part, (0, 128 - local_heads))
@@ -1000,19 +1444,24 @@
     packed = jnp.concatenate([part.reshape(-1, 128) for part in own_parts + sum_parts])
     packed_rows = packed.shape[0]
     packed = jnp.pad(packed, ((0, -packed_rows % 8), (0, 0)))
-    per_owner = seq_devices // group_devices
-    gathered, owned, shared_all, small_all = spread_grads(
-        in_weight_sum[:, : 2 * local_width].astype(bf16),
+    gathered, owned, shared_all, small_all, branch = spread_grads(
+        main_part,
         pieces.reshape(group_devices, per_owner, local_width // group_devices, width),
-        shared.reshape(seq_devices, in_rows // seq_devices, shared_columns),
+        shared_part.reshape(seq_devices, shared_rows, in_rows),
+        own_part,
         packed,
+        swapped,
+        out_full.reshape(seq_devices, local_width, width),
         4,
     )
-    in_weight_grad = assemble_in(
-        gathered.reshape(seq_devices, in_rows, 2 * local_width),
-        shared_all.reshape(in_rows, shared_columns),
-        in_weight.shape[1],
-    )
+    mixed_out = (flat_tokens + valid_rows * branch).astype(bf16).reshape(tokens.shape)
+    tail = jnp.concatenate(
+        [
+            shared_all[:, :shared_rows].reshape(bc_width, in_rows),
+            shared_all[:, shared_rows : shared_rows + local_heads].reshape(head_count, in_rows),
+        ]
+    )
+    in_weight_grad = assemble_in(gathered, tail).T
     out_weight_grad = assemble_out(owned)
 
     tile_rows = local_width // 128

time: 644 us -> 586 us (0.910)
  matrix products: 69.6 us -> 9.9 us
  Pallas kernels: 480 us -> 513 us
  local copies, waits for them, and re-layouts: 44.1 us -> 23.1 us
  other arithmetic: 25.6 us -> 14.1 us
    dot_general x4 -> x0, matrix products: 60.3 us -> none  [the longest x1 19.2 us: body(): lax.dot_general(normed_all, proj_grad, (((0,), (0,)), ((), ())), preferre...]
    unnamed x45 -> x44, local copies, waits for them, and re-layouts: 31.3 us -> 9.18 us
    pallas_call x1, Pallas kernels: 129 us -> 147 us  [reduce_rows(): pl.pallas_call(functools.partial(reduce_kernel, size, groups), out_shape=...]
    pallas_call x5 -> x3, Pallas kernels: 199 us -> 210 us  [the longest x1 107 us: middle(): pl.pallas_call(functools.partial(middle_kernel, widths, head_size, size,...]
  transfers between devices with their start and end apart: 4 -> 3, of which waited for: 1 -> 0; matrix products, arithmetic and copies ran while one was open for 10% -> 1% of each run, Pallas kernels for 35% -> 33%
where the time goes in v3:
time: 586 us; the launch traced here: 580 us
  Pallas kernels  513 us (88%)
  local copies, waits for them, and re-layouts  23.1 us (4%)
  between operations  14.5 us (2%)
  other arithmetic  14.1 us (2%)
  matrix products  9.9 us (2%)
    pallas_call x1, Pallas kernels, reduce_rows(): pl.pallas_call(functools.partial(reduce_kernel, size, groups), out_shape=...  147 us
    pallas_call x1, Pallas kernels, middle(): pl.pallas_call(functools.partial(middle_kernel, widths, head_size, size,...  107 us
    pallas_call x1, Pallas kernels, spread_grads(): pl.pallas_call(functools.partial(spread_kernel, size, groups), out_shape=...  106 us
    pallas_call x1, Pallas kernels, project(): pl.pallas_call(functools.partial(project_kernel, size, groups), out_shape...  93.5 us
    pallas_call x1, Pallas kernels, scan_backward(): pl.pallas_call(functools.partial(backward_kernel, widths, head_size, chun...  43 us
  transfers between devices with their start and end apart: 3, of which 0 were waited for; matrix products, arithmetic and copies ran while one was open for 1% of the time, Pallas kernels for 33%

profile of v3, /device:TPU:0, one launch (start us, length us, event | category | flops | bytes accessed | tf_op | source)
XLA Modules:
  0.0 580.1 jit_solution(1908872183022191172)
XLA Ops:
  9.5 1.1 bitcast_dynamic-update-slice_fusion.1
  10.6 1.1 bitcast_dynamic-update-slice_fusion
  11.7 1.0 slice_dynamic-update-slice_fusion
  17.2 1.3 multiply_convert_fusion.x_ref
  18.5 93.5 %project.1 = (bf16[8,2,2,64,2048]{4,3,2,1,0:T(8,128)(2,1)}, bf16[4,1408,512]{2,1,0:T(8,128)(2,1)}, bf16[8,2,128,1408]{3,2,1,0:T(8,128)(2,1)}) custom-call(bf16[2,2,64,2048]{3,2,1,0:T(8,128)(2,1)} %multiply_convert_fusion.x_ref, bf16[1408,512]{1,0:T(8,128)(2,1)} %copy-done.13), custom_call_target="tpu_custom_call" | custom-call | tf_op jit(solution)/shard_map/project/pallas_call | solution.py:573
  112.7 1.3 dynamic_slice.35
  114.1 1.1 broadcast_multiply_fusion.cot_ref
  115.2 106.9 %middle.1 = (bf16[8,2,128,512]{3,2,1,0:T(8,128)(2,1)}, bf16[8,2,512,128]{3,2,1,0:T(8,128)(2,1)}, bf16[8,2,128,512]{3,2,1,0:T(8,128)(2,1)}, bf16[8,2,128,512]{3,2...) custom-call(bf16[8,2,128,1408]{3,2,1,0:T(8,128)(2,1)} %get-tuple-element.3, ...), custom_call_target="tpu_custom_call" | custom-call | tf_op jit(solution)/shard_map/middle/pallas_call | solution.py:831
  222.1 9.9 %convolution_convert_fusion = bf16[512,2048]{1,0:T(8,128)(2,1)} fusion(bf16[2048,512]{1,0:T(8,128)(2,1)} %bitcast.69, bf16[2048,2048]{1,0:T(8,128)(2,1)} %bitcast.87), kind=kOutput, calls=%fused_computation | convolution fusion | flops 4296015872 | bytes 12582912 | tf_op jit(solution)/shard_map/dot_general | solution.py:1392
  232.8 4.5 all-to-all-start
  237.6 1.9 copy-done.2
  239.5 43.0 %scan_backward.1 = (bf16[8,2,128,1408]{3,2,1,0:T(8,128)(2,1)}, bf16[1408,2048]{1,0:T(8,128)(2,1)}, f32[8,768]{1,0:T(8,128)S(1)}, f32[8,512]{1,0:T(8,128)S(1)}, f32[8,128]{1,0:T(8,128)S(1)}) custom-call(bf16[8,2,128,1408]{3,2,1,0:T(8,128)(2,1)} %get-tuple-element.36.proj_ref.before_ref, bf16[8,2,128,1408]{3,2,1,0:T(8,128)(2,1)} %get-tuple-element.36.proj_ref.before_ref, ...), custom_call_target="tpu_custom_call" | custom-call | tf_op jit(solution)/shard_map/scan_backward/pallas_call | solution.py:307
  283.6 146.7 %reduce_rows.1 = (f32[2,128,2048]{2,1,0:T(8,128)}, bf16[8,2,1,64,2048]{4,3,2,1,0:T(8,128)(2,1)}, bf16[1024,512]{1,0:T(8,128)(2,1)}, bf16[256,512]{1,0:T(8,128)(2,1)}, bf16[16,512]{1,0:T(8,128)(2,1)}) custom-call(bf16[8,2,128,1408]{3,2,1,0:T(8,128)(2,1)} %get-tuple-element.40.grad_ref, bf16[4,1408,512]{2,1,0:T(8,128)(2,1)} %get-tuple-element.41.weight_ref, ...), custom_call_target="tpu_custom_call" | custom-call | tf_op jit(solution)/shard_map/reduce_rows/pallas_call | solution.py:1057
  430.4 2.3 fusion.7
  433.6 3.2 fusion.6
  436.8 106.4 %spread_grads.1 = (bf16[8,2,2,256,512]{4,3,2,1,0:T(8,128)(2,1)}, bf16[4,2,128,2048]{3,2,1,0:T(8,128)(2,1)}, bf16[8,48,512]{2,1,0:T(8,128)(2,1)}, f32[8,56,128]{2,1,0:T(8,128)}, f32[256,2048]{1,0:T(8,128)}) custom-call(bf16[2,2,256,512]{3,2,1,0:T(8,128)(2,1)} %bitcast.71, bf16[4,2,128,2048]{3,2,1,0:T(8,128)(2,1)} %bitcast.68, bf16[8,32,512]{2,1,0:T(8,128)(2,1)} %bitcast.77, ...), custom_call_target="tpu_custom_call" | custom-call | tf_op jit(solution)/shard_map/spread_grads/pallas_call | solution.py:1208
  543.2 0.9 slice.114
  544.1 0.9 slice_reduce_fusion
  545.8 1.0 slice.112
  546.7 0.8 slice_bitcast_fusion
  549.0 7.3 %assemble_out.1 = f32[1024,2048]{1,0:T(8,128)} custom-call(bf16[4,2,128,2048]{3,2,1,0:T(8,128)(2,1)} %get-tuple-element.60.x_ref), custom_call_target="tpu_custom_call" | custom-call | tf_op jit(solution)/shard_map/assemble_out/pallas_call | solution.py:1285
  559.4 3.4 copy-done
  562.7 9.3 %assemble_in.1 = f32[8512,512]{1,0:T(8,128)} custom-call(bf16[8,2,2,256,512]{4,3,2,1,0:T(8,128)(2,1)S(1)} %copy-done, bf16[512,512]{1,0:T(8,128)(2,1)S(1)} %fusion.10.tail_ref), custom_call_target="tpu_custom_call" | custom-call | tf_op jit(solution)/shard_map/assemble_in/pallas_call | solution.py:1262
  572.0 1.3 fusion
  (105 shorter events, 15.5 us)
Async XLA Ops:
  7.2 6.6 %slice-start.1 = ((f32[4352]{0:T(1024)}), f32[256]{0:T(256)S(1)}, s32[]{:S(2)}) async-start(f32[4352]{0:T(1024)} %param.17), calls=%async_computation.5 | async-start | bytes 2048 | tf_op jit(solution)/shard_map/slice | solution.py:1361
  7.2 6.2 %copy-start.10 = (bf16[2,128,2048]{2,1,0:T(8,128)(2,1)S(1)}, bf16[2,128,2048]{2,1,0:T(8,128)(2,1)}, u32[]{:S(2)}) copy-start(bf16[2,128,2048]{2,1,0:T(8,128)(2,1)} %param.12) | copy-start | bytes 3145732
  7.2 7.2 %copy-start.18 = (f32[64]{0:T(128)S(1)}, f32[64]{0:T(128)}, u32[]{:S(2)}) copy-start(f32[64]{0:T(128)} %param.18) | copy-start | bytes 772
  7.2 7.2 %copy-start.17 = (f32[64]{0:T(128)S(1)}, f32[64]{0:T(128)}, u32[]{:S(2)}) copy-start(f32[64]{0:T(128)} %param.19) | copy-start | bytes 772
  7.2 8.5 %copy-start.19 = (f32[64]{0:T(128)S(1)}, f32[64]{0:T(128)}, u32[]{:S(2)}) copy-start(f32[64]{0:T(128)} %param.20) | copy-start | bytes 772
  7.2 276.4 %reduce-scatter.2.cloned.1.call-start = ((), (), s32[]{:S(2)}) async-start(), calls=%async_computation.2 | async-start | bytes 2621440 | tf_op jit(solution)/shard_map/reduce_scatter | solution.py:1391
  7.3 9.9 %copy-start.15 = (f32[2048]{0:T(1024)S(1)}, f32[2048]{0:T(1024)}, u32[]{:S(2)}) copy-start(f32[2048]{0:T(1024)} %param.14) | copy-start | bytes 24580
  13.4 3.8 copy-start.13
  17.2 94.8 %slice-start = ((f32[4,4352]{1,0:T(4,128)}), f32[4,256]{1,0:T(4,128)S(1)}, s32[]{:S(2)}) async-start(f32[4,4352]{1,0:T(4,128)} %param.16), calls=%async_computation.4 | async-start | bytes 8192 | tf_op jit(solution)/shard_map/slice | solution.py:1356
  17.2 96.8 %copy-start.16 = (s32[2]{0:T(128)S(1)}, s32[2]{0:T(128)}, u32[]{:S(2)}) copy-start(s32[2]{0:T(128)} %param.13) | copy-start | bytes 28
  17.2 96.9 %copy-start.12 = (bf16[2,128,2048]{2,1,0:T(8,128)(2,1)S(1)}, bf16[2,128,2048]{2,1,0:T(8,128)(2,1)}, u32[]{:S(2)}) copy-start(bf16[2,128,2048]{2,1,0:T(8,128)(2,1)} %param.23) | copy-start | bytes 3145732
  232.0 204.8 %all-gather.2.cloned.1.call-start = ((), (), s32[]{:S(2)}) async-start(), calls=%async_computation.3 | async-start | bytes 20971520 | tf_op jit(solution)/shard_map/all_gather | solution.py:1384
  232.8 4.7 copy-start.1
  232.8 4.7 copy-start.3
  232.8 4.7 copy-start.4
  232.8 4.7 copy-start.5
  232.8 4.7 copy-start.6
  232.8 4.7 copy-start.7
  232.8 4.7 copy-start.8
  232.8 4.7 copy-start.9
  232.8 203.9 %all-to-all-start = ((bf16[8,256,512]{2,1,0:T(8,128)(2,1)}), bf16[8,256,512]{2,1,0:T(8,128)(2,1)}, u32[]{:S(2)}, u32[]{:S(2)}) async-start(bf16[8,256,512]{2,1,0:T(8,128)(2,1)} %bitcast.70), calls=%async_computation.1 | async-start | bytes 4194304 | tf_op jit(solution)/shard_map/all_to_all | solution.py:1388
  430.4 3.2 copy-start.11
  559.4 3.4 copy-start
  562.7 9.3 %copy-start.14 = (f32[256,2048]{1,0:T(8,128)S(1)}, f32[256,2048]{1,0:T(8,128)}, u32[]{:S(2)}) copy-start(f32[256,2048]{1,0:T(8,128)} %get-tuple-element.56) | copy-start | bytes 6291460
  (1 other events, 1.9 us)
Sparse Core Ops, SparseCore 0:
  232.1 30.0 reduce-scatter.1
  263.9 147.9 all-gather.1

commit v4 on v2

v4 whole, which is shorter than its diff:
```python
import functools

import jax
import jax.numpy as jnp
from jax import lax
from jax.experimental import pallas as pl
from jax.experimental.pallas import tpu as pltpu
from jax.sharding import PartitionSpec as P

KW = 4
EPS = 1e-05
HIGHEST = lax.Precision.HIGHEST
MESH = pl.DeviceIdType.MESH


def row_scale(values):
    return lax.rsqrt(jnp.mean(values * values, axis=-1, keepdims=True) + EPS)


def norm_backward(values, row_scales, gain_vec, grad_out):
    weighted = grad_out * gain_vec
    return row_scales * weighted - values * row_scales**3 * jnp.mean(
        weighted * values, axis=-1, keepdims=True
    )


def dot(a, b, ca, cb, precision=None):
    return lax.dot_general(
        a, b, (((ca,), (cb,)), ((), ())), precision=precision, preferred_element_type=jnp.float32
    )


def chunk_front(proj_ref, ext, taps_ref, shift_ref, bias_ref, slope_ref, tri_ref, widths):
    lw, bc = widths
    rows = proj_ref.shape[2]
    ext[8:, :] = proj_ref[0, 0, :, lw : 2 * lw + bc].astype(jnp.float32)
    conv = shift_ref[0:1, :]
    for k in range(KW):
        conv = conv + taps_ref[k : k + 1, :] * ext[5 + k : 5 + k + rows, :]
    conv_sig = lax.logistic(conv)
    act = conv * conv_sig
    step_in = proj_ref[0, 0, :, 2 * lw + bc :].astype(jnp.float32) + bias_ref[0:1, :]
    steps = jnp.maximum(step_in, 0.0) + jnp.log1p(jnp.exp(-jnp.abs(step_in)))
    rates = slope_ref[0:1, :] * steps
    cum = dot(tri_ref[...], rates, 1, 0, HIGHEST)
    return conv, conv_sig, act, step_in, steps, rates, cum


def head_masks(rows, head_size):
    lane = lax.broadcasted_iota(jnp.int32, (rows, 128), 1)
    row = lax.broadcasted_iota(jnp.int32, (rows, rows), 0)
    col = lax.broadcasted_iota(jnp.int32, (rows, rows), 1)
    return lane, row >= col


def forward_chunk(
    widths,
    head_size,
    start,
    proj_ref,
    taps_ref,
    shift_ref,
    bias_ref,
    slope_ref,
    skip_ref,
    spread_ref,
    tri_ref,
    gated_ref,
    y_ref,
    enter_ref,
    state,
    ext,
    halo,
):
    lw, bc = widths
    bf16, f32 = jnp.bfloat16, jnp.float32
    rows = proj_ref.shape[2]
    per_tile = 128 // head_size

    @pl.when(start)
    def _():
        state[...] = jnp.zeros_like(state)
        halo[...] = jnp.zeros_like(halo)

    ext[0:8, :] = halo[...]
    _, _, act, _, steps, _, cum = chunk_front(
        proj_ref, ext, taps_ref, shift_ref, bias_ref, slope_ref, tri_ref, widths
    )
    halo[...] = ext[rows : rows + 8, :]
    x = act[:, :lw]
    xb = x.astype(bf16)
    b_rows = act[:, lw : lw + bc // 2].astype(bf16)
    c_rows = act[:, lw + bc // 2 :].astype(bf16)
    cum_t, steps_t = cum.T, steps.T
    last = cum[rows - 1 : rows, :]
    grow = dot(jnp.exp(cum).astype(bf16), spread_ref[...], 1, 0)
    tail = dot((jnp.exp(last - cum) * steps).astype(bf16), spread_ref[...], 1, 0)
    scores = dot(c_rows, b_rows, 1, 1)
    entering = state[...].astype(bf16)
    enter_ref[0, 0] = entering
    y = dot(c_rows, entering, 1, 1) * grow + skip_ref[0:1, :] * x
    added = dot((x * tail).astype(bf16), b_rows, 0, 0)
    lane, causal = head_masks(rows, head_size)
    gate = proj_ref[0, 0, :, :lw].astype(f32)
    silu_gate = gate * lax.logistic(gate)
    for tile in range(lw // 128):
        cols = slice(tile * 128, (tile + 1) * 128)
        inner = None
        for sub in range(per_tile):
            head = tile * per_tile + sub
            log_decay = cum[:, head : head + 1] - cum_t[head : head + 1, :]
            decay = jnp.exp(jnp.where(causal, log_decay, -1e30))
            weights = (scores * decay * steps_t[head : head + 1, :]).astype(bf16)
            part = dot(weights, xb[:, cols], 1, 0)
            inner = part if inner is None else jnp.where(lane >= sub * head_size, part, inner)
            span = slice(head * head_size, (head + 1) * head_size)
            state[span, :] = (
                jnp.exp(cum[rows - 1 : rows, head : head + 1]) * state[span, :] + added[span, :]
            )
        y_tile = y[:, cols] + inner
        y_ref[0, 0, :, cols] = y_tile.astype(bf16)
        gated_ref[:, cols] = (y_tile * silu_gate[:, cols]).astype(bf16)


def backward_kernel(
    widths,
    head_size,
    chunks,
    proj_ref,
    before_ref,
    y_ref,
    enter_ref,
    grad_ref,
    taps_ref,
    shift_ref,
    bias_ref,
    slope_ref,
    skip_ref,
    spread_ref,
    fold_ref,
    tri_ref,
    upper_ref,
    out_ref,
    turned_ref,
    taps_acc,
    skip_acc,
    head_acc,
    lam,
    ext,
    later,
    after,
):
    lw, bc = widths
    state_size = bc // 2
    bf16, f32 = jnp.bfloat16, jnp.float32
    rows = proj_ref.shape[2]
    per_tile = 128 // head_size
    chunk = chunks - 1 - pl.program_id(1)

    @pl.when((pl.program_id(0) == 0) & (pl.program_id(1) == 0))
    def _():
        taps_acc[...] = jnp.zeros_like(taps_acc)
        skip_acc[...] = jnp.zeros_like(skip_acc)
        head_acc[...] = jnp.zeros_like(head_acc)

    @pl.when(pl.program_id(1) == 0)
    def _():
        lam[...] = jnp.zeros_like(lam)
        after[...] = jnp.zeros_like(after)

    ext[0:8, :] = jnp.where(
        chunk > 0, before_ref[0, 0, 8:16, lw : 2 * lw + bc].astype(f32), 0.0
    )
    conv, conv_sig, act, step_in, steps, rates, cum = chunk_front(
        proj_ref, ext, taps_ref, shift_ref, bias_ref, slope_ref, tri_ref, widths
    )
    x = act[:, :lw]
    xb = x.astype(bf16)
    b_rows = act[:, lw : lw + state_size].astype(bf16)
    c_rows = act[:, lw + state_size :].astype(bf16)
    cum_t, steps_t = cum.T, steps.T
    last = cum[rows - 1 : rows, :]
    to_end = jnp.exp(last - cum)
    tail_heads = to_end * steps
    grow = dot(jnp.exp(cum).astype(bf16), spread_ref[...], 1, 0)
    tail = dot(tail_heads.astype(bf16), spread_ref[...], 1, 0)
    scores = dot(c_rows, b_rows, 1, 1)

    gate = proj_ref[0, 0, :, :lw].astype(f32)
    gate_sig = lax.logistic(gate)
    grad = grad_ref[0, 0].astype(f32)
    y_grad = grad * gate * gate_sig
    out_ref[0, 0, :, :lw] = (
        grad * y_ref[0, 0].astype(f32) * (gate_sig * (1.0 + gate * (1.0 - gate_sig)))
    ).astype(bf16)
    yb = y_grad.astype(bf16)

    entering = enter_ref[0, 0]
    grown = y_grad * grow
    grown_b = grown.astype(bf16)
    c_grad = dot(grown_b, entering, 1, 0)
    carried = dot((grown * dot(c_rows, entering, 1, 1)).astype(bf16), fold_ref[...], 1, 0)
    lam_now = lam[...]
    lam_b = lam_now.astype(bf16)
    from_lam = dot(b_rows, lam_b, 1, 1)
    b_grad = dot((x * tail).astype(bf16), lam_b, 1, 0)
    x_lam = dot((x * from_lam).astype(bf16), fold_ref[...], 1, 0)
    x_grad = skip_ref[0:1, :] * y_grad + tail * from_lam
    skip_acc[0:1, :] += jnp.sum(y_grad * x, axis=0, keepdims=True)
    ones = jnp.ones((8, state_size), bf16)
    kept = dot(
        dot(ones, (lam_now * entering.astype(f32)).astype(bf16), 1, 1),
        fold_ref[...].astype(f32),
        1,
        0,
        HIGHEST,
    )
    through = jnp.exp(last) * kept[0:1, :]
    lam_add = dot(grown_b, c_rows, 0, 0)

    lane, causal = head_masks(rows, head_size)
    score_grad = None
    row_sums = jnp.zeros((rows, 128), f32)
    col_sums = []
    x_tiles = []
    for tile in range(lw // 128):
        cols = slice(tile * 128, (tile + 1) * 128)
        inner = None
        for sub in range(per_tile):
            head = tile * per_tile + sub
            log_decay = cum[:, head : head + 1] - cum_t[head : head + 1, :]
            decay = jnp.exp(jnp.where(causal, log_decay, -1e30))
            step_row = steps_t[head : head + 1, :]
            weights = (scores * decay * step_row).astype(bf16)
            inside = (lane >= sub * head_size) & (lane < (sub + 1) * head_size)
            y_head = jnp.where(inside, yb[:, cols], jnp.zeros_like(yb[:, cols]))
            weights_grad = dot(y_head, xb[:, cols], 1, 1)
            part = dot(weights, yb[:, cols], 0, 0)
            inner = part if inner is None else jnp.where(lane >= sub * head_size, part, inner)
            decayed = weights_grad * decay
            stepped = decayed * step_row
            score_grad = stepped if score_grad is None else score_grad + stepped
            col_sums.append(jnp.sum(decayed * scores, axis=0, keepdims=True))
            row_sum = jnp.sum(stepped * scores, axis=1, keepdims=True)
            row_sums = row_sums + jnp.where(lane == head, row_sum, 0.0)
            span = slice(head * head_size, (head + 1) * head_size)
            lam[span, :] = (
                jnp.exp(cum[rows - 1 : rows, head : head + 1]) * lam_now[span, :] + lam_add[span, :]
            )
        x_tiles.append(x_grad[:, cols] + inner)
    col_sums.append(jnp.zeros((rows - len(col_sums), rows), f32))
    col_sum = jnp.concatenate(col_sums, axis=0).T
    source = row_sums - steps * col_sum + carried
    rates_grad = (
        dot(upper_ref[...], source, 1, 0, HIGHEST)
        + dot(1.0 - upper_ref[...], tail_heads * x_lam, 1, 0, HIGHEST)
        + through
    )
    steps_grad = col_sum + to_end * x_lam + rates_grad * slope_ref[0:1, :]
    raw_grad = steps_grad * lax.logistic(step_in)
    out_ref[0, 0, :, 2 * lw + bc :] = raw_grad.astype(bf16)
    head_acc[0:1, :] += jnp.sum(raw_grad, axis=0, keepdims=True)
    head_acc[1:2, :] += jnp.sum(rates_grad * rates, axis=0, keepdims=True)
    score_b = score_grad.astype(bf16)
    c_grad = c_grad + dot(score_b, b_rows, 1, 0)
    b_grad = b_grad + dot(score_b, c_rows, 0, 0)
    act_grad = jnp.concatenate(x_tiles + [b_grad, c_grad], axis=1)
    conv_grad = act_grad * (conv_sig * (1.0 + conv * (1.0 - conv_sig)))
    later[0:rows, :] = conv_grad
    later[rows : rows + 8, :] = after[...]
    after[...] = conv_grad[0:8, :]
    total = None
    for k in range(KW):
        term = taps_ref[k : k + 1, :] * later[3 - k : 3 - k + rows, :]
        total = term if total is None else total + term
        taps_acc[k : k + 1, :] += jnp.sum(conv_grad * ext[5 + k : 5 + k + rows, :], axis=0, keepdims=True)
    taps_acc[KW : KW + 1, :] += jnp.sum(conv_grad, axis=0, keepdims=True)

    @pl.when((pl.program_id(0) == pl.num_programs(0) - 1) & (chunk == 0))
    def _():
        head_acc[2:3, :] = dot(
            skip_acc[...], fold_ref[...].astype(f32), 1, 0, HIGHEST
        )[0:1, :]
    out_ref[0, 0, :, lw : 2 * lw + bc] = total.astype(bf16)
    turned_ref[...] = out_ref[0, 0].T


def whole_spec(array):
    return pl.BlockSpec(array.shape, lambda q, c: (0,) * array.ndim)


def scan_tables(rows, local_width, head_size):
    head_of = jnp.arange(local_width) // head_size
    spread = (jnp.arange(128)[:, None] == head_of[None, :]).astype(jnp.bfloat16)
    tri = (jnp.arange(rows)[:, None] >= jnp.arange(rows)[None, :]).astype(jnp.float32)
    return spread, spread.T, tri, tri.T


def scan_backward(
    proj, y, enter, grad, taps, shift, bias, slope, skip, spread, fold, tri, upper, widths, head_size
):
    chunks, seqs, rows, cols = proj.shape
    lw, bc = widths
    block = lambda *tail: pl.BlockSpec((1, 1) + tail, lambda q, c: (chunks - 1 - c, q, 0, 0))
    before = pl.BlockSpec(
        (1, 1, 16, cols),
        lambda q, c: (jnp.maximum(chunks - 2 - c, 0), q, rows // 16 - 1, 0),
    )
    tables = (taps, shift, bias, slope, skip, spread, fold, tri, upper)
    sums = [(8, lw + bc), (8, lw), (8, 128)]
    return pl.pallas_call(
        functools.partial(backward_kernel, widths, head_size, chunks),
        grid=(seqs, chunks),
        in_specs=[block(rows, cols), before, block(rows, lw), block(lw, bc // 2), block(rows, lw)]
        + [whole_spec(t) for t in tables],
        out_specs=[
            block(rows, cols),
            pl.BlockSpec((cols, rows), lambda q, c: (0, (chunks - 1 - c) * seqs + q)),
        ]
        + [pl.BlockSpec(s, lambda q, c: (0, 0)) for s in sums],
        out_shape=[
            jax.ShapeDtypeStruct(proj.shape, jnp.bfloat16),
            jax.ShapeDtypeStruct((cols, chunks * seqs * rows), jnp.bfloat16),
        ]
        + [jax.ShapeDtypeStruct(s, jnp.float32) for s in sums],
        scratch_shapes=[
            pltpu.VMEM((lw, bc // 2), jnp.float32),
            pltpu.VMEM((rows + 8, lw + bc), jnp.float32),
            pltpu.VMEM((rows + 8, lw + bc), jnp.float32),
            pltpu.VMEM((8, lw + bc), jnp.float32),
        ],
        compiler_params=pltpu.CompilerParams(vmem_limit_bytes=48 * 2**20),
        name="scan_backward",
    )(proj, proj, y, enter, grad, *tables)


def ring_pos(index, size):
    row, side = index // 2, index % 2
    return row + side * (size - 1 - 2 * row)


def ring_index(pos, size):
    side = pos // (size // 2)
    row = pos + side * (size - 1 - 2 * pos)
    return row * 2 + side


def greet(peers):
    barrier = pltpu.get_barrier_semaphore()
    for peer in peers:
        pl.semaphore_signal(barrier, inc=1, device_id=peer, device_id_type=MESH)
    pl.semaphore_wait(barrier, len(peers))


def push(source, target, send_sem, recv_sem, peer):
    return pltpu.make_async_remote_copy(
        source, target, send_sem, recv_sem, device_id=peer, device_id_type=MESH
    )


def neighbours(size):
    me, group = lax.axis_index("seq"), lax.axis_index("wa")
    pos = ring_pos(me, size)
    right = (ring_index((pos + 1) % size, size), group)
    left = (ring_index((pos + size - 1) % size, size), group)
    return me, group, pos, right, left


def others(index, size):
    return [(index + offset) % size for offset in range(1, size)]


ANY = pl.BlockSpec(memory_space=pl.ANY)
VMEM = pl.BlockSpec(memory_space=pltpu.VMEM)


def comm_params(collective_id, megabytes=None):
    limit = None if megabytes is None else megabytes * 2**20
    return pltpu.CompilerParams(
        collective_id=collective_id, has_side_effects=True, vmem_limit_bytes=limit
    )


class RingGather:
    def __init__(self, size, x_ref, o_ref, send_sem, recv_sem, local_sem):
        self.size, self.x, self.o = size, x_ref, o_ref
        self.send, self.recv, self.local = send_sem, recv_sem, local_sem
        self.chunks = x_ref.shape[1]
        self.me, _, self.pos, self.right, self.left = neighbours(size)

    def copy(self, step, chunk, way, first=False):
        size = self.size
        if way == 0:
            block, peer = ring_index((self.pos - step + size) % size, size), self.right
        else:
            block, peer = ring_index((self.pos + step) % size, size), self.left
        source = self.x.at[way, chunk] if first else self.o.at[block, way, chunk]
        return push(
            source,
            self.o.at[block, way, chunk],
            self.send.at[step, chunk, way],
            self.recv.at[step, chunk, way],
            peer,
        )

    def kept(self):
        return pltpu.make_async_copy(self.x, self.o.at[self.me], self.local)

    def start(self):
        self.kept().start()
        for chunk in range(self.chunks):
            for way in range(2):
                self.copy(0, chunk, way, True).start()

    def advance(self, step):
        for chunk in range(self.chunks):
            for way in range(2):
                self.copy(step - 1, chunk, way).wait_recv()
                self.copy(step, chunk, way).start()

    def arrive(self):
        last = self.size - 2
        for chunk in range(self.chunks):
            for way in range(2):
                self.copy(last, chunk, way).wait_recv()

    def finish(self):
        self.arrive()
        self.settle()

    def settle(self):
        def drain(step, carry):
            for chunk in range(self.chunks):
                for way in range(2):
                    self.copy(step, chunk, way).wait_send()
            return carry

        lax.fori_loop(0, self.size - 1, drain, 0)
        self.kept().wait()


def ring_parts(x, chunks):
    return x.reshape(2, chunks, x.shape[0] // (2 * chunks), x.shape[1])


def ring_sems(size, chunks):
    return [
        pltpu.SemaphoreType.DMA((size - 1, chunks, 2)),
        pltpu.SemaphoreType.DMA((size - 1, chunks, 2)),
        pltpu.SemaphoreType.DMA,
    ]


def front_kernel(
    widths,
    head_size,
    size,
    groups,
    inner,
    x_ref,
    w_ref,
    cot_ref,
    shard_ref,
    taps_ref,
    shift_ref,
    bias_ref,
    slope_ref,
    skip_ref,
    spread_ref,
    tri_ref,
    gain_ref,
    rows_ref,
    weights_ref,
    proj_ref,
    y_ref,
    enter_ref,
    normed_ref,
    turned_ref,
    grad_ref,
    gain_acc,
    branch_ref,
    part_ref,
    weights,
    projected,
    taken,
    state,
    ext,
    halo,
    gated,
    out_grad,
    y_held,
    enter_held,
    out_rows,
    out_turned,
    sums,
    landing,
    weight_send,
    weight_recv,
    weight_local,
    take_sem,
    proj_sem,
    held_sem,
    shard_send,
    shard_recv,
    shard_local,
    pair_send,
    pair_recv,
    *ring_refs,
):
    bf16, f32 = jnp.bfloat16, jnp.float32
    me, group, pos, right, left = neighbours(size)
    rows, lw = gated.shape[2:]
    depth = weights.shape[2]
    peers = [(other, group) for other in others(me, size)]
    mates = [(me, other) for other in others(group, groups)]
    sibling = (me, group + 1 - 2 * lax.rem(group, 2))
    across = (me, lax.rem(group + 2, groups))
    per_owner = size // groups
    chosen = lax.rem(me, per_owner)
    owner = me // per_owner
    greet(mates + peers)
    ring = RingGather(size, x_ref, rows_ref, *ring_refs[0:3])
    cot_ring = RingGather(size, cot_ref, branch_ref, *ring_refs[3:6])
    ring.start()
    sent = [
        push(w_ref, weights.at[group], weight_send.at[k], weight_recv.at[k], mate)
        for k, mate in enumerate(mates)
    ]
    for copy in sent:
        copy.start()
    kept = pltpu.make_async_copy(w_ref, weights.at[group], weight_local.at[0])
    kept.start()

    def shards(step, offset=0):
        at = lax.rem(chosen + offset, per_owner)
        held_by = across[1] if step == 2 else group
        source = part_ref.at[held_by, at] if step == 2 else shard_ref.at[at]
        return push(
            source,
            part_ref.at[held_by, at],
            shard_send.at[step, offset],
            shard_recv.at[step, offset],
            across if step == 0 else sibling,
        )

    def block_of(pair, way):
        return ring_index((pos - pair + size) % size if way == 0 else (pos + pair) % size, size)

    def stream(source_ref, landed_ref, low, high, compute, own=False):
        def take(pair, slot, way):
            source = source_ref.at[way] if own else landed_ref.at[block_of(pair, way), way]
            return pltpu.make_async_copy(source, taken.at[slot, way], take_sem.at[slot, way])

        for way in range(2):
            take(low, lax.rem(low, 2), way).start()

        def one(pair, carry):
            slot = lax.rem(pair, 2)
            for way in range(2):
                take(pair, slot, way).wait()

            @pl.when(pair + 1 < high)
            def _():
                for way in range(2):
                    take(pair + 1, 1 - slot, way).start()

            compute(pair, slot)
            return carry

        lax.fori_loop(low, high, one, 0)

    def put(pair, way):
        block = block_of(pair, way)
        return pltpu.make_async_copy(
            projected.at[block, way], proj_ref.at[block, way], proj_sem.at[pair, way]
        )

    def project(pair, slot):
        for way in range(2):
            x = taken[slot, way].reshape(rows, taken.shape[4])
            total = None
            for part in range(groups):
                term = dot(x[:, part * depth : (part + 1) * depth], weights[part], 1, 1)
                total = term if total is None else total + term
            projected[block_of(pair, way), way] = total.astype(bf16)
            put(pair, way).start()

    def advance(step, carry):
        ring.advance(step)
        return carry

    def turns(turn, count):
        return 1 + (turn * (size - 2)) // count, 1 + ((turn + 1) * (size - 2)) // count

    middle = size // 2 + 1
    lax.fori_loop(1, middle, advance, 0)
    kept.wait()
    for copy in sent:
        copy.wait_recv()
    flushed = pltpu.make_async_copy(weights, weights_ref, weight_local.at[1])
    flushed.start()
    shards(0).start()
    shards(1).start()
    stream(x_ref, rows_ref, 0, 1, project, own=True)

    def late(step, carry):
        ring.advance(step)
        stream(x_ref, rows_ref, *turns(step - middle, size - 1 - middle), project)
        return carry

    lax.fori_loop(middle, size - 2, late, 0)
    ring.advance(size - 2)
    cot_ring.start()
    stream(x_ref, rows_ref, *turns(size - 2 - middle, size - 1 - middle), project)
    ring.arrive()
    stream(x_ref, rows_ref, size - 1, size, project)
    cot_ring.advance(1)

    def keep(index, slot):
        seq, chunk = index // size, lax.rem(index, size)
        return [
            pltpu.make_async_copy(y_held.at[slot, 0], y_ref.at[chunk, seq], held_sem.at[slot, 0]),
            pltpu.make_async_copy(
                enter_held.at[slot, 0], enter_ref.at[chunk, seq], held_sem.at[slot, 1]
            ),
        ]

    def scan(index, carry):
        seq, chunk = index // size, lax.rem(index, size)
        slot = lax.rem(index, 2)

        @pl.when(index >= 2)
        def _():
            for copy in keep(index - 2, slot):
                copy.wait()

        forward_chunk(
            widths,
            head_size,
            chunk == 0,
            projected.at[pl.ds(chunk, 1), pl.ds(seq, 1)],
            taps_ref,
            shift_ref,
            bias_ref,
            slope_ref,
            skip_ref,
            spread_ref,
            tri_ref,
            gated.at[chunk, seq],
            y_held.at[pl.ds(slot, 1)],
            enter_held.at[pl.ds(slot, 1)],
            state,
            ext,
            halo,
        )
        for copy in keep(index, slot):
            copy.start()

        @pl.when(index == size + 2)
        def _():
            cot_ring.advance(2)

        return carry

    lax.fori_loop(0, 2 * size, scan, 0)
    first, second, third = (shards(step) for step in range(3))
    first.wait_recv()
    third.start()
    for offset in range(1, per_owner):
        shards(0, offset).start()
        shards(1, offset).start()
    second.wait_recv()
    cot_ring.advance(3)
    third.wait_recv()

    @pl.when(owner == group)
    def _():
        loaded = pltpu.make_async_copy(shard_ref.at[chosen], out_rows, shard_local)
        loaded.start()
        loaded.wait()

    @pl.when(owner != group)
    def _():
        loaded = pltpu.make_async_copy(part_ref.at[owner, chosen], out_rows, shard_local)
        loaded.start()
        loaded.wait()

    out_turned[...] = out_rows[...].T
    ones = jnp.ones((8, lw), bf16)

    def compute(pair, slot):
        for way in range(2):
            block = block_of(pair, way)
            values = dot(taken[slot, way].reshape(rows, taken.shape[4]), out_turned[...], 1, 0)
            out_grad[block, way] = values
            here = gated[block, way].astype(f32)
            weighted = values * gain_ref[0:1, :] * here
            at = pl.ds(block * 2 + way, 1)
            sums[0, at, :] = dot(ones, (here * here).astype(bf16), 1, 1)[0:1, :]
            sums[1, at, :] = dot(ones, weighted.astype(bf16), 1, 1)[0:1, :]

    stream(cot_ref, branch_ref, 0, 1, compute, own=True)
    stream(cot_ref, branch_ref, *turns(0, size - 4), compute)

    def cot_late(step, carry):
        cot_ring.advance(step)
        stream(cot_ref, branch_ref, *turns(step - 3, size - 4), compute)
        return carry

    lax.fori_loop(4, size - 1, cot_late, 0)
    cot_ring.arrive()
    stream(cot_ref, branch_ref, size - 1, size, compute)
    copies = [
        push(sums, landing.at[k], pair_send.at[k], pair_recv.at[k], peer)
        for k, peer in enumerate(peers)
    ]
    for copy in copies:
        copy.start()
    total = sums[...]
    for k, copy in enumerate(copies):
        copy.wait_recv()
        total = total + landing[k]
    scale = lax.rsqrt(total[0] / inner + EPS)
    pull = scale * scale * scale * (total[1] / inner)
    fill = jnp.zeros((128 - 2 * size, rows), f32)
    scale_turned = jnp.concatenate([scale, fill]).T
    pull_turned = jnp.concatenate([pull, fill]).T
    lane = lax.broadcasted_iota(jnp.int32, (rows, 128), 1)
    gain_acc[...] = jnp.zeros_like(gain_acc)

    def finish(block, carry):
        for way in range(2):
            mask = lane == block * 2 + way
            by = jnp.sum(jnp.where(mask, scale_turned, 0.0), axis=1, keepdims=True)
            less = jnp.sum(jnp.where(mask, pull_turned, 0.0), axis=1, keepdims=True)
            here = gated[block, way].astype(f32)
            values = out_grad[block, way]
            scaled = here * by
            normed = (scaled * gain_ref[0:1, :]).astype(bf16)
            normed_ref[block, way] = normed
            turned_ref[block, :, way * rows : (way + 1) * rows] = normed.T
            grad_ref[block, way] = (values * gain_ref[0:1, :] * by - here * less).astype(bf16)
            gain_acc[0:1, :] += jnp.sum(values * scaled, axis=0, keepdims=True)
        return carry

    lax.fori_loop(0, size, finish, 0)
    for offset in range(1, per_owner):
        shards(0, offset).wait_recv()
        shards(2, offset).start()
    for copy in sent + copies + [first, second, third]:
        copy.wait_send()
    flushed.wait()
    for index in (2 * size - 2, 2 * size - 1):
        for copy in keep(index, index % 2):
            copy.wait()

    def settle(pair, carry):
        for way in range(2):
            put(pair, way).wait()
        return carry

    lax.fori_loop(0, size, settle, 0)
    ring.settle()
    cot_ring.settle()
    for offset in range(1, per_owner):
        shards(1, offset).wait_recv()
        shards(2, offset).wait_recv()
        for step in range(3):
            shards(step, offset).wait_send()


def front(x, weight, cot, shard, tables, gain, inner, widths, head_size, collective_id):
    size, groups = lax.axis_size("seq"), lax.axis_size("wa")
    parts, cot_parts = ring_parts(x, 2), ring_parts(cot, 2)
    cols, depth = weight.shape
    rows = x.shape[0] // 2
    width = x.shape[1]
    lw, bc = widths
    per_owner = size // groups
    bf16, f32, DMA, vmem = jnp.bfloat16, jnp.float32, pltpu.SemaphoreType.DMA, pltpu.VMEM
    whole = (size, 2, rows, lw)
    shape = jax.ShapeDtypeStruct
    return pl.pallas_call(
        functools.partial(front_kernel, widths, head_size, size, groups, inner),
        out_shape=[
            shape((size,) + parts.shape, bf16),
            shape((groups, cols, depth), bf16),
            shape((size, 2, rows, cols), bf16),
            shape(whole, bf16),
            shape((size, 2, lw, bc // 2), bf16),
            shape(whole, bf16),
            shape((size, lw, 2 * rows), bf16),
            shape(whole, bf16),
            shape((8, lw), f32),
            shape((size,) + parts.shape, bf16),
            shape((groups, per_owner, lw, width), bf16),
        ],
        in_specs=[ANY] * 4 + [VMEM] * 8,
        out_specs=[ANY] * 5 + [VMEM] * 4 + [ANY] * 2,
        scratch_shapes=[
            vmem((groups, cols, depth), bf16),
            vmem((size, 2, rows, cols), bf16),
            vmem((2,) + parts.shape, bf16),
            vmem((lw, bc // 2), f32),
            vmem((rows + 8, lw + bc), f32),
            vmem((8, lw + bc), f32),
            vmem(whole, bf16),
            vmem(whole, f32),
            vmem((2, 1, rows, lw), bf16),
            vmem((2, 1, lw, bc // 2), bf16),
            vmem((lw, width), bf16),
            vmem((width, lw), bf16),
            vmem((2, 2 * size, rows), f32),
            vmem((size - 1, 2, 2 * size, rows), f32),
            DMA((groups - 1,)),
            DMA((groups - 1,)),
            DMA((2,)),
            DMA((2, 2)),
            DMA((size, 2)),
            DMA((2, 2)),
            DMA((3, per_owner)),
            DMA((3, per_owner)),
            DMA,
            DMA((size - 1,)),
            DMA((size - 1,)),
        ]
        + ring_sems(size, 2)
        + ring_sems(size, 2),
        compiler_params=comm_params(collective_id, 62),
        name="front",
    )(parts, weight, cot_parts, shard, *tables, gain)


def finish_kernel(
    size,
    groups,
    counts,
    grad_ref,
    weight_ref,
    normed_ref,
    turned_ref,
    out_ref,
    branch_grad_ref,
    tokens_ref,
    scale_ref,
    taps_ref,
    gain_ref,
    heads_ref,
    swapped_ref,
    shard_ref,
    out_full_ref,
    rows_ref,
    gathered_ref,
    pieces_ref,
    owned_ref,
    shared_out,
    small_out,
    branch_ref,
    landing,
    slots,
    first,
    parts,
    total,
    taken,
    turned,
    out_total,
    out_parts,
    out_landing,
    out_taken,
    piece,
    main,
    shared,
    shared_land,
    shared_sum,
    small,
    small_land,
    send_sem,
    recv_sem,
    part_send,
    part_recv,
    take_sem,
    out_send,
    out_recv,
    owned_send,
    owned_recv,
    owned_local,
    pair_send,
    pair_recv,
    mate_send,
    mate_recv,
    *ring_refs,
):
    me, group, pos, right, left = neighbours(size)
    mates = [(me, index) for index in others(group, groups)]
    peers = [(index, group) for index in others(me, size)]
    greet(mates + peers)
    tiles, rows, tile = slots.shape[2:]
    cols = total.shape[0]
    bf16, f32 = jnp.bfloat16, jnp.float32
    out_ring = RingGather(size, piece, pieces_ref, *ring_refs[0:3])
    main_ring = RingGather(size, main, gathered_ref, *ring_refs[3:6])
    shared_ring = RingGather(size, shared_sum, shared_out, *ring_refs[6:9])
    small_ring = RingGather(size, small, small_out, *ring_refs[9:12])
    fetch_sem, weights_taken, held, held_sem, out_turned = ring_refs[12:17]

    def target(step, way):
        shift = (pos - 1 - step + 2 * size) if way == 0 else (pos + 1 + step)
        return ring_index(shift % size, size)

    def fetch(step, way):
        slot = lax.rem(step, 2)
        return pltpu.make_async_copy(
            grad_ref.at[target(step, way), way], held.at[slot, way], held_sem.at[slot, way]
        )

    def term(step, way, at):
        return dot(held[lax.rem(step, 2), way], weight_ref[at], 1, 0)

    def hop(step, way, at, source):
        return push(
            source,
            slots.at[step, way, at],
            send_sem.at[step, way, at],
            recv_sem.at[step, way, at],
            right if way == 0 else left,
        )

    def begin(at, carry):
        for way in range(2):
            first[way, at] = term(0, way, at).astype(bf16)
            hop(0, way, at, first.at[way, at]).start()
        return carry

    for way in range(2):
        fetch(0, way).start()
    for way in range(2):
        fetch(1, way).start()
    for way in range(2):
        fetch(0, way).wait()
    lax.fori_loop(0, tiles, begin, 0)

    def mate_of(offset):
        return lax.rem(group + offset, groups)

    def send_part(offset):
        return push(
            parts.at[offset - 1],
            landing.at[offset - 1],
            part_send.at[offset - 1],
            part_recv.at[offset - 1],
            (me, mate_of(offset)),
        )

    def send_out(offset):
        return push(
            out_parts.at[mate_of(offset)],
            out_landing.at[offset - 1],
            out_send.at[offset - 1],
            out_recv.at[offset - 1],
            (me, mate_of(offset)),
        )

    def stream(count, take, use):
        for copy in take(0, 0):
            copy.start()

        def one(block, carry):
            slot = lax.rem(block, 2)

            @pl.when(block + 1 < count)
            def _():
                for copy in take(block + 1, 1 - slot):
                    copy.start()

            for copy in take(block, slot):
                copy.wait()
            use(block, slot)
            return carry

        lax.fori_loop(0, count, one, 0)

    def tokens_of(block):
        return pl.ds(pl.multiple_of(block * 2 * rows, 2 * rows), 2 * rows)

    def weight_part(offset):
        columns = pl.ds(pl.multiple_of(mate_of(offset) * tile, tile), tile)

        def take(block, slot):
            return [
                pltpu.make_async_copy(
                    normed_ref.at[block, :, :, columns], taken.at[slot], take_sem.at[slot, 0]
                ),
                pltpu.make_async_copy(
                    turned_ref.at[:, tokens_of(block)], turned.at[slot], take_sem.at[slot, 1]
                ),
            ]

        def use(block, slot):
            values = dot(turned[slot], taken[slot].reshape(2 * rows, tile), 1, 0)

            @pl.when(block == 0)
            def _():
                total[...] = values

            @pl.when(block > 0)
            def _():
                total[...] += values

        stream(size, take, use)

    def out_part(low, count):
        piece_rows = out_parts.shape[1]

        def take(block, slot):
            return [
                pltpu.make_async_copy(
                    branch_grad_ref.at[tokens_of(low + block)],
                    out_taken.at[slot],
                    take_sem.at[slot, 0],
                ),
                pltpu.make_async_copy(
                    out_ref.at[low + block], out_turned.at[slot], take_sem.at[slot, 1]
                ),
            ]

        def use(block, slot):
            values = dot(out_turned[slot], out_taken[slot], 1, 0)

            @pl.when(low + block == 0)
            def _():
                out_total[...] = values

            @pl.when(low + block > 0)
            def _():
                out_total[...] += values

        stream(count, take, use)

    def out_sends():
        piece_rows = out_parts.shape[1]
        for index in range(groups):
            out_parts[index] = out_total[index * piece_rows : (index + 1) * piece_rows].astype(bf16)
        for offset in range(1, groups):
            send_out(offset).start()

    def advance(step, carry):
        for way in range(2):
            fetch(step + 1, way).start()
        for way in range(2):
            fetch(step, way).wait()

        def one(at, inner):
            for way in range(2):
                own = term(step, way, at)
                hop(step - 1, way, at, first.at[way, at]).wait_recv()
                slots[step - 1, way, at] = (slots[step - 1, way, at].astype(f32) + own).astype(bf16)
                hop(step, way, at, slots.at[step - 1, way, at]).start()
            return inner

        lax.fori_loop(0, tiles, one, 0)

        @pl.when(step < 3)
        def _():
            out_part((step - 1) * (size // 2), size // 2)

        @pl.when(step == 2)
        def _():
            out_sends()

        @pl.when((step > 2) & (step <= groups + 2))
        def _():
            weight_part(step - 2)

        @pl.when((step > 2) & (step <= groups + 1))
        def _():
            parts[step - 3] = total[...].astype(bf16)
            send_part(step - 2).start()

        return carry

    lax.fori_loop(1, size - 1, advance, 0)
    for offset in range(1, groups):
        send_out(offset).wait_recv()
    summed = out_parts[group].astype(f32)
    for offset in range(1, groups):
        summed = summed + out_landing[offset - 1].astype(f32)
    piece[...] = summed.astype(bf16).reshape(piece.shape)
    out_ring.start()

    for way in range(2):
        fetch(size - 1, way).wait()

    def end(at, carry):
        columns = pl.ds(pl.multiple_of(at * tile, tile), tile)
        for way in range(2):
            own = term(size - 1, way, at)
            hop(size - 2, way, at, first.at[way, at]).wait_recv()
            rows_ref[way, :, columns] = slots[size - 2, way, at].astype(f32) + own
        return carry

    lax.fori_loop(0, tiles, end, 0)
    width = rows_ref.shape[2]
    own_width = gain_ref.shape[1]
    flat = jnp.zeros((1, width), f32)
    for way in range(2):
        values = tokens_ref[way].astype(f32) * scale_ref[way, :, 0:1]
        flat = flat + jnp.sum(rows_ref[way] * values, axis=0, keepdims=True)
    half = small.shape[2]
    listed = [
        taps_ref[k : k + 1, at : at + 128] for k in range(KW + 1) for at in range(0, own_width, 128)
    ]
    listed += [gain_ref[0:1, at : at + 128] for at in range(0, own_width, 128)]
    listed += [heads_ref[k : k + 1, :] for k in range(3)]
    listed += [
        taps_ref[k : k + 1, at : at + 128]
        for k in range(KW + 1)
        for at in range(own_width, taps_ref.shape[1], 128)
    ]
    listed += [flat[:, at : at + 128] for at in range(0, width, 128)]
    for at, row in enumerate(listed):
        small[at // half, 0, at % half : at % half + 1, :] = row
    small_in = [
        push(small, small_land.at[k], mate_send.at[k], mate_recv.at[k], mate)
        for k, mate in enumerate(mates)
    ]
    for copy in small_in:
        copy.start()

    def out_advance(step, carry):
        out_ring.advance(step)
        return carry

    lax.fori_loop(1, size // 2, out_advance, 0)
    fetched = []
    for offset in range(1, groups):
        send_part(offset).wait()
        fetched.append(
            pltpu.make_async_copy(
                landing.at[offset - 1], parts.at[offset - 1], fetch_sem.at[offset - 1]
            )
        )
        fetched[-1].start()
    for copy, part in zip(fetched, range(groups - 1)):
        copy.wait()
        total[...] += parts[part].astype(f32)
    main[...] = total[: counts[0]].astype(bf16).reshape(main.shape)
    shared[...] = total[counts[0] : counts[0] + counts[1]].astype(bf16).reshape(shared.shape)
    shared_in = [
        push(shared.at[peer[0]], shared_land.at[k], pair_send.at[k], pair_recv.at[k], peer)
        for k, peer in enumerate(peers)
    ]
    lax.fori_loop(size // 2, size - 1, out_advance, 0)
    for copy in shared_in:
        copy.start()
    main_ring.start()
    out_ring.finish()
    owned = [
        push(pieces_by_owner(pieces_ref, mate[1], groups), owned_ref.at[group], owned_send.at[k], owned_recv.at[k], mate)
        for k, mate in enumerate(mates)
    ]
    kept = pltpu.make_async_copy(
        pieces_by_owner(pieces_ref, group, groups), owned_ref.at[group], owned_local
    )
    for copy in owned:
        copy.start()
    kept.start()
    main_ring.advance(1)
    for copy in small_in + shared_in:
        copy.wait()
    values = small[...]
    for k in range(groups - 1):
        values = values + small_land[k]
    small[...] = values
    values = shared[me].astype(f32)
    for k in range(size - 1):
        values = values + shared_land[k].astype(f32)
    shared_rows = values.shape[0]
    own_rows = shared_sum.shape[0] * shared_sum.shape[2] - shared_rows
    tail = jnp.concatenate([values, total[counts[0] + counts[1] :][:own_rows]]).astype(bf16)
    shared_sum[...] = tail.reshape(shared_sum.shape)
    small_ring.start()
    shared_ring.start()
    branch_ref[...] = jnp.zeros_like(branch_ref)

    per_owner = size // groups

    def weight_take(block, slot):
        owner, at = block // per_owner, lax.rem(block, per_owner)

        @pl.when(owner == group)
        def _():
            pltpu.make_async_copy(
                shard_ref.at[at], weights_taken.at[slot], take_sem.at[slot, 0]
            ).start()

        @pl.when(owner != group)
        def _():
            pltpu.make_async_copy(
                out_full_ref.at[owner, at], weights_taken.at[slot], take_sem.at[slot, 0]
            ).start()

    def multiply(block, carry):
        slot = lax.rem(block, 2)

        @pl.when(block + 1 < size)
        def _():
            weight_take(block + 1, 1 - slot)

        pltpu.make_async_copy(
            shard_ref.at[0], weights_taken.at[slot], take_sem.at[slot, 0]
        ).wait()
        branch_ref[...] += dot(swapped_ref[block], weights_taken[slot], 1, 0)
        return carry

    weight_take(0, 0)
    count = size - 3

    def main_advance(step, carry):
        main_ring.advance(step)
        small_ring.advance(step - 1)
        shared_ring.advance(step - 1)
        lax.fori_loop(((step - 2) * size) // count, ((step - 1) * size) // count, multiply, 0)
        return carry

    lax.fori_loop(2, size - 1, main_advance, 0)
    small_ring.advance(size - 2)
    shared_ring.advance(size - 2)

    def drain(step, carry):
        def one(at, inner):
            for way in range(2):
                hop(step, way, at, first.at[way, at]).wait_send()
            return inner

        return lax.fori_loop(0, tiles, one, carry)

    lax.fori_loop(0, size - 1, drain, 0)
    for offset in range(1, groups):
        send_out(offset).wait_send()
    main_ring.finish()
    small_ring.finish()
    shared_ring.finish()
    for copy in owned:
        copy.wait()
    kept.wait()


def pieces_by_owner(pieces_ref, owner, groups):
    count = pieces_ref.shape[0] // groups
    return pieces_ref.at[pl.ds(owner * count, count)]


def finish(
    grad,
    weight,
    normed,
    turned,
    out,
    branch_grad,
    tokens,
    scale,
    taps,
    gain,
    heads,
    swapped,
    shard,
    out_full,
    counts,
    collective_id,
):
    size, groups = lax.axis_size("seq"), lax.axis_size("wa")
    _, ways, rows, cols = grad.shape
    tile, tiles = weight.shape[2], groups
    width = tiles * tile
    lw = out.shape[1]
    bc = taps.shape[1] - lw
    piece_rows = lw // groups
    per_owner = size // groups
    bf16, f32, DMA = jnp.bfloat16, jnp.float32, pltpu.SemaphoreType.DMA
    total_small = ((KW + 2) * lw + (KW + 1) * bc + width) // 128 + 3
    half = -(-total_small // 16) * 8
    piece = (2, 1, piece_rows // 2, width)
    main = (2, 2, counts[0] // 4, tile)
    shared_rows = counts[1] // size
    both = (2, 1, (shared_rows + counts[2]) // 2, tile)
    small_shape = (2, 1, half, 128)
    vmem = pltpu.VMEM
    return pl.pallas_call(
        functools.partial(finish_kernel, size, groups, counts),
        out_shape=[
            jax.ShapeDtypeStruct((ways, rows, width), f32),
            jax.ShapeDtypeStruct((size,) + main, bf16),
            jax.ShapeDtypeStruct((size,) + piece, bf16),
            jax.ShapeDtypeStruct((groups, per_owner) + piece, bf16),
            jax.ShapeDtypeStruct((size,) + both, bf16),
            jax.ShapeDtypeStruct((size,) + small_shape, f32),
            jax.ShapeDtypeStruct((ways * rows, width), f32),
            jax.ShapeDtypeStruct((groups - 1, cols, tile), bf16),
        ],
        in_specs=[ANY, VMEM, ANY, ANY, ANY, ANY] + [VMEM] * 6 + [ANY, ANY],
        out_specs=[VMEM, ANY, ANY, ANY, ANY, ANY, VMEM, ANY],
        scratch_shapes=[
            vmem((size - 1, 2, tiles, rows, tile), bf16),
            vmem((2, tiles, rows, tile), bf16),
            vmem((groups - 1, cols, tile), bf16),
            vmem((cols, tile), f32),
            vmem((2, ways, rows, tile), bf16),
            vmem((2, cols, 2 * rows), bf16),
            vmem((lw, width), f32),
            vmem((groups, piece_rows, width), bf16),
            vmem((groups - 1, piece_rows, width), bf16),
            vmem((2, 2 * rows, width), bf16),
            vmem(piece, bf16),
            vmem(main, bf16),
            vmem((size, shared_rows, tile), bf16),
            vmem((size - 1, shared_rows, tile), bf16),
            vmem(both, bf16),
            vmem(small_shape, f32),
            vmem((groups - 1,) + small_shape, f32),
            DMA((size - 1, 2, tiles)),
            DMA((size - 1, 2, tiles)),
            DMA((groups - 1,)),
            DMA((groups - 1,)),
            DMA((2, 2)),
            DMA((groups - 1,)),
            DMA((groups - 1,)),
            DMA((groups - 1,)),
            DMA((groups - 1,)),
            DMA,
            DMA((size - 1,)),
            DMA((size - 1,)),
            DMA((groups - 1,)),
            DMA((groups - 1,)),
        ]
        + ring_sems(size, 1)
        + ring_sems(size, 2)
        + ring_sems(size, 1)
        + ring_sems(size, 1)
        + [DMA((groups - 1,)), vmem((2, lw, width), bf16)]
        + [vmem((2, 2, rows, cols), bf16), DMA((2, 2)), vmem((2, lw, 2 * rows), bf16)],
        compiler_params=comm_params(collective_id, 63),
        name="finish",
    )(
        grad,
        weight,
        normed,
        turned,
        out,
        branch_grad,
        tokens,
        scale,
        taps,
        gain,
        heads,
        swapped,
        shard,
        out_full,
    )


def assemble_kernel(blocks, gathered_ref, tail_ref, o_ref):
    @pl.when(pl.program_id(0) < blocks)
    def _():
        o_ref[...] = gathered_ref[0, 0].reshape(o_ref.shape).astype(jnp.float32)

    @pl.when(pl.program_id(0) == blocks)
    def _():
        o_ref[...] = tail_ref[...].astype(jnp.float32)


def assemble_in(gathered, tail):
    size, ways, chunks, rows, width = gathered.shape
    step = chunks * rows
    blocks = size * ways
    total = blocks * step + tail.shape[0]
    steps = blocks + 1
    pad = -tail.shape[0] % step
    if tail.shape[0] > step:
        out = jnp.swapaxes(gathered, 0, 1).reshape(blocks * step, width)
        return jnp.concatenate([out, tail]).astype(jnp.float32)
    return pl.pallas_call(
        functools.partial(assemble_kernel, blocks),
        grid=(steps,),
        in_specs=[
            pl.BlockSpec(
                (1, 1, chunks, rows, width),
                lambda i: (lax.rem(i, size), jnp.minimum(i // size, ways - 1), 0, 0, 0),
            ),
            pl.BlockSpec((step, width), lambda i: (0, 0)),
        ],
        out_specs=pl.BlockSpec((step, width), lambda i: (i, 0)),
        out_shape=jax.ShapeDtypeStruct((total, width), jnp.float32),
        compiler_params=pltpu.CompilerParams(vmem_limit_bytes=32 * 2**20),
        name="assemble_in",
    )(gathered, jnp.pad(tail, ((0, pad), (0, 0))))


def widen_kernel(x_ref, o_ref):
    o_ref[...] = x_ref[0, 0].astype(jnp.float32)


def assemble_out(owned):
    groups, count, rows, width = owned.shape
    return pl.pallas_call(
        widen_kernel,
        grid=(count, groups),
        in_specs=[pl.BlockSpec((1, 1, rows, width), lambda t, g: (g, t, 0, 0))],
        out_specs=pl.BlockSpec((rows, width), lambda t, g: (t * groups + g, 0)),
        out_shape=jax.ShapeDtypeStruct((groups * count * rows, width), jnp.float32),
        name="assemble_out",
    )(owned)


def body(
    tokens,
    lengths,
    norm_gain,
    in_weight,
    conv_weight,
    conv_bias,
    dt_bias,
    a_log,
    skip_gain,
    out_gain,
    out_weight,
    cotangent,
):
    seqs_here, slot_rows, width = tokens.shape
    row_count = seqs_here * slot_rows
    inner_width = out_gain.shape[0]
    channels = conv_bias.shape[0]
    bc_width = channels - inner_width
    state_size = bc_width // 2
    head_count = dt_bias.shape[0]
    head_size = inner_width // head_count
    seq_devices = lax.axis_size("seq")
    group_devices = lax.axis_size("wa")
    seq_index = lax.axis_index("seq")
    length = seq_devices * slot_rows
    local_heads = head_count // seq_devices
    local_width = local_heads * head_size
    channel_start = seq_index * local_width
    head_start = seq_index * local_heads
    bf16, f32 = jnp.bfloat16, jnp.float32

    def take(array, start, size, axis):
        return lax.dynamic_slice_in_dim(array, start, size, axis)

    positions = seq_index * slot_rows + jnp.arange(slot_rows)
    valid_rows = (positions[None, :] < lengths[:, None]).astype(f32).reshape(row_count, 1)
    flat_tokens = tokens.reshape(row_count, width).astype(f32)
    in_scale = row_scale(flat_tokens)
    normed = (flat_tokens * in_scale * norm_gain).astype(bf16)
    cot_rows = cotangent.reshape(row_count, width)

    in_turned = in_weight.T
    local_columns = jnp.concatenate(
        [
            take(in_turned, channel_start, local_width, 0),
            take(in_turned, inner_width + channel_start, local_width, 0),
            in_turned[2 * inner_width : 2 * inner_width + bc_width],
            take(in_turned, 2 * inner_width + bc_width + head_start, local_heads, 0),
            jnp.zeros((128 - local_heads, in_weight.shape[0]), bf16),
        ]
    )
    columns_here = local_columns.shape[0]
    blocks = (seq_devices, seqs_here, slot_rows)
    def lanes(part):
        return jnp.pad(part[None], ((0, 7), (0, 128 - local_heads)))

    taps = jnp.pad(
        jnp.concatenate(
            [take(conv_weight, channel_start, local_width, 1), conv_weight[:, inner_width:]], axis=1
        ),
        ((0, 8 - KW), (0, 0)),
    )
    shift = jnp.concatenate(
        [take(conv_bias, channel_start, local_width, 0), conv_bias[inner_width:]]
    )[None]
    bias = lanes(take(dt_bias, head_start, local_heads, 0))
    slope = lanes(-jnp.exp(take(a_log, head_start, local_heads, 0)))
    skip = jnp.repeat(take(skip_gain, head_start, local_heads, 0), head_size)[None]
    gain_local = take(out_gain, channel_start, local_width, 0)
    spread, fold, tri, upper = scan_tables(slot_rows, local_width, head_size)
    widths = (local_width, bc_width)
    per_owner = seq_devices // group_devices
    (
        normed_all,
        in_columns,
        projected,
        y_heads,
        entering,
        normed_out,
        turned_out,
        gated_grad,
        gain_sum,
        branch_grad,
        out_full,
    ) = front(
        normed,
        local_columns,
        cot_rows * valid_rows.astype(bf16),
        out_weight.reshape(per_owner, local_width, width),
        (taps, shift, bias, slope, skip, spread, tri),
        gain_local[None],
        inner_width,
        widths,
        head_size,
        0,
    )
    normed_out = normed_out.reshape(-1, local_width)
    branch_grad = branch_grad.reshape(-1, width)
    swapped = lax.all_to_all(
        normed_out.reshape(seq_devices, row_count, local_width), "seq", 0, 0, tiled=True
    )
    proj_grad, turned_grad, taps_sum, _, head_sum = scan_backward(
        projected,
        y_heads,
        entering,
        gated_grad,
        taps,
        shift,
        bias,
        slope,
        skip,
        spread,
        fold,
        tri,
        upper,
        widths,
        head_size,
    )
    proj_grad = proj_grad.reshape(-1, columns_here)
    in_rows = in_weight.shape[0]
    own_rows = (KW + 2) * (local_width // 128)
    packed_rows = own_rows + 3 + ((KW + 1) * bc_width + width) // 128
    shared_rows = bc_width // seq_devices
    normed_grad, gathered, _, owned, shared_all, small_all, branch, _ = finish(
        proj_grad.reshape(blocks + (columns_here,)),
        in_columns,
        normed_all.reshape(blocks + (width,)),
        turned_grad,
        turned_out,
        branch_grad,
        tokens,
        jnp.broadcast_to(in_scale.reshape(seqs_here, slot_rows, 1), (seqs_here, slot_rows, 128)),
        taps_sum,
        gain_sum,
        head_sum,
        swapped,
        out_weight.reshape(per_owner, local_width, width),
        out_full,
        (2 * local_width, bc_width, 16),
        2,
    )
    normed_grad = normed_grad.reshape(row_count, width)
    token_grad = norm_backward(flat_tokens, in_scale, norm_gain, normed_grad)
    token_grad = token_grad + cot_rows.astype(f32)
    owned = owned.reshape(
        group_devices, per_owner, local_width // group_devices, width
    )
    shared_all = shared_all.reshape(seq_devices, shared_rows + 16, in_rows)
    small_all = small_all.reshape(seq_devices, -1, 128)
    mixed_out = (flat_tokens + valid_rows * branch).astype(bf16).reshape(tokens.shape)
    tail = jnp.concatenate(
        [
            shared_all[:, :shared_rows].reshape(bc_width, in_rows),
            shared_all[:, shared_rows : shared_rows + local_heads].reshape(head_count, in_rows),
        ]
    )
    in_weight_grad = assemble_in(gathered, tail).T
    out_weight_grad = assemble_out(owned)

    own_all = small_all[:, :own_rows].reshape(seq_devices, KW + 2, local_width)
    own_all = jnp.swapaxes(own_all, 0, 1).reshape(KW + 2, inner_width)
    head_all = jnp.swapaxes(small_all[:, own_rows : own_rows + 3, :local_heads], 0, 1)
    head_all = head_all.reshape(3, head_count)
    summed = jnp.sum(small_all[:, own_rows + 3 : packed_rows], axis=0).reshape(-1)
    conv_weight_grad = jnp.concatenate(
        [own_all[:KW], summed[: KW * bc_width].reshape(KW, bc_width)], axis=1
    )
    conv_bias_grad = jnp.concatenate(
        [own_all[KW], summed[KW * bc_width : (KW + 1) * bc_width]]
    )
    norm_gain_total = summed[(KW + 1) * bc_width :]
    return (
        mixed_out,
        token_grad.reshape(tokens.shape),
        norm_gain_total,
        in_weight_grad,
        conv_weight_grad,
        conv_bias_grad,
        head_all[0],
        head_all[1],
        head_all[2],
        own_all[KW + 1],
        out_weight_grad,
    )


def solution(mesh):
    placed = (
        P("wa", "seq", None),
        P("wa"),
        P(),
        P("wa", None),
        P(),
        P(),
        P(),
        P(),
        P(),
        P(),
        P("wa", None),
        P("wa", "seq", None),
    )
    return jax.shard_map(
        body,
        mesh=mesh,
        in_specs=placed,
        out_specs=(
            P("wa", "seq", None),
            P("wa", "seq", None),
            P(),
            P("wa", None),
            P(),
            P(),
            P(),
            P(),
            P(),
            P(),
            P("wa", None),
        ),
        check_vma=False,
    )
```

time: 644 us -> 552 us (0.86)
  matrix products: 69.6 us -> 0 us
  Pallas kernels: 480 us -> 499 us
  local copies, waits for them, and re-layouts: 44.1 us -> 30.3 us
  between operations: 14.3 us -> 0.95 us
  other arithmetic: 25.6 us -> 13.4 us
    dot_general x5 -> x0, matrix products: 69.6 us -> none  [the longest x1 19.2 us: body(): lax.dot_general(normed_all, proj_grad, (((0,), (0,)), ((), ())), preferre...]
    unnamed x45 -> x59, local copies, waits for them, and re-layouts: 31.3 us -> 13 us
    pallas_call x7 -> x3, Pallas kernels: 431 us -> 447 us  [the longest x1 246 us: finish(): pl.pallas_call(functools.partial(finish_kernel, size, groups, counts), ou...]
    reduce_sum x5 -> x1, other arithmetic: 8.79 us -> 0.36 us  [norm_backward(): jnp.mean(weighted * values, axis=-1, keepdims=True)]
  transfers between devices with their start and end apart: 4 -> 1, of which waited for: 1 -> 1; matrix products, arithmetic and copies ran while one was open for 10% -> 0% of each run, Pallas kernels for 35% -> 8%
where the time goes in v4:
time: 552 us; the launch traced here: 549 us
  Pallas kernels  499 us (90%)
  local copies, waits for them, and re-layouts  30.3 us (5%)
  other arithmetic  13.4 us (2%)
    pallas_call x1, Pallas kernels, finish(): pl.pallas_call(functools.partial(finish_kernel, size, groups, counts), ou...  246 us
    pallas_call x1, Pallas kernels, front(): pl.pallas_call(functools.partial(front_kernel, widths, head_size, size, g...  192 us
    pallas_call x1, Pallas kernels, scan_backward(): pl.pallas_call(functools.partial(backward_kernel, widths, head_size, chun...  44.3 us
    unnamed x59, local copies, waits for them, and re-layouts  13 us
  transfers between devices with their start and end apart: 1, of which 1 were waited for; matrix products, arithmetic and copies ran while one was open for 0% of the time, Pallas kernels for 8%

profile of v4, /device:TPU:0, one launch (start us, length us, event | category | flops | bytes accessed | tf_op | source)
XLA Modules:
  0.0 549.3 jit_solution(12259200760052907463)
XLA Ops:
  2.9 1.9 bitcast_dynamic-update-slice_fusion.1
  4.8 1.9 bitcast_dynamic-update-slice_fusion
  6.7 1.7 slice_dynamic-update-slice_fusion
  8.3 1.3 constant_dynamic-update-slice_fusion
  15.2 1.3 dynamic_slice.35
  16.7 1.1 broadcast_multiply_fusion.cot_ref
  17.8 1.3 multiply_convert_fusion.x_ref
  19.0 191.9 %front.1 = (bf16[8,2,2,64,2048]{4,3,2,1,0:T(8,128)(2,1)}, bf16[4,1408,512]{2,1,0:T(8,128)(2,1)}, bf16[8,2,128,1408]{3,2,1,0:T(8,128)(2,1)}, bf16[8,2,128,512]{3,...) custom-call(bf16[2,2,64,2048]{3,2,1,0:T(8,128)(2,1)} %multiply_conve, ...), custom_call_target="tpu_custom_call" | custom-call | tf_op jit(solution)/shard_map/front/pallas_call | solution.py:783
  211.1 4.8 all-to-all-start
  216.1 1.6 copy-done.2
  217.7 44.3 %scan_backward.1 = (bf16[8,2,128,1408]{3,2,1,0:T(8,128)(2,1)}, bf16[1408,2048]{1,0:T(8,128)(2,1)}, f32[8,768]{1,0:T(8,128)S(1)}, f32[8,512]{1,0:T(8,128)}, f32[8,128]{1,0:T(8,128)S(1)}) custom-call(bf16[8,2,128,1408]{3,2,1,0:T(8,128)(2,1)} %get-tuple-element.32.proj_ref.before_ref, bf16[8,2,128,1408]{3,2,1,0:T(8,128)(2,1)} %get-tuple-element.32.proj_ref.before_ref, ...), custom_call_target="tpu_custom_call" | custom-call | tf_op jit(solution)/shard_map/scan_backward/pallas_call | solution.py:311
  265.3 246.3 %finish.1 = (f32[2,128,2048]{2,1,0:T(8,128)}, bf16[8,2,2,256,512]{4,3,2,1,0:T(8,128)(2,1)}, bf16[8,2,1,64,2048]{4,3,2,1,0:T(8,128)(2,1)}, bf16[4,2,2,1,64,2048]{...) custom-call(bf16[8,2,128,1408]{3,2,1,0:T(8,128)(2,1)} %get-tuple-ele, ...), custom_call_target="tpu_custom_call" | custom-call | tf_op jit(solution)/shard_map/finish/pallas_call | solution.py:1288
  512.5 0.9 slice_reduce_fusion
  514.7 1.0 slice.89
  516.5 1.4 slice.96
  518.5 7.4 %assemble_out.1 = f32[1024,2048]{1,0:T(8,128)} custom-call(bf16[4,2,128,2048]{3,2,1,0:T(8,128)(2,1)} %bitcast.50), custom_call_target="tpu_custom_call" | custom-call | tf_op jit(solution)/shard_map/assemble_out/pallas_call | solution.py:1404
  527.5 1.3 squeeze.16
  528.8 1.3 squeeze.17
  530.1 1.3 squeeze.18
  531.3 1.3 pad_maximum_fusion.1
  533.4 3.4 copy-done
  536.7 9.3 %assemble_in.1 = f32[8512,512]{1,0:T(8,128)} custom-call(bf16[8,2,2,256,512]{4,3,2,1,0:T(8,128)(2,1)S(1)} %copy-done, bf16[512,512]{1,0:T(8,128)(2,1)S(1)} %fusion.3.tail_ref), custom_call_target="tpu_custom_call" | custom-call | tf_op jit(solution)/shard_map/assemble_in/pallas_call | solution.py:1381
  546.0 2.0 convert_add_fusion
  548.0 1.3 fusion
  (96 shorter events, 17.3 us)
Async XLA Ops:
  0.6 9.7 %slice-start.1 = ((f32[4352]{0:T(1024)}), f32[256]{0:T(256)S(1)}, s32[]{:S(2)}) async-start(f32[4352]{0:T(1024)} %param.17), calls=%async_computation.2 | async-start | bytes 2048 | tf_op jit(solution)/shard_map/slice | solution.py:1478
  0.7 10.2 %copy-start.25 = (f32[64]{0:T(128)S(1)}, f32[64]{0:T(128)}, u32[]{:S(2)}) copy-start(f32[64]{0:T(128)} %param.18) | copy-start | bytes 772
  0.7 10.2 %copy-start.24 = (f32[64]{0:T(128)S(1)}, f32[64]{0:T(128)}, u32[]{:S(2)}) copy-start(f32[64]{0:T(128)} %param.19) | copy-start | bytes 772
  0.7 11.5 %copy-start.26 = (f32[64]{0:T(128)S(1)}, f32[64]{0:T(128)}, u32[]{:S(2)}) copy-start(f32[64]{0:T(128)} %param.20) | copy-start | bytes 772
  0.7 12.3 %copy-start.12 = (bf16[2,128,2048]{2,1,0:T(8,128)(2,1)S(1)}, bf16[2,128,2048]{2,1,0:T(8,128)(2,1)}, u32[]{:S(2)}) copy-start(bf16[2,128,2048]{2,1,0:T(8,128)(2,1)} %tokens_ref.1) | copy-start | bytes 3145732
  0.7 13.9 %slice-start = ((f32[4,4352]{1,0:T(4,128)}), f32[4,256]{1,0:T(4,128)S(1)}, s32[]{:S(2)}) async-start(f32[4,4352]{1,0:T(4,128)} %param.16), calls=%async_computation.1 | async-start | bytes 8192 | tf_op jit(solution)/shard_map/slice | solution.py:1473
  2.3 14.3 %copy-start.23 = (s32[2]{0:T(128)S(1)}, s32[2]{0:T(128)}, u32[]{:S(2)}) copy-start(s32[2]{0:T(128)} %param.13) | copy-start | bytes 28
  2.3 14.4 %copy-start.15 = (bf16[2,128,2048]{2,1,0:T(8,128)(2,1)S(1)}, bf16[2,128,2048]{2,1,0:T(8,128)(2,1)}, u32[]{:S(2)}) copy-start(bf16[2,128,2048]{2,1,0:T(8,128)(2,1)} %param.23) | copy-start | bytes 3145732
  6.7 11.1 %copy-start.18 = (f32[2048]{0:T(1024)S(1)}, f32[2048]{0:T(1024)}, u32[]{:S(2)}) copy-start(f32[2048]{0:T(1024)} %param.14) | copy-start | bytes 24580
  211.0 5.0 copy-start.1
  211.0 5.0 copy-start.3
  211.0 5.0 copy-start.4
  211.0 5.0 copy-start.5
  211.0 5.0 copy-start.6
  211.0 5.0 copy-start.7
  211.0 5.0 copy-start.8
  211.0 5.0 copy-start.10
  211.1 53.5 %all-to-all-start = ((bf16[8,256,512]{2,1,0:T(8,128)(2,1)}), bf16[8,256,512]{2,1,0:T(8,128)(2,1)}, u32[]{:S(2)}, u32[]{:S(2)}) async-start(bf16[8,256,512]{2,1,0:T(8,128)(2,1)} %bitcast.52), calls=%async_computation | async-start | bytes 4194304 | tf_op jit(solution)/shard_map/all_to_all | solution.py:1513
  518.5 7.5 %copy-start.13 = (bf16[2,128,2048]{2,1,0:T(8,128)(2,1)S(1)}, bf16[2,128,2048]{2,1,0:T(8,128)(2,1)}, u32[]{:S(2)}) copy-start(bf16[2,128,2048]{2,1,0:T(8,128)(2,1)} %tokens_ref.1) | copy-start | bytes 3145732
  518.5 7.5 %copy-start.14 = (f32[2,128,2048]{2,1,0:T(8,128)S(1)}, f32[2,128,2048]{2,1,0:T(8,128)}, u32[]{:S(2)}) copy-start(f32[2,128,2048]{2,1,0:T(8,128)} %get-tuple-element.48) | copy-start | bytes 6291460
  533.4 3.4 copy-start
  536.7 9.3 %copy-start.16 = (bf16[2,128,2048]{2,1,0:T(8,128)(2,1)S(1)}, bf16[2,128,2048]{2,1,0:T(8,128)(2,1)}, u32[]{:S(2)}) copy-start(bf16[2,128,2048]{2,1,0:T(8,128)(2,1)} %param.23) | copy-start | bytes 3145732
  536.7 9.3 %copy-start.20 = (f32[2,128]{1,0:T(2,128)S(1)}, f32[2,128]{1,0:T(2,128)}, u32[]{:S(2)}) copy-start(f32[2,128]{1,0:T(2,128)} %get-tuple-element.58) | copy-start | bytes 3076
  536.7 9.3 %copy-start.22 = (f32[2,128]{1,0:T(2,128)S(1)}, f32[2,128]{1,0:T(2,128)}, u32[]{:S(2)}) copy-start(f32[2,128]{1,0:T(2,128)} %broadcast_multiply_fusion.1) | copy-start | bytes 3076
  (6 other events, 7.8 us)

commit v5 on v4

--- a/solution.py
+++ b/solution.py
@@ -2,6 +2,7 @@
 
 import jax
 import jax.numpy as jnp
+import numpy as np
 from jax import lax
 from jax.experimental import pallas as pl
 from jax.experimental.pallas import tpu as pltpu
@@ -30,18 +31,19 @@
     )
 
 
-def chunk_front(proj_ref, ext, taps_ref, shift_ref, bias_ref, slope_ref, tri_ref, widths):
+def chunk_front(proj_ref, ext, taps_ref, heads_ref, tri_ref, widths, head_start):
     lw, bc = widths
     rows = proj_ref.shape[2]
     ext[8:, :] = proj_ref[0, 0, :, lw : 2 * lw + bc].astype(jnp.float32)
-    conv = shift_ref[0:1, :]
+    conv = taps_ref[KW : KW + 1, :]
     for k in range(KW):
         conv = conv + taps_ref[k : k + 1, :] * ext[5 + k : 5 + k + rows, :]
     conv_sig = lax.logistic(conv)
     act = conv * conv_sig
-    step_in = proj_ref[0, 0, :, 2 * lw + bc :].astype(jnp.float32) + bias_ref[0:1, :]
+    raw = proj_ref[0, 0, :, 2 * lw + bc :].astype(jnp.float32)
+    step_in = pltpu.roll(raw, lax.rem(128 - head_start, 128), 1) + heads_ref[0:1, :]
     steps = jnp.maximum(step_in, 0.0) + jnp.log1p(jnp.exp(-jnp.abs(step_in)))
-    rates = slope_ref[0:1, :] * steps
+    rates = heads_ref[1:2, :] * steps
     cum = dot(tri_ref[...], rates, 1, 0, HIGHEST)
     return conv, conv_sig, act, step_in, steps, rates, cum
 
@@ -56,13 +58,12 @@
 def forward_chunk(
     widths,
     head_size,
+    head_start,
     start,
     proj_ref,
     taps_ref,
-    shift_ref,
-    bias_ref,
-    slope_ref,
-    skip_ref,
+    heads_ref,
+    wide_ref,
     spread_ref,
     tri_ref,
     gated_ref,
@@ -84,7 +85,7 @@
 
     ext[0:8, :] = halo[...]
     _, _, act, _, steps, _, cum = chunk_front(
-        proj_ref, ext, taps_ref, shift_ref, bias_ref, slope_ref, tri_ref, widths
+        proj_ref, ext, taps_ref, heads_ref, tri_ref, widths, head_start
     )
     halo[...] = ext[rows : rows + 8, :]
     x = act[:, :lw]
@@ -98,7 +99,7 @@
     scores = dot(c_rows, b_rows, 1, 1)
     entering = state[...].astype(bf16)
     enter_ref[0, 0] = entering
-    y = dot(c_rows, entering, 1, 1) * grow + skip_ref[0:1, :] * x
+    y = dot(c_rows, entering, 1, 1) * grow + wide_ref[1:2, :] * x
     added = dot((x * tail).astype(bf16), b_rows, 0, 0)
     lane, causal = head_masks(rows, head_size)
     gate = proj_ref[0, 0, :, :lw].astype(f32)
@@ -132,10 +133,8 @@
     enter_ref,
     grad_ref,
     taps_ref,
-    shift_ref,
-    bias_ref,
-    slope_ref,
-    skip_ref,
+    heads_ref,
+    wide_ref,
     spread_ref,
     fold_ref,
     tri_ref,
@@ -156,6 +155,7 @@
     rows = proj_ref.shape[2]
     per_tile = 128 // head_size
     chunk = chunks - 1 - pl.program_id(1)
+    head_start = lax.axis_index("seq") * (lw // head_size)
 
     @pl.when((pl.program_id(0) == 0) & (pl.program_id(1) == 0))
     def _():
@@ -172,7 +172,7 @@
         chunk > 0, before_ref[0, 0, 8:16, lw : 2 * lw + bc].astype(f32), 0.0
     )
     conv, conv_sig, act, step_in, steps, rates, cum = chunk_front(
-        proj_ref, ext, taps_ref, shift_ref, bias_ref, slope_ref, tri_ref, widths
+        proj_ref, ext, taps_ref, heads_ref, tri_ref, widths, head_start
     )
     x = act[:, :lw]
     xb = x.astype(bf16)
@@ -205,7 +205,7 @@
     from_lam = dot(b_rows, lam_b, 1, 1)
     b_grad = dot((x * tail).astype(bf16), lam_b, 1, 0)
     x_lam = dot((x * from_lam).astype(bf16), fold_ref[...], 1, 0)
-    x_grad = skip_ref[0:1, :] * y_grad + tail * from_lam
+    x_grad = wide_ref[1:2, :] * y_grad + tail * from_lam
     skip_acc[0:1, :] += jnp.sum(y_grad * x, axis=0, keepdims=True)
     ones = jnp.ones((8, state_size), bf16)
     kept = dot(
@@ -256,9 +256,9 @@
         + dot(1.0 - upper_ref[...], tail_heads * x_lam, 1, 0, HIGHEST)
         + through
     )
-    steps_grad = col_sum + to_end * x_lam + rates_grad * slope_ref[0:1, :]
+    steps_grad = col_sum + to_end * x_lam + rates_grad * heads_ref[1:2, :]
     raw_grad = steps_grad * lax.logistic(step_in)
-    out_ref[0, 0, :, 2 * lw + bc :] = raw_grad.astype(bf16)
+    out_ref[0, 0, :, 2 * lw + bc :] = pltpu.roll(raw_grad, head_start, 1).astype(bf16)
     head_acc[0:1, :] += jnp.sum(raw_grad, axis=0, keepdims=True)
     head_acc[1:2, :] += jnp.sum(rates_grad * rates, axis=0, keepdims=True)
     score_b = score_grad.astype(bf16)
@@ -290,14 +290,14 @@
 
 
 def scan_tables(rows, local_width, head_size):
-    head_of = jnp.arange(local_width) // head_size
-    spread = (jnp.arange(128)[:, None] == head_of[None, :]).astype(jnp.bfloat16)
-    tri = (jnp.arange(rows)[:, None] >= jnp.arange(rows)[None, :]).astype(jnp.float32)
-    return spread, spread.T, tri, tri.T
+    head_of = np.arange(local_width) // head_size
+    spread = (np.arange(128)[:, None] == head_of[None, :]).astype(jnp.bfloat16)
+    tri = (np.arange(rows)[:, None] >= np.arange(rows)[None, :]).astype(np.float32)
+    return [jnp.asarray(t) for t in (spread, spread.T.copy(), tri, tri.T.copy())]
 
 
 def scan_backward(
-    proj, y, enter, grad, taps, shift, bias, slope, skip, spread, fold, tri, upper, widths, head_size
+    proj, y, enter, grad, taps, heads, wide, spread, fold, tri, upper, widths, head_size
 ):
     chunks, seqs, rows, cols = proj.shape
     lw, bc = widths
@@ -306,7 +306,7 @@
         (1, 1, 16, cols),
         lambda q, c: (jnp.maximum(chunks - 2 - c, 0), q, rows // 16 - 1, 0),
     )
-    tables = (taps, shift, bias, slope, skip, spread, fold, tri, upper)
+    tables = (taps, heads, wide, spread, fold, tri, upper)
     sums = [(8, lw + bc), (8, lw), (8, 128)]
     return pl.pallas_call(
         functools.partial(backward_kernel, widths, head_size, chunks),
@@ -461,14 +461,12 @@
     w_ref,
     cot_ref,
     shard_ref,
-    taps_ref,
-    shift_ref,
-    bias_ref,
-    slope_ref,
-    skip_ref,
+    conv_ref,
+    conv_bias_ref,
+    params_ref,
+    out_gain_ref,
     spread_ref,
     tri_ref,
-    gain_ref,
     rows_ref,
     weights_ref,
     proj_ref,
@@ -478,6 +476,9 @@
     turned_ref,
     grad_ref,
     gain_acc,
+    taps_ref,
+    heads_ref,
+    wide_ref,
     branch_ref,
     part_ref,
     weights,
@@ -522,14 +523,54 @@
     ring = RingGather(size, x_ref, rows_ref, *ring_refs[0:3])
     cot_ring = RingGather(size, cot_ref, branch_ref, *ring_refs[3:6])
     ring.start()
+    bc = widths[1]
+    used = w_ref.shape[0] - 2 * inner
+    lane_at = pl.multiple_of(me * lw, 128)
+    spans = (
+        (pl.ds(lane_at, lw), pl.ds(0, lw)),
+        (pl.ds(pl.multiple_of(inner + me * lw, 128), lw), pl.ds(lw, lw)),
+        (pl.ds(2 * inner, used), pl.ds(2 * lw, used)),
+    )
     sent = [
-        push(w_ref, weights.at[group], weight_send.at[k], weight_recv.at[k], mate)
+        push(
+            w_ref.at[here],
+            weights.at[group, there],
+            weight_send.at[k, part],
+            weight_recv.at[k, part],
+            mate,
+        )
         for k, mate in enumerate(mates)
+        for part, (here, there) in enumerate(spans)
     ]
     for copy in sent:
         copy.start()
-    kept = pltpu.make_async_copy(w_ref, weights.at[group], weight_local.at[0])
-    kept.start()
+    kept = [
+        pltpu.make_async_copy(w_ref.at[here], weights.at[group, there], weight_local.at[part])
+        for part, (here, there) in enumerate(spans)
+    ]
+    for copy in kept:
+        copy.start()
+    blank = weights.shape[1] - 2 * lw - used
+    for part in range(groups):
+        weights[part, 2 * lw + used :, :] = jnp.zeros((blank, depth), bf16)
+    heads_here = lw // head_size
+    head_start = me * heads_here
+    taps_ref[...] = jnp.zeros_like(taps_ref)
+    taps_ref[0:KW, :lw] = conv_ref[:, pl.ds(lane_at, lw)]
+    taps_ref[0:KW, lw:] = conv_ref[:, inner:]
+    taps_ref[KW : KW + 1, :lw] = conv_bias_ref[:, pl.ds(lane_at, lw)]
+    taps_ref[KW : KW + 1, lw:] = conv_bias_ref[:, inner:]
+    params = pltpu.roll(params_ref[...], lax.rem(128 - head_start, 128), 1)
+    params = jnp.where(
+        lax.broadcasted_iota(jnp.int32, params.shape, 1) < heads_here, params, 0.0
+    )
+    at_row = lax.broadcasted_iota(jnp.int32, params.shape, 0)
+    at_lane = lax.broadcasted_iota(jnp.int32, params.shape, 1)
+    slopes = jnp.where(at_lane < heads_here, -jnp.exp(params), 0.0)
+    heads_ref[...] = jnp.where(at_row == 1, slopes, params)
+    wide_ref[...] = jnp.zeros_like(wide_ref)
+    wide_ref[0:1, :] = out_gain_ref[:, pl.ds(lane_at, lw)]
+    wide_ref[1:2, :] = dot(params, spread_ref[...].astype(f32), 1, 0, HIGHEST)[2:3, :]
 
     def shards(step, offset=0):
         at = lax.rem(chosen + offset, per_owner)
@@ -594,10 +635,11 @@
 
     middle = size // 2 + 1
     lax.fori_loop(1, middle, advance, 0)
-    kept.wait()
+    for copy in kept:
+        copy.wait()
     for copy in sent:
         copy.wait_recv()
-    flushed = pltpu.make_async_copy(weights, weights_ref, weight_local.at[1])
+    flushed = pltpu.make_async_copy(weights, weights_ref, weight_local.at[0])
     flushed.start()
     shards(0).start()
     shards(1).start()
@@ -637,13 +679,12 @@
         forward_chunk(
             widths,
             head_size,
+            head_start,
             chunk == 0,
             projected.at[pl.ds(chunk, 1), pl.ds(seq, 1)],
             taps_ref,
-            shift_ref,
-            bias_ref,
-            slope_ref,
-            skip_ref,
+            heads_ref,
+            wide_ref,
             spread_ref,
             tri_ref,
             gated.at[chunk, seq],
@@ -694,7 +735,7 @@
             values = dot(taken[slot, way].reshape(rows, taken.shape[4]), out_turned[...], 1, 0)
             out_grad[block, way] = values
             here = gated[block, way].astype(f32)
-            weighted = values * gain_ref[0:1, :] * here
+            weighted = values * wide_ref[0:1, :] * here
             at = pl.ds(block * 2 + way, 1)
             sums[0, at, :] = dot(ones, (here * here).astype(bf16), 1, 1)[0:1, :]
             sums[1, at, :] = dot(ones, weighted.astype(bf16), 1, 1)[0:1, :]
@@ -736,10 +777,10 @@
             here = gated[block, way].astype(f32)
             values = out_grad[block, way]
             scaled = here * by
-            normed = (scaled * gain_ref[0:1, :]).astype(bf16)
+            normed = (scaled * wide_ref[0:1, :]).astype(bf16)
             normed_ref[block, way] = normed
             turned_ref[block, :, way * rows : (way + 1) * rows] = normed.T
-            grad_ref[block, way] = (values * gain_ref[0:1, :] * by - here * less).astype(bf16)
+            grad_ref[block, way] = (values * wide_ref[0:1, :] * by - here * less).astype(bf16)
             gain_acc[0:1, :] += jnp.sum(values * scaled, axis=0, keepdims=True)
         return carry
 
@@ -769,13 +810,14 @@
             shards(step, offset).wait_send()
 
 
-def front(x, weight, cot, shard, tables, gain, inner, widths, head_size, collective_id):
+def front(x, weight, cot, shard, params, inner, widths, head_size, collective_id):
     size, groups = lax.axis_size("seq"), lax.axis_size("wa")
     parts, cot_parts = ring_parts(x, 2), ring_parts(cot, 2)
-    cols, depth = weight.shape
+    depth = weight.shape[1]
     rows = x.shape[0] // 2
     width = x.shape[1]
     lw, bc = widths
+    cols = 2 * lw + bc + 128
     per_owner = size // groups
     bf16, f32, DMA, vmem = jnp.bfloat16, jnp.float32, pltpu.SemaphoreType.DMA, pltpu.VMEM
     whole = (size, 2, rows, lw)
@@ -792,11 +834,14 @@
             shape((size, lw, 2 * rows), bf16),
             shape(whole, bf16),
             shape((8, lw), f32),
+            shape((8, lw + bc), f32),
+            shape((8, 128), f32),
+            shape((8, lw), f32),
             shape((size,) + parts.shape, bf16),
             shape((groups, per_owner, lw, width), bf16),
         ],
-        in_specs=[ANY] * 4 + [VMEM] * 8,
-        out_specs=[ANY] * 5 + [VMEM] * 4 + [ANY] * 2,
+        in_specs=[ANY] * 4 + [VMEM] * 6,
+        out_specs=[ANY] * 5 + [VMEM] * 7 + [ANY] * 2,
         scratch_shapes=[
             vmem((groups, cols, depth), bf16),
             vmem((size, 2, rows, cols), bf16),
@@ -812,9 +857,9 @@
             vmem((width, lw), bf16),
             vmem((2, 2 * size, rows), f32),
             vmem((size - 1, 2, 2 * size, rows), f32),
-            DMA((groups - 1,)),
-            DMA((groups - 1,)),
-            DMA((2,)),
+            DMA((groups - 1, 3)),
+            DMA((groups - 1, 3)),
+            DMA((3,)),
             DMA((2, 2)),
             DMA((size, 2)),
             DMA((2, 2)),
@@ -828,7 +873,7 @@
         + ring_sems(size, 2),
         compiler_params=comm_params(collective_id, 62),
         name="front",
-    )(parts, weight, cot_parts, shard, *tables, gain)
+    )(parts, weight, cot_parts, shard, *params)
 
 
 def finish_kernel(
@@ -893,7 +938,6 @@
     me, group, pos, right, left = neighbours(size)
     mates = [(me, index) for index in others(group, groups)]
     peers = [(index, group) for index in others(me, size)]
-    greet(mates + peers)
     tiles, rows, tile = slots.shape[2:]
     cols = total.shape[0]
     bf16, f32 = jnp.bfloat16, jnp.float32
@@ -902,6 +946,12 @@
     shared_ring = RingGather(size, shared_sum, shared_out, *ring_refs[6:9])
     small_ring = RingGather(size, small, small_out, *ring_refs[9:12])
     fetch_sem, weights_taken, held, held_sem, out_turned = ring_refs[12:17]
+    weight_held, swapped_held, load_sem = ring_refs[17:20]
+    loads = [
+        pltpu.make_async_copy(weight_ref.at[part], weight_held.at[part], load_sem.at[part])
+        for part in range(groups)
+    ]
+    swapped_load = pltpu.make_async_copy(swapped_ref, swapped_held, load_sem.at[groups])
 
     def target(step, way):
         shift = (pos - 1 - step + 2 * size) if way == 0 else (pos + 1 + step)
@@ -914,7 +964,7 @@
         )
 
     def term(step, way, at):
-        return dot(held[lax.rem(step, 2), way], weight_ref[at], 1, 0)
+        return dot(held[lax.rem(step, 2), way], weight_held[at], 1, 0)
 
     def hop(step, way, at, source):
         return push(
@@ -933,11 +983,17 @@
 
     for way in range(2):
         fetch(0, way).start()
+    for copy in loads:
+        copy.start()
     for way in range(2):
         fetch(1, way).start()
+    swapped_load.start()
+    greet(mates + peers)
     for way in range(2):
         fetch(0, way).wait()
-    lax.fori_loop(0, tiles, begin, 0)
+    for part in range(groups):
+        loads[part].wait()
+        begin(part, 0)
 
     def mate_of(offset):
         return lax.rem(group + offset, groups)
@@ -1174,10 +1230,9 @@
     values = shared[me].astype(f32)
     for k in range(size - 1):
         values = values + shared_land[k].astype(f32)
-    shared_rows = values.shape[0]
-    own_rows = shared_sum.shape[0] * shared_sum.shape[2] - shared_rows
-    tail = jnp.concatenate([values, total[counts[0] + counts[1] :][:own_rows]]).astype(bf16)
-    shared_sum[...] = tail.reshape(shared_sum.shape)
+    across = shared_sum.shape[3]
+    for way in range(2):
+        shared_sum[way, 0] = values[:, way * across : (way + 1) * across].astype(bf16)
     small_ring.start()
     shared_ring.start()
     branch_ref[...] = jnp.zeros_like(branch_ref)
@@ -1209,10 +1264,11 @@
         pltpu.make_async_copy(
             shard_ref.at[0], weights_taken.at[slot], take_sem.at[slot, 0]
         ).wait()
-        branch_ref[...] += dot(swapped_ref[block], weights_taken[slot], 1, 0)
+        branch_ref[...] += dot(swapped_held[block], weights_taken[slot], 1, 0)
         return carry
 
     weight_take(0, 0)
+    swapped_load.wait()
     count = size - 3
 
     def main_advance(step, carry):
@@ -1279,10 +1335,10 @@
     bf16, f32, DMA = jnp.bfloat16, jnp.float32, pltpu.SemaphoreType.DMA
     total_small = ((KW + 2) * lw + (KW + 1) * bc + width) // 128 + 3
     half = -(-total_small // 16) * 8
-    piece = (2, 1, piece_rows // 2, width)
+    piece = (2, 2, piece_rows // 4, width)
     main = (2, 2, counts[0] // 4, tile)
     shared_rows = counts[1] // size
-    both = (2, 1, (shared_rows + counts[2]) // 2, tile)
+    both = (2, 1, shared_rows, tile // 2)
     small_shape = (2, 1, half, 128)
     vmem = pltpu.VMEM
     return pl.pallas_call(
@@ -1297,7 +1353,7 @@
             jax.ShapeDtypeStruct((ways * rows, width), f32),
             jax.ShapeDtypeStruct((groups - 1, cols, tile), bf16),
         ],
-        in_specs=[ANY, VMEM, ANY, ANY, ANY, ANY] + [VMEM] * 6 + [ANY, ANY],
+        in_specs=[ANY] * 6 + [VMEM] * 5 + [ANY] * 3,
         out_specs=[VMEM, ANY, ANY, ANY, ANY, ANY, VMEM, ANY],
         scratch_shapes=[
             vmem((size - 1, 2, tiles, rows, tile), bf16),
@@ -1332,12 +1388,13 @@
             DMA((groups - 1,)),
             DMA((groups - 1,)),
         ]
-        + ring_sems(size, 1)
+        + ring_sems(size, 2)
         + ring_sems(size, 2)
         + ring_sems(size, 1)
         + ring_sems(size, 1)
         + [DMA((groups - 1,)), vmem((2, lw, width), bf16)]
-        + [vmem((2, 2, rows, cols), bf16), DMA((2, 2)), vmem((2, lw, 2 * rows), bf16)],
+        + [vmem((2, 2, rows, cols), bf16), DMA((2, 2)), vmem((2, lw, 2 * rows), bf16)]
+        + [vmem(weight.shape, bf16), vmem(swapped.shape, bf16), DMA((groups + 1,))],
         compiler_params=comm_params(collective_id, 63),
         name="finish",
     )(
@@ -1395,20 +1452,68 @@
     )(gathered, jnp.pad(tail, ((0, pad), (0, 0))))
 
 
-def widen_kernel(x_ref, o_ref):
+def widen_kernel(
+    widths, heads, x_ref, small_ref, o_ref, conv_ref, bias_ref, gain_ref, heads_ref, norm_ref
+):
     o_ref[...] = x_ref[0, 0].astype(jnp.float32)
 
-
-def assemble_out(owned):
+    @pl.when((pl.program_id(0) == 0) & (pl.program_id(1) == 0))
+    def _():
+        lw, bc = widths
+        size = small_ref.shape[0]
+        tiles, shared = lw // 128, bc // 128
+        inner = size * lw
+        found = jnp.zeros((8, 128), jnp.float32)
+        first = (KW + 2) * tiles
+        for block in range(size):
+            for tile in range(tiles):
+                at = slice(block * lw + tile * 128, block * lw + (tile + 1) * 128)
+                for k in range(KW):
+                    row = k * tiles + tile
+                    conv_ref[k : k + 1, at] = small_ref[block, row : row + 1, :]
+                row = KW * tiles + tile
+                bias_ref[:, at] = small_ref[block, row : row + 1, :]
+                row = (KW + 1) * tiles + tile
+                gain_ref[:, at] = small_ref[block, row : row + 1, :]
+            found = found + pltpu.roll(small_ref[block, first : first + 8, :], block * heads, 1)
+        heads_ref[...] = found
+        total = small_ref[0]
+        for block in range(1, size):
+            total = total + small_ref[block]
+        row = first + 3
+        for k in range(KW + 1):
+            for tile in range(shared):
+                at = slice(inner + tile * 128, inner + (tile + 1) * 128)
+                if k < KW:
+                    conv_ref[k : k + 1, at] = total[row : row + 1, :]
+                else:
+                    bias_ref[:, at] = total[row : row + 1, :]
+                row += 1
+        for tile in range(norm_ref.shape[1] // 128):
+            norm_ref[:, tile * 128 : (tile + 1) * 128] = total[row : row + 1, :]
+            row += 1
+
+
+def assemble_out(owned, small, widths, heads):
     groups, count, rows, width = owned.shape
+    size = small.shape[0]
+    lw, bc = widths
+    inner = size * lw
+    f32 = jnp.float32
+    shapes = [(KW, inner + bc), (1, inner + bc), (1, inner), (8, 128), (1, width)]
     return pl.pallas_call(
-        widen_kernel,
+        functools.partial(widen_kernel, widths, heads),
         grid=(count, groups),
-        in_specs=[pl.BlockSpec((1, 1, rows, width), lambda t, g: (g, t, 0, 0))],
-        out_specs=pl.BlockSpec((rows, width), lambda t, g: (t * groups + g, 0)),
-        out_shape=jax.ShapeDtypeStruct((groups * count * rows, width), jnp.float32),
+        in_specs=[
+            pl.BlockSpec((1, 1, rows, width), lambda t, g: (g, t, 0, 0)),
+            pl.BlockSpec(small.shape, lambda t, g: (0, 0, 0)),
+        ],
+        out_specs=[pl.BlockSpec((rows, width), lambda t, g: (t * groups + g, 0))]
+        + [pl.BlockSpec(s, lambda t, g: (0, 0)) for s in shapes],
+        out_shape=[jax.ShapeDtypeStruct((groups * count * rows, width), f32)]
+        + [jax.ShapeDtypeStruct(s, f32) for s in shapes],
         name="assemble_out",
-    )(owned)
+    )(owned, small)
 
 
 def body(
@@ -1453,34 +1558,8 @@
     normed = (flat_tokens * in_scale * norm_gain).astype(bf16)
     cot_rows = cotangent.reshape(row_count, width)
 
-    in_turned = in_weight.T
-    local_columns = jnp.concatenate(
-        [
-            take(in_turned, channel_start, local_width, 0),
-            take(in_turned, inner_width + channel_start, local_width, 0),
-            in_turned[2 * inner_width : 2 * inner_width + bc_width],
-            take(in_turned, 2 * inner_width + bc_width + head_start, local_heads, 0),
-            jnp.zeros((128 - local_heads, in_weight.shape[0]), bf16),
-        ]
-    )
-    columns_here = local_columns.shape[0]
     blocks = (seq_devices, seqs_here, slot_rows)
-    def lanes(part):
-        return jnp.pad(part[None], ((0, 7), (0, 128 - local_heads)))
-
-    taps = jnp.pad(
-        jnp.concatenate(
-            [take(conv_weight, channel_start, local_width, 1), conv_weight[:, inner_width:]], axis=1
-        ),
-        ((0, 8 - KW), (0, 0)),
-    )
-    shift = jnp.concatenate(
-        [take(conv_bias, channel_start, local_width, 0), conv_bias[inner_width:]]
-    )[None]
-    bias = lanes(take(dt_bias, head_start, local_heads, 0))
-    slope = lanes(-jnp.exp(take(a_log, head_start, local_heads, 0)))
-    skip = jnp.repeat(take(skip_gain, head_start, local_heads, 0), head_size)[None]
-    gain_local = take(out_gain, channel_start, local_width, 0)
+    params = jnp.pad(jnp.stack([dt_bias, a_log, skip_gain]), ((0, 5), (0, 128 - head_count)))
     spread, fold, tri, upper = scan_tables(slot_rows, local_width, head_size)
     widths = (local_width, bc_width)
     per_owner = seq_devices // group_devices
@@ -1494,15 +1573,17 @@
         turned_out,
         gated_grad,
         gain_sum,
+        taps,
+        heads,
+        wide,
         branch_grad,
         out_full,
     ) = front(
         normed,
-        local_columns,
+        in_weight.T,
         cot_rows * valid_rows.astype(bf16),
         out_weight.reshape(per_owner, local_width, width),
-        (taps, shift, bias, slope, skip, spread, tri),
-        gain_local[None],
+        (conv_weight, conv_bias[None], params, out_gain[None], spread, tri),
         inner_width,
         widths,
         head_size,
@@ -1519,10 +1600,8 @@
         entering,
         gated_grad,
         taps,
-        shift,
-        bias,
-        slope,
-        skip,
+        heads,
+        wide,
         spread,
         fold,
         tri,
@@ -1530,11 +1609,11 @@
         widths,
         head_size,
     )
+    columns_here = proj_grad.shape[3]
     proj_grad = proj_grad.reshape(-1, columns_here)
     in_rows = in_weight.shape[0]
-    own_rows = (KW + 2) * (local_width // 128)
-    packed_rows = own_rows + 3 + ((KW + 1) * bc_width + width) // 128
-    shared_rows = bc_width // seq_devices
+    shared_count = bc_width + head_count
+    shared_rows = shared_count // seq_devices
     normed_grad, gathered, _, owned, shared_all, small_all, branch, _ = finish(
         proj_grad.reshape(blocks + (columns_here,)),
         in_columns,
@@ -1550,7 +1629,7 @@
         swapped,
         out_weight.reshape(per_owner, local_width, width),
         out_full,
-        (2 * local_width, bc_width, 16),
+        (2 * local_width, shared_count),
         2,
     )
     normed_grad = normed_grad.reshape(row_count, width)
@@ -1559,41 +1638,25 @@
     owned = owned.reshape(
         group_devices, per_owner, local_width // group_devices, width
     )
-    shared_all = shared_all.reshape(seq_devices, shared_rows + 16, in_rows)
+    shared_all = shared_all.reshape(seq_devices, 2, shared_rows, in_rows // 2)
     small_all = small_all.reshape(seq_devices, -1, 128)
     mixed_out = (flat_tokens + valid_rows * branch).astype(bf16).reshape(tokens.shape)
-    tail = jnp.concatenate(
-        [
-            shared_all[:, :shared_rows].reshape(bc_width, in_rows),
-            shared_all[:, shared_rows : shared_rows + local_heads].reshape(head_count, in_rows),
-        ]
-    )
+    tail = jnp.transpose(shared_all, (0, 2, 1, 3)).reshape(shared_count, in_rows)
     in_weight_grad = assemble_in(gathered, tail).T
-    out_weight_grad = assemble_out(owned)
-
-    own_all = small_all[:, :own_rows].reshape(seq_devices, KW + 2, local_width)
-    own_all = jnp.swapaxes(own_all, 0, 1).reshape(KW + 2, inner_width)
-    head_all = jnp.swapaxes(small_all[:, own_rows : own_rows + 3, :local_heads], 0, 1)
-    head_all = head_all.reshape(3, head_count)
-    summed = jnp.sum(small_all[:, own_rows + 3 : packed_rows], axis=0).reshape(-1)
-    conv_weight_grad = jnp.concatenate(
-        [own_all[:KW], summed[: KW * bc_width].reshape(KW, bc_width)], axis=1
-    )
-    conv_bias_grad = jnp.concatenate(
-        [own_all[KW], summed[KW * bc_width : (KW + 1) * bc_width]]
-    )
-    norm_gain_total = summed[(KW + 1) * bc_width :]
+    out_weight_grad, conv_weight_grad, conv_bias_grad, gain_grad, head_all, norm_grad = (
+        assemble_out(owned, small_all, widths, local_heads)
+    )
     return (
         mixed_out,
         token_grad.reshape(tokens.shape),
-        norm_gain_total,
+        norm_grad[0],
         in_weight_grad,
         conv_weight_grad,
-        conv_bias_grad,
-        head_all[0],
-        head_all[1],
-        head_all[2],
-        own_all[KW + 1],
+        conv_bias_grad[0],
+        head_all[0, :head_count],
+        head_all[1, :head_count],
+        head_all[2, :head_count],
+        gain_grad[0],
         out_weight_grad,
     )
 

time: 552 us -> 528 us (0.957)
  local copies, waits for them, and re-layouts: 30.3 us -> 11.1 us
    unnamed x59 -> x45, local copies, waits for them, and re-layouts: 13 us -> 6.29 us
    slice x13 -> x0, local copies, waits for them, and re-layouts: 5.68 us -> none  [the longest x1 1.36 us: body(): small_all[:, own_rows:own_rows + 3, :local_heads]]
  transfers between devices with their start and end apart: 1 -> 1, of which waited for: 1 -> 0; matrix products, arithmetic and copies ran while one was open for 0% -> 0% of each run, Pallas kernels for 8% -> 9%
where the time goes in v5:
time: 528 us; the launch traced here: 526 us
  Pallas kernels  496 us (94%)
  other arithmetic  12.3 us (2%)
  local copies, waits for them, and re-layouts  11.1 us (2%)
    pallas_call x1, Pallas kernels, finish(): pl.pallas_call(functools.partial(finish_kernel, size, groups, counts), ou...  242 us
    pallas_call x1, Pallas kernels, front(): pl.pallas_call(functools.partial(front_kernel, widths, head_size, size, g...  191 us
    pallas_call x1, Pallas kernels, scan_backward(): pl.pallas_call(functools.partial(backward_kernel, widths, head_size, chun...  46.1 us
  transfers between devices with their start and end apart: 1, of which 0 were waited for; matrix products, arithmetic and copies ran while one was open for 0% of the time, Pallas kernels for 9%

profile of v5, /device:TPU:0, one launch (start us, length us, event | category | flops | bytes accessed | tf_op | source)
XLA Modules:
  0.0 525.7 jit_solution(12668996857800741357)
XLA Ops:
  0.7 1.6 multiply_reduce_fusion.1
  2.3 0.1 rsqrt.20
  2.4 1.4 broadcast_in_dim.6.conv_bias_ref
  3.7 0.7 fusion.1
  4.5 2.4 broadcast_multiply_fusion.cot_ref
  6.8 1.3 multiply_convert_fusion.x_ref
  8.1 0.6 select_maximum_fusion.params_ref
  8.7 191.1 %front.1 = (bf16[8,2,2,64,2048]{4,3,2,1,0:T(8,128)(2,1)}, bf16[4,1408,512]{2,1,0:T(8,128)(2,1)}, bf16[8,2,128,1408]{3,2,1,0:T(8,128)(2,1)}, bf16[8,2,128,512]{3,...) custom-call(bf16[2,2,64,2048]{3,2,1,0:T(8,128)(2,1)} %multiply_conve, ...), custom_call_target="tpu_custom_call" | custom-call | tf_op jit(solution)/shard_map/front/pallas_call | solution.py:825
  199.9 5.1 all-to-all-start
  205.1 1.6 copy-done.2
  206.6 46.1 %scan_backward.1 = (bf16[8,2,128,1408]{3,2,1,0:T(8,128)(2,1)}, bf16[1408,2048]{1,0:T(8,128)(2,1)}, f32[8,768]{1,0:T(8,128)S(1)}, f32[8,512]{1,0:T(8,128)}, f32[8,128]{1,0:T(8,128)S(1)}) custom-call(bf16[8,2,128,1408]{3,2,1,0:T(8,128)(2,1)} %get-tuple-element.41.proj_ref.before_ref, bf16[8,2,128,1408]{3,2,1,0:T(8,128)(2,1)} %get-tuple-element.41.proj_ref.before_ref, ...), custom_call_target="tpu_custom_call" | custom-call | tf_op jit(solution)/shard_map/scan_backward/pallas_call | solution.py:311
  252.8 0.6 copy-done.7
  253.4 0.6 copy-done.11
  254.0 0.8 broadcast_in_dim.8.scale_ref
  254.8 242.2 %finish.1 = (f32[2,128,2048]{2,1,0:T(8,128)}, bf16[8,2,2,256,512]{4,3,2,1,0:T(8,128)(2,1)}, bf16[8,2,2,32,2048]{4,3,2,1,0:T(8,128)(2,1)}, bf16[4,2,2,2,32,2048]{...) custom-call(bf16[8,2,128,1408]{3,2,1,0:T(8,128)(2,1)} %get-tuple-ele, ...), custom_call_target="tpu_custom_call" | custom-call | tf_op jit(solution)/shard_map/finish/pallas_call | solution.py:1344
  497.0 1.2 copy.27
  498.3 7.6 %assemble_out.1 = (f32[1024,2048]{1,0:T(8,128)}, f32[4,4352]{1,0:T(4,128)}, f32[1,4352]{1,0:T(1,128)}, f32[1,4096]{1,0:T(1,128)}, f32[8,128]{1,0:T(8,128)}, /*index=5*/f32[1,2048]{1,0:T(1,128)}) custom-call(bf16[4,2,128,2048]{3,2,1,0:T(8,128)(2,1)} %bitcast.44, f32[8,64,128]{2,1,0:T(8,128)} %bitcast.50), custom_call_target="tpu_custom_call" | custom-call | tf_op jit(solution)/shard_map/assemble_out/pallas_call | solution.py:1504
  506.0 1.3 slice_bitcast_fusion
  507.3 0.4 multiply_reduce_fusion
  507.7 3.4 copy-done
  511.1 9.3 %assemble_in.1 = f32[8512,512]{1,0:T(8,128)} custom-call(bf16[8,2,2,256,512]{4,3,2,1,0:T(8,128)(2,1)S(1)} %copy-done, bf16[512,512]{1,0:T(8,128)(2,1)S(1)} %pad.9.tail_ref), custom_call_target="tpu_custom_call" | custom-call | tf_op jit(solution)/shard_map/assemble_in/pallas_call | solution.py:1438
  520.4 0.7 reduce.2
  521.0 3.3 convert_add_fusion
  524.4 1.3 fusion
  (48 shorter events, 0.3 us)
Async XLA Ops:
  0.6 6.2 %copy-start.12 = (bf16[2,128,2048]{2,1,0:T(8,128)(2,1)S(1)}, bf16[2,128,2048]{2,1,0:T(8,128)(2,1)}, u32[]{:S(2)}) copy-start(bf16[2,128,2048]{2,1,0:T(8,128)(2,1)} %tokens_ref.1) | copy-start | bytes 3145732
  0.7 6.2 %copy-start.16 = (f32[2048]{0:T(1024)S(1)}, f32[2048]{0:T(1024)}, u32[]{:S(2)}) copy-start(f32[2048]{0:T(1024)} %param.18) | copy-start | bytes 24580
  4.4 3.7 copy-start.19
  4.4 3.7 copy-start.20
  4.4 3.7 copy-start.21
  199.8 5.2 copy-start.1
  199.8 5.1 copy-start.3
  199.8 5.1 copy-start.4
  199.8 5.1 copy-start.5
  199.9 5.1 copy-start.6
  199.9 5.1 copy-start.8
  199.9 5.1 copy-start.9
  199.9 5.1 copy-start.10
  199.9 54.1 %all-to-all-start = ((bf16[8,256,512]{2,1,0:T(8,128)(2,1)}), bf16[8,256,512]{2,1,0:T(8,128)(2,1)}, u32[]{:S(2)}, u32[]{:S(2)}) async-start(bf16[8,256,512]{2,1,0:T(8,128)(2,1)} %bitcast.45), calls=%async_computation | async-start | bytes 4194304 | tf_op jit(solution)/shard_map/all_to_all | solution.py:1594
  205.0 1.6 copy-start.2
  206.6 47.3 %copy-start.18 = (s32[2]{0:T(128)S(1)}, s32[2]{0:T(128)}, u32[]{:S(2)}) copy-start(s32[2]{0:T(128)} %param.17) | copy-start | bytes 28
  252.8 0.6 copy-start.7
  253.4 0.6 copy-start.11
  498.3 9.0 %copy-start.13 = (bf16[2,128,2048]{2,1,0:T(8,128)(2,1)S(1)}, bf16[2,128,2048]{2,1,0:T(8,128)(2,1)}, u32[]{:S(2)}) copy-start(bf16[2,128,2048]{2,1,0:T(8,128)(2,1)} %tokens_ref.1) | copy-start | bytes 3145732
  498.3 9.0 %copy-start.14 = (f32[2,128,2048]{2,1,0:T(8,128)S(1)}, f32[2,128,2048]{2,1,0:T(8,128)}, u32[]{:S(2)}) copy-start(f32[2,128,2048]{2,1,0:T(8,128)} %get-tuple-element.60) | copy-start | bytes 6291460
  507.7 3.4 copy-start
  511.1 9.3 %copy-start.17 = (f32[1,4352]{1,0:T(1,128)S(1)}, f32[1,4352]{1,0:T(1,128)}, u32[]{:S(2)}) copy-start(f32[1,4352]{1,0:T(1,128)} %get-tuple-element.67) | copy-start | bytes 52228
  521.0 3.3 copy-start.15

commit v6 on v5

--- a/solution.py
+++ b/solution.py
@@ -139,15 +139,20 @@
     fold_ref,
     tri_ref,
     upper_ref,
+    normed_ref,
     out_ref,
     turned_ref,
     taps_acc,
     skip_acc,
     head_acc,
+    swapped_ref,
     lam,
     ext,
     later,
     after,
+    swap_send,
+    swap_recv,
+    swap_local,
 ):
     lw, bc = widths
     state_size = bc // 2
@@ -157,8 +162,25 @@
     chunk = chunks - 1 - pl.program_id(1)
     head_start = lax.axis_index("seq") * (lw // head_size)
 
+    me, group = lax.axis_index("seq"), lax.axis_index("wa")
+    swaps = [
+        push(
+            normed_ref.at[other],
+            swapped_ref.at[me],
+            swap_send.at[k],
+            swap_recv.at[k],
+            (other, group),
+        )
+        for k, other in enumerate(others(me, chunks))
+    ]
+    swap_kept = pltpu.make_async_copy(normed_ref.at[me], swapped_ref.at[me], swap_local)
+
     @pl.when((pl.program_id(0) == 0) & (pl.program_id(1) == 0))
     def _():
+        greet([(other, group) for other in others(me, chunks)])
+        for copy in swaps:
+            copy.start()
+        swap_kept.start()
         taps_acc[...] = jnp.zeros_like(taps_acc)
         skip_acc[...] = jnp.zeros_like(skip_acc)
         head_acc[...] = jnp.zeros_like(head_acc)
@@ -281,6 +303,9 @@
         head_acc[2:3, :] = dot(
             skip_acc[...], fold_ref[...].astype(f32), 1, 0, HIGHEST
         )[0:1, :]
+        for copy in swaps:
+            copy.wait()
+        swap_kept.wait()
     out_ref[0, 0, :, lw : 2 * lw + bc] = total.astype(bf16)
     turned_ref[...] = out_ref[0, 0].T
 
@@ -297,7 +322,7 @@
 
 
 def scan_backward(
-    proj, y, enter, grad, taps, heads, wide, spread, fold, tri, upper, widths, head_size
+    proj, y, enter, grad, taps, heads, wide, spread, fold, tri, upper, normed, widths, head_size, collective_id
 ):
     chunks, seqs, rows, cols = proj.shape
     lw, bc = widths
@@ -312,26 +337,32 @@
         functools.partial(backward_kernel, widths, head_size, chunks),
         grid=(seqs, chunks),
         in_specs=[block(rows, cols), before, block(rows, lw), block(lw, bc // 2), block(rows, lw)]
-        + [whole_spec(t) for t in tables],
+        + [whole_spec(t) for t in tables]
+        + [ANY],
         out_specs=[
             block(rows, cols),
             pl.BlockSpec((cols, rows), lambda q, c: (0, (chunks - 1 - c) * seqs + q)),
         ]
-        + [pl.BlockSpec(s, lambda q, c: (0, 0)) for s in sums],
+        + [pl.BlockSpec(s, lambda q, c: (0, 0)) for s in sums]
+        + [ANY],
         out_shape=[
             jax.ShapeDtypeStruct(proj.shape, jnp.bfloat16),
             jax.ShapeDtypeStruct((cols, chunks * seqs * rows), jnp.bfloat16),
         ]
-        + [jax.ShapeDtypeStruct(s, jnp.float32) for s in sums],
+        + [jax.ShapeDtypeStruct(s, jnp.float32) for s in sums]
+        + [jax.ShapeDtypeStruct(normed.shape, normed.dtype)],
         scratch_shapes=[
             pltpu.VMEM((lw, bc // 2), jnp.float32),
             pltpu.VMEM((rows + 8, lw + bc), jnp.float32),
             pltpu.VMEM((rows + 8, lw + bc), jnp.float32),
             pltpu.VMEM((8, lw + bc), jnp.float32),
+            pltpu.SemaphoreType.DMA((chunks - 1,)),
+            pltpu.SemaphoreType.DMA((chunks - 1,)),
+            pltpu.SemaphoreType.DMA,
         ],
-        compiler_params=pltpu.CompilerParams(vmem_limit_bytes=48 * 2**20),
+        compiler_params=comm_params(collective_id, 60),
         name="scan_backward",
-    )(proj, proj, y, enter, grad, *tables)
+    )(proj, proj, y, enter, grad, *tables, normed)
 
 
 def ring_pos(index, size):
@@ -495,6 +526,10 @@
     out_turned,
     sums,
     landing,
+    normed_held,
+    turned_held,
+    grad_held,
+    result_sem,
     weight_send,
     weight_recv,
     weight_local,
@@ -769,6 +804,13 @@
     lane = lax.broadcasted_iota(jnp.int32, (rows, 128), 1)
     gain_acc[...] = jnp.zeros_like(gain_acc)
 
+    def results(block):
+        pairs = ((normed_held, normed_ref), (turned_held, turned_ref), (grad_held, grad_ref))
+        return [
+            pltpu.make_async_copy(held.at[block], out.at[block], result_sem.at[k, block])
+            for k, (held, out) in enumerate(pairs)
+        ]
+
     def finish(block, carry):
         for way in range(2):
             mask = lane == block * 2 + way
@@ -778,10 +820,12 @@
             values = out_grad[block, way]
             scaled = here * by
             normed = (scaled * wide_ref[0:1, :]).astype(bf16)
-            normed_ref[block, way] = normed
-            turned_ref[block, :, way * rows : (way + 1) * rows] = normed.T
-            grad_ref[block, way] = (values * wide_ref[0:1, :] * by - here * less).astype(bf16)
+            normed_held[block, way] = normed
+            turned_held[block, :, way * rows : (way + 1) * rows] = normed.T
+            grad_held[block, way] = (values * wide_ref[0:1, :] * by - here * less).astype(bf16)
             gain_acc[0:1, :] += jnp.sum(values * scaled, axis=0, keepdims=True)
+        for copy in results(block):
+            copy.start()
         return carry
 
     lax.fori_loop(0, size, finish, 0)
@@ -798,6 +842,8 @@
     def settle(pair, carry):
         for way in range(2):
             put(pair, way).wait()
+        for copy in results(pair):
+            copy.wait()
         return carry
 
     lax.fori_loop(0, size, settle, 0)
@@ -841,7 +887,7 @@
             shape((groups, per_owner, lw, width), bf16),
         ],
         in_specs=[ANY] * 4 + [VMEM] * 6,
-        out_specs=[ANY] * 5 + [VMEM] * 7 + [ANY] * 2,
+        out_specs=[ANY] * 8 + [VMEM] * 4 + [ANY] * 2,
         scratch_shapes=[
             vmem((groups, cols, depth), bf16),
             vmem((size, 2, rows, cols), bf16),
@@ -857,6 +903,10 @@
             vmem((width, lw), bf16),
             vmem((2, 2 * size, rows), f32),
             vmem((size - 1, 2, 2 * size, rows), f32),
+            vmem(whole, bf16),
+            vmem((size, lw, 2 * rows), bf16),
+            vmem(whole, bf16),
+            DMA((3, size)),
             DMA((groups - 1, 3)),
             DMA((groups - 1, 3)),
             DMA((3,)),
@@ -1589,12 +1639,8 @@
         head_size,
         0,
     )
-    normed_out = normed_out.reshape(-1, local_width)
     branch_grad = branch_grad.reshape(-1, width)
-    swapped = lax.all_to_all(
-        normed_out.reshape(seq_devices, row_count, local_width), "seq", 0, 0, tiled=True
-    )
-    proj_grad, turned_grad, taps_sum, _, head_sum = scan_backward(
+    proj_grad, turned_grad, taps_sum, _, head_sum, swapped = scan_backward(
         projected,
         y_heads,
         entering,
@@ -1606,9 +1652,12 @@
         fold,
         tri,
         upper,
+        normed_out,
         widths,
         head_size,
-    )
+        1,
+    )
+    swapped = swapped.reshape(seq_devices, row_count, local_width)
     columns_here = proj_grad.shape[3]
     proj_grad = proj_grad.reshape(-1, columns_here)
     in_rows = in_weight.shape[0]

time: 528 us -> 520 us (0.985)
    pallas_call x1, Pallas kernels: 46.1 us -> 51.4 us  [scan_backward(): pl.pallas_call(functools.partial(backward_kernel, widths, head_size, chun...]
  transfers between devices with their start and end apart: 1 -> 0, of which waited for: 0 -> 0; matrix products, arithmetic and copies ran while one was open for 0% -> 0% of each run, Pallas kernels for 9% -> 0%
where the time goes in v6:
time: 520 us; the launch traced here: 519 us
  Pallas kernels  499 us (96%)
  other arithmetic  11.1 us (2%)
  local copies, waits for them, and re-layouts  7.51 us (1%)
    pallas_call x1, Pallas kernels, finish(): pl.pallas_call(functools.partial(finish_kernel, size, groups, counts), ou...  242 us
    pallas_call x1, Pallas kernels, front(): pl.pallas_call(functools.partial(front_kernel, widths, head_size, size, g...  189 us
    pallas_call x1, Pallas kernels, scan_backward(): pl.pallas_call(functools.partial(backward_kernel, widths, head_size, chun...  51.4 us

profile of v6, /device:TPU:0, one launch (start us, length us, event | category | flops | bytes accessed | tf_op | source)
XLA Modules:
  0.0 518.6 jit_solution(769097709411950248)
XLA Ops:
  0.6 0.0 copy-start.8
  0.7 0.0 copy-start.3
  0.7 1.6 multiply_reduce_fusion.1
  2.3 0.1 rsqrt.20
  2.4 2.6 multiply_convert_fusion.x_ref
  5.0 0.1 fusion.1
  5.0 1.1 broadcast_multiply_fusion.cot_ref
  6.1 0.6 broadcast_in_dim.6.conv_bias_ref
  6.8 0.0 copy-done.9
  6.8 0.6 select_maximum_fusion.params_ref
  7.4 189.3 %front.1 = (bf16[8,2,2,64,2048]{4,3,2,1,0:T(8,128)(2,1)}, bf16[4,1408,512]{2,1,0:T(8,128)(2,1)}, bf16[8,2,128,1408]{3,2,1,0:T(8,128)(2,1)}, bf16[8,2,128,512]{3,...) custom-call(bf16[2,2,64,2048]{3,2,1,0:T(8,128)(2,1)} %multiply_conve, ...), custom_call_target="tpu_custom_call" | custom-call | tf_op jit(solution)/shard_map/front/pallas_call | solution.py:871
  196.6 51.4 %scan_backward.1 = (bf16[8,2,128,1408]{3,2,1,0:T(8,128)(2,1)}, bf16[1408,2048]{1,0:T(8,128)(2,1)}, f32[8,768]{1,0:T(8,128)}, f32[8,512]{1,0:T(8,128)}, f32[8,128...) custom-call(bf16[8,2,128,1408]{3,2,1,0:T(8,128)(2,1)} %get-tuple-element.42.proj_ref.before_ref, ...), custom_call_target="tpu_custom_call" | custom-call | tf_op jit(solution)/shard_map/scan_backward/pallas_call | solution.py:336
  248.1 0.8 broadcast_in_dim.8.scale_ref
  248.8 241.6 %finish.1 = (f32[2,128,2048]{2,1,0:T(8,128)}, bf16[8,2,2,256,512]{4,3,2,1,0:T(8,128)(2,1)}, bf16[8,2,2,32,2048]{4,3,2,1,0:T(8,128)(2,1)}, bf16[4,2,2,2,32,2048]{...) custom-call(bf16[8,2,128,1408]{3,2,1,0:T(8,128)(2,1)} %get-tuple-ele, ...), custom_call_target="tpu_custom_call" | custom-call | tf_op jit(solution)/shard_map/finish/pallas_call | solution.py:1394
  490.4 1.2 copy.27
  491.8 3.4 copy-done
  495.2 9.3 %assemble_in.1 = f32[8512,512]{1,0:T(8,128)} custom-call(bf16[8,2,2,256,512]{4,3,2,1,0:T(8,128)(2,1)S(1)} %copy-done, bf16[512,512]{1,0:T(8,128)(2,1)S(1)} %pad.9.tail_ref), custom_call_target="tpu_custom_call" | custom-call | tf_op jit(solution)/shard_map/assemble_in/pallas_call | solution.py:1488
  504.4 7.6 %assemble_out.1 = (f32[1024,2048]{1,0:T(8,128)}, f32[4,4352]{1,0:T(4,128)}, f32[1,4352]{1,0:T(1,128)}, f32[1,4096]{1,0:T(1,128)}, f32[8,128]{1,0:T(8,128)}, /*index=5*/f32[1,2048]{1,0:T(1,128)}) custom-call(bf16[4,2,128,2048]{3,2,1,0:T(8,128)(2,1)} %bitcast.44, f32[8,64,128]{2,1,0:T(8,128)} %bitcast.50), custom_call_target="tpu_custom_call" | custom-call | tf_op jit(solution)/shard_map/assemble_out/pallas_call | solution.py:1554
  512.0 1.4 reduce.2
  513.4 1.3 slice_bitcast_fusion
  514.8 0.4 multiply_reduce_fusion
  515.1 2.0 convert_add_fusion
  517.2 0.1 fusion.2
  517.2 1.3 fusion
  (26 shorter events, 0.1 us)
Async XLA Ops:
  0.6 4.3 copy-start.8
  0.7 4.4 copy-start.3
  2.4 3.8 copy-start.7
  2.4 4.4 copy-start.9
  2.4 4.4 copy-start.10
  2.4 4.4 copy-start.11
  491.8 3.4 copy-start
  504.4 10.3 %copy-start.1 = (bf16[2,128,2048]{2,1,0:T(8,128)(2,1)S(1)}, bf16[2,128,2048]{2,1,0:T(8,128)(2,1)}, u32[]{:S(2)}) copy-start(bf16[2,128,2048]{2,1,0:T(8,128)(2,1)} %tokens_ref.1) | copy-start | bytes 3145732
  504.4 10.3 %copy-start.2 = (f32[2,128,2048]{2,1,0:T(8,128)S(1)}, f32[2,128,2048]{2,1,0:T(8,128)}, u32[]{:S(2)}) copy-start(f32[2,128,2048]{2,1,0:T(8,128)} %get-tuple-element.62) | copy-start | bytes 6291460
  504.4 10.3 %copy-start.6 = (f32[2048]{0:T(1024)S(1)}, f32[2048]{0:T(1024)}, u32[]{:S(2)}) copy-start(f32[2048]{0:T(1024)} %param.18) | copy-start | bytes 24580
  513.4 1.7 copy-start.4
  515.1 2.1 copy-start.5

commit v7 on v6

--- a/solution.py
+++ b/solution.py
@@ -1173,12 +1173,9 @@
         def _():
             out_sends()
 
-        @pl.when((step > 2) & (step <= groups + 2))
+        @pl.when((step > 2) & (step <= groups + 1))
         def _():
             weight_part(step - 2)
-
-        @pl.when((step > 2) & (step <= groups + 1))
-        def _():
             parts[step - 3] = total[...].astype(bf16)
             send_part(step - 2).start()
 
@@ -1236,7 +1233,9 @@
         out_ring.advance(step)
         return carry
 
-    lax.fori_loop(1, size // 2, out_advance, 0)
+    lax.fori_loop(1, 2, out_advance, 0)
+    weight_part(groups)
+    lax.fori_loop(2, size // 2, out_advance, 0)
     fetched = []
     for offset in range(1, groups):
         send_part(offset).wait()
@@ -1255,22 +1254,10 @@
         push(shared.at[peer[0]], shared_land.at[k], pair_send.at[k], pair_recv.at[k], peer)
         for k, peer in enumerate(peers)
     ]
-    lax.fori_loop(size // 2, size - 1, out_advance, 0)
     for copy in shared_in:
         copy.start()
+    lax.fori_loop(size // 2, size - 1, out_advance, 0)
     main_ring.start()
-    out_ring.finish()
-    owned = [
-        push(pieces_by_owner(pieces_ref, mate[1], groups), owned_ref.at[group], owned_send.at[k], owned_recv.at[k], mate)
-        for k, mate in enumerate(mates)
-    ]
-    kept = pltpu.make_async_copy(
-        pieces_by_owner(pieces_ref, group, groups), owned_ref.at[group], owned_local
-    )
-    for copy in owned:
-        copy.start()
-    kept.start()
-    main_ring.advance(1)
     for copy in small_in + shared_in:
         copy.wait()
     values = small[...]
@@ -1285,6 +1272,17 @@
         shared_sum[way, 0] = values[:, way * across : (way + 1) * across].astype(bf16)
     small_ring.start()
     shared_ring.start()
+    out_ring.finish()
+    owned = [
+        push(pieces_by_owner(pieces_ref, mate[1], groups), owned_ref.at[group], owned_send.at[k], owned_recv.at[k], mate)
+        for k, mate in enumerate(mates)
+    ]
+    kept = pltpu.make_async_copy(
+        pieces_by_owner(pieces_ref, group, groups), owned_ref.at[group], owned_local
+    )
+    for copy in owned:
+        copy.start()
+    kept.start()
     branch_ref[...] = jnp.zeros_like(branch_ref)
 
     per_owner = size // groups
@@ -1319,18 +1317,16 @@
 
     weight_take(0, 0)
     swapped_load.wait()
-    count = size - 3
+    count = size - 2
 
     def main_advance(step, carry):
         main_ring.advance(step)
-        small_ring.advance(step - 1)
-        shared_ring.advance(step - 1)
-        lax.fori_loop(((step - 2) * size) // count, ((step - 1) * size) // count, multiply, 0)
+        small_ring.advance(step)
+        shared_ring.advance(step)
+        lax.fori_loop(((step - 1) * size) // count, (step * size) // count, multiply, 0)
         return carry
 
-    lax.fori_loop(2, size - 1, main_advance, 0)
-    small_ring.advance(size - 2)
-    shared_ring.advance(size - 2)
+    lax.fori_loop(1, size - 1, main_advance, 0)
 
     def drain(step, carry):
         def one(at, inner):

time: 520 us -> 516 us (level)
  no operation moved by 1% of the time
where the time goes in v7:
time: 516 us; the launch traced here: 515 us
  Pallas kernels  495 us (96%)
  other arithmetic  11.1 us (2%)
  local copies, waits for them, and re-layouts  7.51 us (1%)
    pallas_call x1, Pallas kernels, finish(): pl.pallas_call(functools.partial(finish_kernel, size, groups, counts), ou...  238 us
    pallas_call x1, Pallas kernels, front(): pl.pallas_call(functools.partial(front_kernel, widths, head_size, size, g...  189 us
    pallas_call x1, Pallas kernels, scan_backward(): pl.pallas_call(functools.partial(backward_kernel, widths, head_size, chun...  51.4 us

profile of v7, /device:TPU:0, one launch (start us, length us, event | category | flops | bytes accessed | tf_op | source)
XLA Modules:
  0.0 514.6 jit_solution(143224181007104976)
XLA Ops:
  0.7 0.0 copy-start.3
  0.7 1.6 multiply_reduce_fusion.1
  2.3 0.1 rsqrt.20
  2.4 2.6 multiply_convert_fusion.x_ref
  5.0 0.1 fusion.1
  5.0 1.1 broadcast_multiply_fusion.cot_ref
  6.1 0.6 broadcast_in_dim.6.conv_bias_ref
  6.8 0.0 copy-done.11
  6.8 0.6 select_maximum_fusion.params_ref
  7.4 189.3 %front.1 = (bf16[8,2,2,64,2048]{4,3,2,1,0:T(8,128)(2,1)}, bf16[4,1408,512]{2,1,0:T(8,128)(2,1)}, bf16[8,2,128,1408]{3,2,1,0:T(8,128)(2,1)}, bf16[8,2,128,512]{3,...) custom-call(bf16[2,2,64,2048]{3,2,1,0:T(8,128)(2,1)} %multiply_conve, ...), custom_call_target="tpu_custom_call" | custom-call | tf_op jit(solution)/shard_map/front/pallas_call | solution.py:871
  196.6 51.4 %scan_backward.1 = (bf16[8,2,128,1408]{3,2,1,0:T(8,128)(2,1)}, bf16[1408,2048]{1,0:T(8,128)(2,1)}, f32[8,768]{1,0:T(8,128)}, f32[8,512]{1,0:T(8,128)}, f32[8,128...) custom-call(bf16[8,2,128,1408]{3,2,1,0:T(8,128)(2,1)} %get-tuple-element.42.proj_ref.before_ref, ...), custom_call_target="tpu_custom_call" | custom-call | tf_op jit(solution)/shard_map/scan_backward/pallas_call | solution.py:336
  248.1 0.8 broadcast_in_dim.8.scale_ref
  248.8 237.6 %finish.1 = (f32[2,128,2048]{2,1,0:T(8,128)}, bf16[8,2,2,256,512]{4,3,2,1,0:T(8,128)(2,1)}, bf16[8,2,2,32,2048]{4,3,2,1,0:T(8,128)(2,1)}, bf16[4,2,2,2,32,2048]{...) custom-call(bf16[8,2,128,1408]{3,2,1,0:T(8,128)(2,1)} %get-tuple-ele, ...), custom_call_target="tpu_custom_call" | custom-call | tf_op jit(solution)/shard_map/finish/pallas_call | solution.py:1390
  486.5 1.2 copy.27
  487.8 0.0 copy-start
  487.8 3.4 copy-done
  491.2 9.3 %assemble_in.1 = f32[8512,512]{1,0:T(8,128)} custom-call(bf16[8,2,2,256,512]{4,3,2,1,0:T(8,128)(2,1)S(1)} %copy-done, bf16[512,512]{1,0:T(8,128)(2,1)S(1)} %pad.9.tail_ref), custom_call_target="tpu_custom_call" | custom-call | tf_op jit(solution)/shard_map/assemble_in/pallas_call | solution.py:1484
  500.4 7.6 %assemble_out.1 = (f32[1024,2048]{1,0:T(8,128)}, f32[4,4352]{1,0:T(4,128)}, f32[1,4352]{1,0:T(1,128)}, f32[1,4096]{1,0:T(1,128)}, f32[8,128]{1,0:T(8,128)}, /*index=5*/f32[1,2048]{1,0:T(1,128)}) custom-call(bf16[4,2,128,2048]{3,2,1,0:T(8,128)(2,1)} %bitcast.44, f32[8,64,128]{2,1,0:T(8,128)} %bitcast.50), custom_call_target="tpu_custom_call" | custom-call | tf_op jit(solution)/shard_map/assemble_out/pallas_call | solution.py:1550
  508.1 1.4 reduce.2
  509.4 1.3 slice_bitcast_fusion
  510.8 0.4 multiply_reduce_fusion
  511.2 2.0 convert_add_fusion
  513.2 0.1 fusion.2
  513.3 1.3 fusion
  (26 shorter events, 0.1 us)
Async XLA Ops:
  0.6 4.3 copy-start.8
  0.7 4.4 copy-start.3
  2.4 3.8 copy-start.7
  2.4 4.4 copy-start.9
  2.4 4.4 copy-start.10
  2.4 4.4 copy-start.11
  487.8 3.4 copy-start
  500.4 10.3 %copy-start.1 = (bf16[2,128,2048]{2,1,0:T(8,128)(2,1)S(1)}, bf16[2,128,2048]{2,1,0:T(8,128)(2,1)}, u32[]{:S(2)}) copy-start(bf16[2,128,2048]{2,1,0:T(8,128)(2,1)} %tokens_ref.1) | copy-start | bytes 3145732
  500.4 10.3 %copy-start.2 = (f32[2,128,2048]{2,1,0:T(8,128)S(1)}, f32[2,128,2048]{2,1,0:T(8,128)}, u32[]{:S(2)}) copy-start(f32[2,128,2048]{2,1,0:T(8,128)} %get-tuple-element.62) | copy-start | bytes 6291460
  500.4 10.3 %copy-start.6 = (f32[2048]{0:T(1024)S(1)}, f32[2048]{0:T(1024)}, u32[]{:S(2)}) copy-start(f32[2048]{0:T(1024)} %param.18) | copy-start | bytes 24580
  509.4 1.7 copy-start.4
  511.2 2.1 copy-start.5

commit v8 on v7

--- a/solution.py
+++ b/solution.py
@@ -1235,7 +1235,7 @@
 
     lax.fori_loop(1, 2, out_advance, 0)
     weight_part(groups)
-    lax.fori_loop(2, size // 2, out_advance, 0)
+    lax.fori_loop(2, size - 2, out_advance, 0)
     fetched = []
     for offset in range(1, groups):
         send_part(offset).wait()
@@ -1256,7 +1256,7 @@
     ]
     for copy in shared_in:
         copy.start()
-    lax.fori_loop(size // 2, size - 1, out_advance, 0)
+    lax.fori_loop(size - 2, size - 1, out_advance, 0)
     main_ring.start()
     for copy in small_in + shared_in:
         copy.wait()

time: 516 us -> 507 us (0.983)
  Pallas kernels: 495 us -> 486 us
    pallas_call x1, Pallas kernels: 238 us -> 228 us  [finish(): pl.pallas_call(functools.partial(finish_kernel, size, groups, counts), ou...]
where the time goes in v8:
time: 507 us; the launch traced here: 505 us
  Pallas kernels  486 us (96%)
  other arithmetic  11.1 us (2%)
  local copies, waits for them, and re-layouts  7.51 us (1%)
    pallas_call x1, Pallas kernels, finish(): pl.pallas_call(functools.partial(finish_kernel, size, groups, counts), ou...  228 us
    pallas_call x1, Pallas kernels, front(): pl.pallas_call(functools.partial(front_kernel, widths, head_size, size, g...  189 us
    pallas_call x1, Pallas kernels, scan_backward(): pl.pallas_call(functools.partial(backward_kernel, widths, head_size, chun...  51.4 us

profile of v8, /device:TPU:0, one launch (start us, length us, event | category | flops | bytes accessed | tf_op | source)
XLA Modules:
  0.0 504.9 jit_solution(15413075825391246743)
XLA Ops:
  0.7 0.0 copy-start.3
  0.7 1.6 multiply_reduce_fusion.1
  2.3 0.1 rsqrt.20
  2.4 2.6 multiply_convert_fusion.x_ref
  5.0 0.0 copy-done.8
  5.0 0.1 fusion.1
  5.0 1.1 broadcast_multiply_fusion.cot_ref
  6.1 0.6 broadcast_in_dim.6.conv_bias_ref
  6.8 0.6 select_maximum_fusion.params_ref
  7.4 189.3 %front.1 = (bf16[8,2,2,64,2048]{4,3,2,1,0:T(8,128)(2,1)}, bf16[4,1408,512]{2,1,0:T(8,128)(2,1)}, bf16[8,2,128,1408]{3,2,1,0:T(8,128)(2,1)}, bf16[8,2,128,512]{3,...) custom-call(bf16[2,2,64,2048]{3,2,1,0:T(8,128)(2,1)} %multiply_conve, ...), custom_call_target="tpu_custom_call" | custom-call | tf_op jit(solution)/shard_map/front/pallas_call | solution.py:871
  196.6 51.4 %scan_backward.1 = (bf16[8,2,128,1408]{3,2,1,0:T(8,128)(2,1)}, bf16[1408,2048]{1,0:T(8,128)(2,1)}, f32[8,768]{1,0:T(8,128)}, f32[8,512]{1,0:T(8,128)}, f32[8,128...) custom-call(bf16[8,2,128,1408]{3,2,1,0:T(8,128)(2,1)} %get-tuple-element.42.proj_ref.before_ref, ...), custom_call_target="tpu_custom_call" | custom-call | tf_op jit(solution)/shard_map/scan_backward/pallas_call | solution.py:336
  248.1 0.8 broadcast_in_dim.8.scale_ref
  248.8 227.9 %finish.1 = (f32[2,128,2048]{2,1,0:T(8,128)}, bf16[8,2,2,256,512]{4,3,2,1,0:T(8,128)(2,1)}, bf16[8,2,2,32,2048]{4,3,2,1,0:T(8,128)(2,1)}, bf16[4,2,2,2,32,2048]{...) custom-call(bf16[8,2,128,1408]{3,2,1,0:T(8,128)(2,1)} %get-tuple-ele, ...), custom_call_target="tpu_custom_call" | custom-call | tf_op jit(solution)/shard_map/finish/pallas_call | solution.py:1390
  476.8 1.2 copy.27
  478.1 3.4 copy-done
  481.5 9.3 %assemble_in.1 = f32[8512,512]{1,0:T(8,128)} custom-call(bf16[8,2,2,256,512]{4,3,2,1,0:T(8,128)(2,1)S(1)} %copy-done, bf16[512,512]{1,0:T(8,128)(2,1)S(1)} %pad.9.tail_ref), custom_call_target="tpu_custom_call" | custom-call | tf_op jit(solution)/shard_map/assemble_in/pallas_call | solution.py:1484
  490.7 7.6 %assemble_out.1 = (f32[1024,2048]{1,0:T(8,128)}, f32[4,4352]{1,0:T(4,128)}, f32[1,4352]{1,0:T(1,128)}, f32[1,4096]{1,0:T(1,128)}, f32[8,128]{1,0:T(8,128)}, /*index=5*/f32[1,2048]{1,0:T(1,128)}) custom-call(bf16[4,2,128,2048]{3,2,1,0:T(8,128)(2,1)} %bitcast.44, f32[8,64,128]{2,1,0:T(8,128)} %bitcast.50), custom_call_target="tpu_custom_call" | custom-call | tf_op jit(solution)/shard_map/assemble_out/pallas_call | solution.py:1550
  498.4 1.4 reduce.2
  499.8 1.3 slice_bitcast_fusion
  501.1 0.0 copy-done.6
  501.1 0.4 multiply_reduce_fusion
  501.5 2.0 convert_add_fusion
  503.5 0.1 fusion.2
  503.6 1.3 fusion
  (26 shorter events, 0.1 us)
Async XLA Ops:
  0.6 4.3 copy-start.8
  0.7 4.4 copy-start.3
  2.4 3.8 copy-start.7
  2.4 4.4 copy-start.9
  2.4 4.4 copy-start.10
  2.4 4.4 copy-start.11
  478.1 3.4 copy-start
  490.7 10.3 %copy-start.1 = (bf16[2,128,2048]{2,1,0:T(8,128)(2,1)S(1)}, bf16[2,128,2048]{2,1,0:T(8,128)(2,1)}, u32[]{:S(2)}) copy-start(bf16[2,128,2048]{2,1,0:T(8,128)(2,1)} %tokens_ref.1) | copy-start | bytes 3145732
  490.7 10.3 %copy-start.2 = (f32[2,128,2048]{2,1,0:T(8,128)S(1)}, f32[2,128,2048]{2,1,0:T(8,128)}, u32[]{:S(2)}) copy-start(f32[2,128,2048]{2,1,0:T(8,128)} %get-tuple-element.62) | copy-start | bytes 6291460
  490.7 10.3 %copy-start.6 = (f32[2048]{0:T(1024)S(1)}, f32[2048]{0:T(1024)}, u32[]{:S(2)}) copy-start(f32[2048]{0:T(1024)} %param.18) | copy-start | bytes 24580
  499.8 1.7 copy-start.4
  501.5 2.1 copy-start.5

commit v9 on v8

--- a/solution.py
+++ b/solution.py
@@ -944,13 +944,13 @@
     swapped_ref,
     shard_ref,
     out_full_ref,
-    rows_ref,
+    rows_out,
     gathered_ref,
     pieces_ref,
     owned_ref,
     shared_out,
     small_out,
-    branch_ref,
+    branch_out,
     landing,
     slots,
     first,
@@ -997,6 +997,9 @@
     small_ring = RingGather(size, small, small_out, *ring_refs[9:12])
     fetch_sem, weights_taken, held, held_sem, out_turned = ring_refs[12:17]
     weight_held, swapped_held, load_sem = ring_refs[17:20]
+    rows_ref, branch_ref, result_sem = ring_refs[20:23]
+    rows_kept = pltpu.make_async_copy(rows_ref, rows_out, result_sem.at[0])
+    branch_kept = pltpu.make_async_copy(branch_ref, branch_out, result_sem.at[1])
     loads = [
         pltpu.make_async_copy(weight_ref.at[part], weight_held.at[part], load_sem.at[part])
         for part in range(groups)
@@ -1202,6 +1205,7 @@
         return carry
 
     lax.fori_loop(0, tiles, end, 0)
+    rows_kept.start()
     width = rows_ref.shape[2]
     own_width = gain_ref.shape[1]
     flat = jnp.zeros((1, width), f32)
@@ -1327,6 +1331,7 @@
         return carry
 
     lax.fori_loop(1, size - 1, main_advance, 0)
+    branch_kept.start()
 
     def drain(step, carry):
         def one(at, inner):
@@ -1340,6 +1345,8 @@
     for offset in range(1, groups):
         send_out(offset).wait_send()
     main_ring.finish()
+    rows_kept.wait()
+    branch_kept.wait()
     small_ring.finish()
     shared_ring.finish()
     for copy in owned:
@@ -1400,7 +1407,7 @@
             jax.ShapeDtypeStruct((groups - 1, cols, tile), bf16),
         ],
         in_specs=[ANY] * 6 + [VMEM] * 5 + [ANY] * 3,
-        out_specs=[VMEM, ANY, ANY, ANY, ANY, ANY, VMEM, ANY],
+        out_specs=[ANY] * 8,
         scratch_shapes=[
             vmem((size - 1, 2, tiles, rows, tile), bf16),
             vmem((2, tiles, rows, tile), bf16),
@@ -1440,7 +1447,8 @@
         + ring_sems(size, 1)
         + [DMA((groups - 1,)), vmem((2, lw, width), bf16)]
         + [vmem((2, 2, rows, cols), bf16), DMA((2, 2)), vmem((2, lw, 2 * rows), bf16)]
-        + [vmem(weight.shape, bf16), vmem(swapped.shape, bf16), DMA((groups + 1,))],
+        + [vmem(weight.shape, bf16), vmem(swapped.shape, bf16), DMA((groups + 1,))]
+        + [vmem((ways, rows, width), f32), vmem((ways * rows, width), f32), DMA((2,))],
         compiler_params=comm_params(collective_id, 63),
         name="finish",
     )(

time: 507 us -> 505 us (level)
  no operation moved by 1% of the time
where the time goes in v9:
time: 505 us; the launch traced here: 503 us
  Pallas kernels  483 us (96%)
  other arithmetic  11.1 us (2%)
  local copies, waits for them, and re-layouts  7.51 us (1%)
    pallas_call x1, Pallas kernels, finish(): pl.pallas_call(functools.partial(finish_kernel, size, groups, counts), ou...  226 us
    pallas_call x1, Pallas kernels, front(): pl.pallas_call(functools.partial(front_kernel, widths, head_size, size, g...  189 us
    pallas_call x1, Pallas kernels, scan_backward(): pl.pallas_call(functools.partial(backward_kernel, widths, head_size, chun...  51.4 us

profile of v9, /device:TPU:0, one launch (start us, length us, event | category | flops | bytes accessed | tf_op | source)
XLA Modules:
  0.0 502.8 jit_solution(15253822770882685123)
XLA Ops:
  0.7 0.0 copy-start.3
  0.7 1.6 multiply_reduce_fusion.1
  2.3 0.1 rsqrt.20
  2.4 2.6 multiply_convert_fusion.x_ref
  5.0 0.0 copy-done.8
  5.0 0.1 fusion.1
  5.0 1.1 broadcast_multiply_fusion.cot_ref
  6.1 0.6 broadcast_in_dim.6.conv_bias_ref
  6.8 0.6 select_maximum_fusion.params_ref
  7.4 189.3 %front.1 = (bf16[8,2,2,64,2048]{4,3,2,1,0:T(8,128)(2,1)}, bf16[4,1408,512]{2,1,0:T(8,128)(2,1)}, bf16[8,2,128,1408]{3,2,1,0:T(8,128)(2,1)}, bf16[8,2,128,512]{3,...) custom-call(bf16[2,2,64,2048]{3,2,1,0:T(8,128)(2,1)} %multiply_conve, ...), custom_call_target="tpu_custom_call" | custom-call | tf_op jit(solution)/shard_map/front/pallas_call | solution.py:871
  196.6 51.4 %scan_backward.1 = (bf16[8,2,128,1408]{3,2,1,0:T(8,128)(2,1)}, bf16[1408,2048]{1,0:T(8,128)(2,1)}, f32[8,768]{1,0:T(8,128)}, f32[8,512]{1,0:T(8,128)}, f32[8,128...) custom-call(bf16[8,2,128,1408]{3,2,1,0:T(8,128)(2,1)} %get-tuple-element.42.proj_ref.before_ref, ...), custom_call_target="tpu_custom_call" | custom-call | tf_op jit(solution)/shard_map/scan_backward/pallas_call | solution.py:336
  248.1 0.8 broadcast_in_dim.8.scale_ref
  248.8 225.9 %finish.1 = (f32[2,128,2048]{2,1,0:T(8,128)}, bf16[8,2,2,256,512]{4,3,2,1,0:T(8,128)(2,1)}, bf16[8,2,2,32,2048]{4,3,2,1,0:T(8,128)(2,1)}, bf16[4,2,2,2,32,2048]{...) custom-call(bf16[8,2,128,1408]{3,2,1,0:T(8,128)(2,1)} %get-tuple-ele, ...), custom_call_target="tpu_custom_call" | custom-call | tf_op jit(solution)/shard_map/finish/pallas_call | solution.py:1397
  474.7 1.2 copy.27
  476.1 3.4 copy-done
  479.4 9.3 %assemble_in.1 = f32[8512,512]{1,0:T(8,128)} custom-call(bf16[8,2,2,256,512]{4,3,2,1,0:T(8,128)(2,1)S(1)} %copy-done, bf16[512,512]{1,0:T(8,128)(2,1)S(1)} %pad.9.tail_ref), custom_call_target="tpu_custom_call" | custom-call | tf_op jit(solution)/shard_map/assemble_in/pallas_call | solution.py:1492
  488.7 7.6 %assemble_out.1 = (f32[1024,2048]{1,0:T(8,128)}, f32[4,4352]{1,0:T(4,128)}, f32[1,4352]{1,0:T(1,128)}, f32[1,4096]{1,0:T(1,128)}, f32[8,128]{1,0:T(8,128)}, /*index=5*/f32[1,2048]{1,0:T(1,128)}) custom-call(bf16[4,2,128,2048]{3,2,1,0:T(8,128)(2,1)} %bitcast.44, f32[8,64,128]{2,1,0:T(8,128)} %bitcast.50), custom_call_target="tpu_custom_call" | custom-call | tf_op jit(solution)/shard_map/assemble_out/pallas_call | solution.py:1558
  496.3 1.4 reduce.2
  497.7 1.3 slice_bitcast_fusion
  499.0 0.0 copy-done.1
  499.1 0.4 multiply_reduce_fusion
  499.4 2.0 convert_add_fusion
  501.5 0.1 fusion.2
  501.5 1.3 fusion
  (26 shorter events, 0.1 us)
Async XLA Ops:
  0.6 4.3 copy-start.8
  0.7 4.4 copy-start.3
  2.4 3.8 copy-start.7
  2.4 4.4 copy-start.9
  2.4 4.4 copy-start.10
  2.4 4.4 copy-start.11
  476.1 3.4 copy-start
  488.7 10.3 %copy-start.1 = (bf16[2,128,2048]{2,1,0:T(8,128)(2,1)S(1)}, bf16[2,128,2048]{2,1,0:T(8,128)(2,1)}, u32[]{:S(2)}) copy-start(bf16[2,128,2048]{2,1,0:T(8,128)(2,1)} %tokens_ref.1) | copy-start | bytes 3145732
  488.7 10.3 %copy-start.2 = (f32[2,128,2048]{2,1,0:T(8,128)S(1)}, f32[2,128,2048]{2,1,0:T(8,128)}, u32[]{:S(2)}) copy-start(f32[2,128,2048]{2,1,0:T(8,128)} %get-tuple-element.62) | copy-start | bytes 6291460
  488.7 10.3 %copy-start.6 = (f32[2048]{0:T(1024)S(1)}, f32[2048]{0:T(1024)}, u32[]{:S(2)}) copy-start(f32[2048]{0:T(1024)} %param.18) | copy-start | bytes 24580
  497.7 1.7 copy-start.4
  499.4 2.1 copy-start.5
